TPU v7x, 256 devices: a whole 4x4x8 slice. The times are simulated.
256 devices in a mesh: patch: 32 (over x, y, z_lo), shard: 8 (over z_hi, core).
Axes of the slice: x: 4, y: 4, z: 8 (z_hi: 4, z_lo: 2; z = z_hi * 2 + z_lo), core: 2. Of those that a mesh axis runs over, the one named last changes fastest.
Arguments:
- node_latent: bfloat16 [32768, 512], P(('patch', 'shard')), may hold values from -6 to 6
- edge_latent: bfloat16 [262144, 512], P(('patch', 'shard')), may hold values from -6 to 6
- senders: int32 [262144], P(('patch', 'shard')), may hold values from 0 to 1535
- receivers: int32 [262144], P(('patch', 'shard')), may hold values from 0 to 1023
- halo_list: int32 [32, 512], P('patch'), may hold values from 0 to 1023
- w_edge_first: bfloat16 [1536, 512], replicated, may hold values from -0.15625 to 0.15625
- w_edge_second: bfloat16 [512, 512], replicated, may hold values from -0.25 to 0.25
- w_node_first: bfloat16 [1024, 512], replicated, may hold values from -0.1875 to 0.1875
- w_node_second: bfloat16 [512, 512], replicated, may hold values from -0.25 to 0.25
- grad_node_new: bfloat16 [32768, 512], P(('patch', 'shard')), may hold values from -24 to 24
- grad_edge_new: bfloat16 [262144, 512], P(('patch', 'shard')), may hold values from -24 to 24
Outputs:
- grad_node_latent: bfloat16 [32768, 512], P(('patch', 'shard'))
- grad_edge_latent: bfloat16 [262144, 512], P(('patch', 'shard'))
- grad_edge_first: float32 [1536, 512], P(None, 'patch')
- grad_edge_second: float32 [512, 512], P(None, 'patch')
- grad_node_first: float32 [1024, 512], P(None, 'patch')
- grad_node_second: float32 [512, 512], P(None, 'patch')
All inputs are finite; a program needn't handle non-finite values.
Results may differ from a plain program's by a relative error of at most 0.03.
Values may be sent and summed in bfloat16 or wider, within the bound.
No kernel may reach another device: no remote copies, remote signals or barrier semaphores. Data moves between devices by JAX's collectives and lax.ppermute only.
A program may use at most 128 MiB of HBM per device.

v0:
```python
import jax
import jax.numpy as jnp
from jax import lax
from jax.sharding import PartitionSpec as P

epsilon = 1e-05


def copy_for_each(x, axis):
    copies = jnp.broadcast_to(x, (lax.axis_size(axis), *x.shape))
    return lax.all_to_all(copies, axis, split_axis=0, concat_axis=0, tiled=True)


def in_order(blocks, dim):
    shape = list(blocks.shape[1:])
    shape[dim] *= blocks.shape[0]
    return jnp.moveaxis(blocks, 0, dim).reshape(shape)


def gathered_copies(x, axis, dim):
    blocks = copy_for_each(x, axis)
    return in_order(blocks, dim)


def padded(block, sides, width):
    for axis, dim in sides:
        count = lax.axis_size(axis)
        forward = [(i, i + 1) for i in range(count - 1)]
        forward.append((count - 1, 0))
        backward = [(target, source) for source, target in forward]
        low = lax.ppermute(
            lax.slice_in_dim(block, block.shape[dim] - width, None, axis=dim), axis, forward
        )
        high = lax.ppermute(lax.slice_in_dim(block, 0, width, axis=dim), axis, backward)
        block = jnp.concatenate([low, block, high], axis=dim)
    return block


def split_up(x, dim, size):
    before, after = (x.shape[:dim], x.shape[dim + 1 :])
    return jnp.moveaxis(x.reshape(*before, size, -1, *after), dim, 0)


def summed_on_arrival(x, axis, dim):
    size = lax.axis_size(axis)
    blocks = lax.all_to_all(split_up(x, dim, size), axis, 0, 0, tiled=True)
    return jnp.sum(blocks.astype(jnp.float32), axis=0)


def sent_together(arrays, axis, dim, along):
    both = jnp.concatenate(arrays, axis=along)
    filled, at, gathered = (lax.psum_scatter(both, axis, scatter_dimension=dim, tiled=True), 0, [])
    for a in arrays:
        gathered.append(lax.slice_in_dim(filled, at, at + a.shape[along], axis=along))
        at += a.shape[along]
    return tuple(gathered)


def taken_together(x, axis):
    everything = copy_for_each(x, axis)
    return jnp.sum(everything.astype(jnp.float32), axis=0)


def swish_slope(values):
    sig = jax.nn.sigmoid(values)
    return sig * (1.0 + values * (1.0 - sig))


def contract_rows(left, right):
    return lax.dot_general(
        left, right, (((0,), (0,)), ((), ())), preferred_element_type=jnp.float32
    )


def times_transpose(left, right):
    return lax.dot_general(
        left, right, (((1,), (1,)), ((), ())), preferred_element_type=jnp.float32
    )


def mlp_forward(joined, w_first, w_second):
    pre_act = jnp.dot(joined, w_first, preferred_element_type=jnp.float32)
    activated = (pre_act * jax.nn.sigmoid(pre_act)).astype(jnp.bfloat16)
    output = jnp.dot(activated, w_second, preferred_element_type=jnp.float32)
    center = output - jnp.mean(output, axis=-1, keepdims=True)
    inv_scale = lax.rsqrt(jnp.mean(center * center, axis=-1, keepdims=True) + epsilon)
    return (pre_act, activated, center * inv_scale, inv_scale)


def mlp_backward(joined, w_first, w_second, pre_act, activated, normed, inv_scale, cotangent):
    d_out = inv_scale * (
        cotangent
        - jnp.mean(cotangent, axis=-1, keepdims=True)
        - normed * jnp.mean(cotangent * normed, axis=-1, keepdims=True)
    )
    d_out = d_out.astype(jnp.bfloat16)
    d_act = times_transpose(d_out, w_second)
    d_pre = (d_act * swish_slope(pre_act)).astype(jnp.bfloat16)
    grad_second = contract_rows(activated, d_out)
    grad_first = contract_rows(joined, d_pre)
    d_joined = times_transpose(d_pre, w_first)
    return (d_joined, grad_first, grad_second)


def body(
    node_latent,
    edge_latent,
    senders,
    receivers,
    halo_list,
    w_edge_first,
    w_edge_second,
    w_node_first,
    w_node_second,
    grad_node_new,
    grad_edge_new,
):
    shards = lax.axis_size("shard")
    node_rows = node_latent.shape[0]
    width = node_latent.shape[1]
    patch_rows = node_rows * shards
    send_lists = halo_list[0]
    halo_width = send_lists.shape[0] // 2
    gathered = gathered_copies(node_latent, "shard", 0)
    outgoing = jnp.take(gathered, send_lists, axis=0)
    widened = padded(outgoing, (("patch", 0),), halo_width)
    from_prev = widened[:halo_width]
    from_next = widened[halo_width * 3 :]
    extended = jnp.concatenate([from_prev, gathered, from_next], axis=0)
    joined = jnp.concatenate(
        [edge_latent, jnp.take(extended, senders, axis=0), jnp.take(gathered, receivers, axis=0)],
        axis=1,
    )
    pre_act, activated, normed, inv_scale = mlp_forward(joined, w_edge_first, w_edge_second)
    edge_new = (edge_latent.astype(jnp.float32) + normed).astype(jnp.bfloat16)
    partial_value = jax.ops.segment_sum(
        edge_new.astype(jnp.float32), receivers, num_segments=patch_rows
    )
    aggregate = summed_on_arrival(partial_value.astype(jnp.bfloat16), "shard", 0).astype(
        jnp.bfloat16
    )
    node_joined = jnp.concatenate([node_latent, aggregate], axis=1)
    n_pre, n_act, n_normed, n_inv = mlp_forward(node_joined, w_node_first, w_node_second)
    node_grad = grad_node_new.astype(jnp.float32)
    d_node, g_node_first, g_node_second = mlp_backward(
        node_joined, w_node_first, w_node_second, n_pre, n_act, n_normed, n_inv, node_grad
    )
    d_aggregate = d_node[:, width:]
    spread = gathered_copies(d_aggregate.astype(jnp.bfloat16), "shard", 0).astype(d_aggregate.dtype)
    edge_grad = grad_edge_new.astype(jnp.float32) + jnp.take(spread, receivers, axis=0)
    d_edge, g_edge_first, g_edge_second = mlp_backward(
        joined, w_edge_first, w_edge_second, pre_act, activated, normed, inv_scale, edge_grad
    )
    grad_edge_latent = (edge_grad + d_edge[:, :width]).astype(jnp.bfloat16)
    sender_part = jax.ops.segment_sum(
        d_edge[:, width : 2 * width], senders, num_segments=patch_rows + 2 * halo_width
    )
    receiver_part = jax.ops.segment_sum(d_edge[:, 2 * width :], receivers, num_segments=patch_rows)
    back_part = jnp.concatenate(
        [sender_part[:halo_width], sender_part[halo_width + patch_rows :]], axis=0
    )
    returned = padded(back_part.astype(jnp.bfloat16), (("patch", 0),), halo_width).astype(
        back_part.dtype
    )
    own_rows = sender_part[halo_width : halo_width + patch_rows] + receiver_part
    own_rows = own_rows.at[send_lists[:halo_width]].add(returned[:halo_width])
    own_rows = own_rows.at[send_lists[halo_width:]].add(returned[halo_width * 3 :])
    node_total = lax.psum_scatter(
        own_rows.astype(jnp.bfloat16), "shard", scatter_dimension=0, tiled=True
    ).astype(jnp.float32)
    grad_node_latent = (node_total + node_grad + d_node[:, :width]).astype(jnp.bfloat16)
    parted = tuple(
        (
            part.astype(jnp.float32)
            for part in sent_together(
                (
                    g_edge_first.astype(jnp.bfloat16),
                    g_edge_second.astype(jnp.bfloat16),
                    g_node_first.astype(jnp.bfloat16),
                    g_node_second.astype(jnp.bfloat16),
                ),
                "patch",
                1,
                0,
            )
        )
    )
    sliced = (
        taken_together(parted[0].astype(jnp.bfloat16), "shard").astype(jnp.float32),
        taken_together(parted[1].astype(jnp.bfloat16), "shard").astype(jnp.float32),
        taken_together(parted[2].astype(jnp.bfloat16), "shard").astype(jnp.float32),
        taken_together(parted[3].astype(jnp.bfloat16), "shard").astype(jnp.float32),
    )
    return (grad_node_latent, grad_edge_latent, sliced[0], sliced[1], sliced[2], sliced[3])


def solution(mesh):
    in_specs = (
        P(("patch", "shard"), None),
        P(("patch", "shard"), None),
        P(("patch", "shard")),
        P(("patch", "shard")),
        P("patch", None),
        P(),
        P(),
        P(),
        P(),
        P(("patch", "shard"), None),
        P(("patch", "shard"), None),
    )
    out_specs = (
        P(("patch", "shard"), None),
        P(("patch", "shard"), None),
        P(None, "patch"),
        P(None, "patch"),
        P(None, "patch"),
        P(None, "patch"),
    )
    return jax.shard_map(body, mesh=mesh, in_specs=in_specs, out_specs=out_specs, check_vma=False)
```

profile of v0, /device:TPU:1, one launch (start us, length us, event | category | flops | bytes accessed | tf_op | source)
XLA Modules:
  0.0 443.4 jit_solution(4752144645570744425)
XLA Ops:
  7.2 2.1 broadcast_in_dim.82
  9.3 10.0 %all-to-all-start = ((bf16[8,128,512]{2,1,0:T(8,128)(2,1)}), bf16[8,128,512]{2,1,0:T(8,128)(2,1)S(1)}, u32[]{:S(2)}, u32[]{:S(2)}) async-start(bf16[8,128,512]{2,1,0:T(8,128)(2,1)} %broadcast_in_dim.82), calls=%async_computation | async-start | bytes 2097152 | tf_op jit(solution)/shard_map/all_to_all | solution.py:11
  19.3 23.9 %all-to-all-done = bf16[8,128,512]{2,1,0:T(8,128)(2,1)S(1)} async-done(((bf16[8,128,512]{2,1,0:T(8,128)(2,1)}), bf16[8,128,512]{2,1,0:T(8,128)(2,1)S(1)}, u32[]{:S(2)}, u32[]{:S(2)}) %all-to-all-start) | async-done | bytes 1048608 | tf_op jit(solution)/shard_map/all_to_all | solution.py:11
  43.2 2.0 gather_fusion
  46.1 5.2 %collective-permute-start = (bf16[256,512]{1,0:T(8,128)(2,1)}, bf16[256,512]{1,0:T(8,128)(2,1)S(1)}, u32[]{:S(2)}, u32[]{:S(2)}) collective-permute-start(bf16[256,512]{1,0:T(8,128)(2,1)} %get-tuple-element.30), channel_id=1, source_target_pairs={{0,8},{8,16},{16,24},{24,32},{32,40},{40,48},{48,56},{56,64},{64,7... | collective-permute-start | bytes 786440 | tf_op jit(solution)/shard_map/ppermute | solution.py:31
  51.3 4.6 %collective-permute-start.1 = (bf16[256,512]{1,0:T(8,128)(2,1)S(1)}, bf16[256,512]{1,0:T(8,128)(2,1)S(1)}, u32[]{:S(2)}, u32[]{:S(2)}) collective-permute-start(bf16[256,512]{1,0:T(8,128)(2,1)S(1)} %get-tuple-element.31), channel_id=1, source_target_pairs={{8,0},{16,8},{24,16},{32,24},{40,32},{48,40},{56,48},{64,56},{72,6... | collective-permute-start | bytes 786440 | tf_op jit(solution)/shard_map/ppermute | solution.py:34
  56.0 2.3 copy.36
  58.3 5.1 %gather_fusion.2 = bf16[1024,512]{1,0:T(8,128)(2,1)} fusion(bf16[1024,512]{1,0:T(8,128)(2,1)S(1)} %bitcast.34, s32[1024]{0:T(1024)S(1)} %fusion.30), kind=kCustom, calls=%fused_computation.2 | custom fusion | bytes 2101248 | tf_op jit(solution)/shard_map/jit(_take)/gather | solution.py:131
  63.4 2.3 copy.35
  65.7 1.3 pad_maximum_fusion.2
  66.9 5.6 %gather_fusion.1 = bf16[1024,512]{1,0:T(8,128)(2,1)S(1)} fusion(bf16[1536,512]{1,0:T(8,128)(2,1)} %pad_maximum_fusion.2, s32[1024]{0:T(1024)S(1)} %fusion.29), kind=kCustom, calls=%fused_computation.1 | custom fusion | bytes 2101248 | tf_op jit(solution)/shard_map/jit(_take)/gather | solution.py:131
  72.5 1.3 copy.34
  73.8 1.8 broadcast_select_fusion
  75.7 3.3 multiply_convert_fusion.2
  79.1 0.8 fusion.42
  80.2 1.0 copy-done.1
  81.2 1.7 fusion.7
  82.9 2.9 copy.39
  85.8 8.7 %scatter_custom_fusion = f32[1024,512]{1,0:T(8,128)} fusion(s32[1024]{0:T(1024)S(1)} %copy-done.28, f32[1024,512]{1,0:T(8,128)} %copy.39, f32[]{:T(128)} %constant.51.clone.1), kind=kCustom, calls=%fused_computation.36 | custom fusion | flops 524288 | bytes 2097664 | tf_op jit(solution)/shard_map/scatter-add | solution.py:136
  94.5 1.7 convert_element_type.98
  96.2 32.0 %all_to_all.35 = bf16[8,128,512]{2,1,0:T(8,128)(2,1)} all-to-all(bf16[8,128,512]{2,1,0:T(8,128)(2,1)S(1)} %bitcast.37), channel_id=1, replica_groups=mesh['patch'=32,'shard'=8] {'shard'}, dimensions={0} | all-to-all | bytes 2097152 | tf_op jit(solution)/shard_map/all_to_all | solution.py:46
  128.2 1.4 reduce_sum.122
  130.0 1.5 fusion.43
  132.9 0.8 copy-done.9
  133.7 1.1 broadcast_in_dim.89
  134.8 5.2 %all-to-all-start.2 = ((bf16[8,128,512]{2,1,0:T(8,128)(2,1)}), bf16[8,128,512]{2,1,0:T(8,128)(2,1)}, u32[]{:S(2)}, u32[]{:S(2)}) async-start(bf16[8,128,512]{2,1,0:T(8,128)(2,1)} %broadcast_in_dim.89), calls=%async_computation.2 | async-start | bytes 2097152 | tf_op jit(solution)/shard_map/all_to_all | solution.py:11
  140.0 1.5 copy.37
  141.5 1.4 convolution_convert_fusion.1
  143.0 2.2 convolution_convert_fusion.2
  145.2 16.9 %all-to-all-done.2 = bf16[8,128,512]{2,1,0:T(8,128)(2,1)} async-done(((bf16[8,128,512]{2,1,0:T(8,128)(2,1)}), bf16[8,128,512]{2,1,0:T(8,128)(2,1)}, u32[]{:S(2)}, u32[]{:S(2)}) %all-to-all-start.2) | async-done | bytes 1048608 | tf_op jit(solution)/shard_map/all_to_all | solution.py:11
  162.1 2.8 bitcast_convert_fusion
  164.9 6.9 %gather_fusion.3 = f32[1024,512]{1,0:T(8,128)} fusion(f32[1024,512]{1,0:T(8,128)} %bitcast_convert_fusion, s32[1024]{0:T(1024)S(1)} %fusion.30), kind=kCustom, calls=%fused_computation.3 | custom fusion | bytes 4198400 | tf_op jit(solution)/shard_map/jit(_take)/gather | solution.py:150
  171.8 2.9 copy.40
  174.7 3.0 fusion.36
  181.2 1.2 multiply_convert_fusion
  183.1 1.9 convolution_convert_fusion
  185.0 2.0 pad_maximum_fusion
  186.9 6.0 %copy.47 = bf16[3584,512]{0,1:T(8,128)(2,1)} copy(bf16[3584,512]{1,0:T(8,128)(2,1)} %pad_maximum_fusion) | data formatting | bytes 7340032
  193.2 5.7 %fusion.45 = f32[1024,1536]{1,0:T(8,128)} fusion(bf16[1024,512]{1,0:T(8,128)(2,1)} %copy-done.38, bf16[1536,512]{1,0:T(8,128)(2,1)S(1)} %copy-done), kind=kOutput, calls=%fused_computation.108 | convolution fusion | flops 1610612736 | bytes 8912896 | tf_op jit(solution)/shard_map/dot_general | solution.py:76
  198.9 9.2 %scatter_custom_fusion.1 = f32[1536,512]{1,0:T(8,128)} fusion(s32[1024]{0:T(1024)} %param.13, f32[1024,1536]{1,0:T(8,128)} %fusion.45, f32[]{:T(128)} %constant.51.clone.1), kind=kCustom, calls=%fused_computation.14 | custom fusion | flops 524288 | bytes 5243392 | tf_op jit(solution)/shard_map/scatter-add | solution.py:155
  208.2 2.2 convert.12
  210.5 7.3 %collective-permute-start.2 = (bf16[256,512]{1,0:T(8,128)(2,1)S(1)}, bf16[256,512]{1,0:T(8,128)(2,1)S(1)}, u32[]{:S(2)}, u32[]{:S(2)}) collective-permute-start(bf16[256,512]{1,0:T(8,128)(2,1)S(1)} %get-tuple-element.28), channel_id=1, source_target_pairs={{0,8},{8,16},{16,24},{24,32},{32,40},{40,48},{48,56},{56,64},{64,7... | collective-permute-start | bytes 786440 | tf_op jit(solution)/shard_map/ppermute | solution.py:31
  217.8 1.5 slice.97
  219.3 10.2 %scatter_custom_fusion.2 = f32[1024,512]{1,0:T(8,128)} fusion(f32[1024,512]{1,0:T(8,128)} %slice.97, s32[1024]{0:T(1024)} %param.14, f32[1024,1536]{1,0:T(8,128)} %fusion.45), kind=kCustom, calls=%fused_computation.12 | custom fusion | flops 524288 | bytes 4194304 | tf_op jit(solution)/shard_map/scatter-add | solution.py:158
  229.5 10.1 %collective-permute-done.3 = bf16[256,512]{1,0:T(8,128)(2,1)} collective-permute-done((bf16[256,512]{1,0:T(8,128)(2,1)S(1)}, bf16[256,512]{1,0:T(8,128)(2,1)}, u32[]{:S(2)}, u32[]{:S(2)}) %collective-permute-start.3) | collective-permute-done | bytes 262176 | tf_op jit(solution)/shard_map/ppermute | solution.py:34
  239.6 5.0 %scatter_custom_fusion.3 = f32[1024,512]{1,0:T(8,128)} fusion(f32[1024,512]{1,0:T(8,128)} %scatter_custom_fusion.2, s32[256]{0:T(256)S(1)} %bitcast.44, bf16[256,512]{1,0:T(8,128)(2,1)} %collective-permute-done.3, bf16[]{:T(256)} %constant.83, bf16[256,512]{1,0:T(8,128)(2,1)S(1)} %get-tuple-element.28, bf16[256,512]{1,0:T(8,128)(2,1)S(1)} %get-tuple-element.29, ...), kind=kCustom, calls=%fused_computation.41 | custom fusion | flops 1179648 | bytes 3146240 | tf_op jit(solution)/shard_map/scatter-add | solution.py:166
  244.7 5.4 %scatter_custom_fusion.4 = f32[1024,512]{1,0:T(8,128)} fusion(f32[1024,512]{1,0:T(8,128)} %scatter_custom_fusion.3, s32[256]{0:T(256)S(1)} %bitcast.43, bf16[256,512]{1,0:T(8,128)(2,1)} %collective-permute-done.3, bf16[]{:T(256)} %constant.83, bf16[256,512]{1,0:T(8,128)(2,1)S(1)} %get-tuple-element.28, bf16[256,512]{1,0:T(8,128)(2,1)S(1)} %get-tuple-element.29, ...), kind=kCustom, calls=%fused_computation.44 | custom fusion | flops 1179648 | bytes 3146240 | tf_op jit(solution)/shard_map/scatter-add | solution.py:167
  250.0 2.7 convert_element_type.108
  252.8 95.5 %reduce-scatter.7.cloned.1.call-done = bf16[16,3584]{1,0:T(8,128)(2,1)} async-done(((bf16[512,3584]{1,0:T(8,128)(2,1)}), bf16[16,3584]{1,0:T(8,128)(2,1)}) %reduce-scatter.7.cloned.1.call-update) | async-done | bytes 114704
  349.1 40.1 %all_to_all.36 = bf16[8,512,16]{1,2,0:T(8,128)(2,1)S(1)} all-to-all(bf16[8,512,16]{1,2,0:T(8,128)(2,1)S(1)} %broadcast_in_dim.94), channel_id=1, replica_groups=mesh['patch'=32,'shard'=8] {'shard'}, dimensions={0} | all-to-all | bytes 262144 | tf_op jit(solution)/shard_map/all_to_all | solution.py:11
  389.9 4.1 all-to-all-start.4
  394.0 0.8 slice.105
  394.8 8.1 %all-to-all-done.4 = bf16[8,512,16]{1,2,0:T(8,128)(2,1)S(1)} async-done(((bf16[8,512,16]{1,2,0:T(8,128)(2,1)}), bf16[8,512,16]{1,2,0:T(8,128)(2,1)S(1)}, u32[]{:S(2)}, u32[]{:S(2)}) %all-to-all-start.4) | async-done | bytes 131104 | tf_op jit(solution)/shard_map/all_to_all | solution.py:11
  403.7 4.2 all-to-all-start.5
  407.8 3.1 slice.102
  411.0 2.9 copy.49
  413.9 0.8 slice.103
  414.7 4.0 all-to-all-done.5
  418.7 0.8 broadcast_in_dim.91
  419.5 4.0 all-to-all-start.3
  423.5 3.8 add_convert_fusion
  427.3 2.3 copy.46
  429.6 1.6 fusion.19
  433.2 2.7 all-to-all-done.3
  (123 shorter events, 12.2 us)
Async XLA Ops:
  7.2 68.5 %copy-start = (bf16[1536,512]{1,0:T(8,128)(2,1)S(1)}, bf16[1536,512]{1,0:T(8,128)(2,1)}, u32[]{:S(2)}) copy-start(bf16[1536,512]{1,0:T(8,128)(2,1)} %param.16) | copy-start | bytes 4718596
  7.2 12.1 %copy-start.25 = (s32[1,512]{1,0:T(1,128)S(1)}, s32[1,512]{1,0:T(1,128)}, u32[]{:S(2)}) copy-start(s32[1,512]{1,0:T(1,128)} %param.15) | copy-start | bytes 6148
  7.2 12.1 %copy-start.27 = (s32[1024]{0:T(1024)S(1)}, s32[1024]{0:T(1024)}, u32[]{:S(2)}) copy-start(s32[1024]{0:T(1024)} %param.13) | copy-start | bytes 12292
  9.3 33.9 %all-to-all-start = ((bf16[8,128,512]{2,1,0:T(8,128)(2,1)}), bf16[8,128,512]{2,1,0:T(8,128)(2,1)S(1)}, u32[]{:S(2)}, u32[]{:S(2)}) async-start(bf16[8,128,512]{2,1,0:T(8,128)(2,1)} %broadcast_in_dim.82), calls=%async_computation | async-start | bytes 2097152 | tf_op jit(solution)/shard_map/all_to_all | solution.py:11
  45.2 10.8 %copy-start.28 = (s32[1024]{0:T(1024)S(1)}, s32[1024]{0:T(1024)}, u32[]{:S(2)}) copy-start(s32[1024]{0:T(1024)} %param.14) | copy-start | bytes 12292
  46.1 19.6 %collective-permute-start = (bf16[256,512]{1,0:T(8,128)(2,1)}, bf16[256,512]{1,0:T(8,128)(2,1)S(1)}, u32[]{:S(2)}, u32[]{:S(2)}) collective-permute-start(bf16[256,512]{1,0:T(8,128)(2,1)} %get-tuple-element.30), channel_id=1, source_target_pairs={{0,8},{8,16},{16,24},{24,32},{32,40},{40,48},{48,56},{56,64},{64,7... | collective-permute-start | bytes 786440 | tf_op jit(solution)/shard_map/ppermute | solution.py:31
  51.3 14.3 %collective-permute-start.1 = (bf16[256,512]{1,0:T(8,128)(2,1)S(1)}, bf16[256,512]{1,0:T(8,128)(2,1)S(1)}, u32[]{:S(2)}, u32[]{:S(2)}) collective-permute-start(bf16[256,512]{1,0:T(8,128)(2,1)S(1)} %get-tuple-element.31), channel_id=1, source_target_pairs={{8,0},{16,8},{24,16},{32,24},{40,32},{48,40},{56,48},{64,56},{72,6... | collective-permute-start | bytes 786440 | tf_op jit(solution)/shard_map/ppermute | solution.py:34
  73.8 1.9 copy-start.5
  75.7 3.4 copy-start.12
  75.7 3.4 copy-start.14
  75.7 3.4 copy-start.22
  79.1 1.1 copy-start.16
  79.8 1.3 copy-start.1
  96.2 33.4 %copy-start.8 = (bf16[1024,512]{1,0:T(8,128)(2,1)S(1)}, bf16[1024,512]{1,0:T(8,128)(2,1)}, u32[]{:S(2)}) copy-start(bf16[1024,512]{1,0:T(8,128)(2,1)} %param.18) | copy-start | bytes 3145732
  96.2 33.4 %copy-start.11 = (bf16[128,512]{1,0:T(8,128)(2,1)S(1)}, bf16[128,512]{1,0:T(8,128)(2,1)}, u32[]{:S(2)}) copy-start(bf16[128,512]{1,0:T(8,128)(2,1)} %param.11) | copy-start | bytes 393220
  128.2 3.4 copy-start.19
  129.6 2.3 copy-start.33
  130.0 1.9 copy-start.24
  131.4 0.8 copy-start.29
  131.7 0.6 copy-start.31
  131.9 0.5 copy-start.34
  131.9 0.5 copy-start.36
  132.9 0.8 copy-start.9
  134.8 27.3 %all-to-all-start.2 = ((bf16[8,128,512]{2,1,0:T(8,128)(2,1)}), bf16[8,128,512]{2,1,0:T(8,128)(2,1)}, u32[]{:S(2)}, u32[]{:S(2)}) async-start(bf16[8,128,512]{2,1,0:T(8,128)(2,1)} %broadcast_in_dim.89), calls=%async_computation.2 | async-start | bytes 2097152 | tf_op jit(solution)/shard_map/all_to_all | solution.py:11
  139.9 3.0 copy-start.30
  139.9 3.0 copy-start.32
  140.0 3.0 copy-start.35
  140.0 3.0 copy-start.37
  140.0 208.4 %reduce-scatter.7.cloned.1.call-start = ((), (), s32[]{:S(2)}) async-start(), calls=%async_computation.10 | async-start | bytes 3784704
  174.7 3.0 copy-start.2
  174.7 3.5 copy-start.3
  178.2 1.2 copy-start.17
  179.4 1.0 copy-start.23
  179.4 1.8 copy-start.39
  181.2 1.3 copy-start.6
  181.2 1.5 copy-start.13
  181.2 1.9 copy-start.15
  183.1 1.9 copy-start.38
  183.1 1.9 copy-start.7
  183.1 1.9 copy-start.18
  193.0 236.7 %reduce-scatter.5.cloned.1.call-start = ((), (), s32[]{:S(2)}) async-start(), calls=%async_computation.9 | async-start | bytes 1179648 | tf_op jit(solution)/shard_map/reduce_scatter | solution.py:168
  208.2 9.6 %copy-start.26 = (s32[1,512]{1,0:T(1,128)S(1)}, s32[1,512]{1,0:T(1,128)}, u32[]{:S(2)}) copy-start(s32[1,512]{1,0:T(1,128)} %param.15) | copy-start | bytes 6148
  208.2 9.6 %copy-start.4 = (f32[1536,512]{1,0:T(8,128)S(1)}, f32[1536,512]{1,0:T(8,128)}, u32[]{:S(2)}) copy-start(f32[1536,512]{1,0:T(8,128)} %scatter_custom_fusion.1) | copy-start | bytes 9437188
  210.5 19.1 %collective-permute-start.2 = (bf16[256,512]{1,0:T(8,128)(2,1)S(1)}, bf16[256,512]{1,0:T(8,128)(2,1)S(1)}, u32[]{:S(2)}, u32[]{:S(2)}) collective-permute-start(bf16[256,512]{1,0:T(8,128)(2,1)S(1)} %get-tuple-element.28), channel_id=1, source_target_pairs={{0,8},{8,16},{16,24},{24,32},{32,40},{40,48},{48,56},{56,64},{64,7... | collective-permute-start | bytes 786440 | tf_op jit(solution)/shard_map/ppermute | solution.py:31
  217.8 21.8 %collective-permute-start.3 = (bf16[256,512]{1,0:T(8,128)(2,1)S(1)}, bf16[256,512]{1,0:T(8,128)(2,1)}, u32[]{:S(2)}, u32[]{:S(2)}) collective-permute-start(bf16[256,512]{1,0:T(8,128)(2,1)S(1)} %get-tuple-element.29), channel_id=1, source_target_pairs={{8,0},{16,8},{24,16},{32,24},{40,32},{48,40},{56,48},{64,56},{72,6... | collective-permute-start | bytes 786440 | tf_op jit(solution)/shard_map/ppermute | solution.py:34
  389.9 13.0 %all-to-all-start.4 = ((bf16[8,512,16]{1,2,0:T(8,128)(2,1)}), bf16[8,512,16]{1,2,0:T(8,128)(2,1)S(1)}, u32[]{:S(2)}, u32[]{:S(2)}) async-start(bf16[8,512,16]{1,2,0:T(8,128)(2,1)} %broadcast_in_dim.92), calls=%async_computation.5 | async-start | bytes 262144 | tf_op jit(solution)/shard_map/all_to_all | solution.py:11
  402.9 8.1 %copy-start.20 = (bf16[8,512,16]{1,2,0:T(8,128)(2,1)}, bf16[8,512,16]{1,2,0:T(8,128)(2,1)S(1)}, u32[]{:S(2)}) copy-start(bf16[8,512,16]{1,2,0:T(8,128)(2,1)S(1)} %all-to-all-done.4) | copy-start | bytes 393220
  403.7 15.0 %all-to-all-start.5 = ((bf16[8,1024,16]{1,2,0:T(8,128)(2,1)}), bf16[8,1024,16]{1,2,0:T(8,128)(2,1)S(1)}, u32[]{:S(2)}, u32[]{:S(2)}) async-start(bf16[8,1024,16]{1,2,0:T(8,128)(2,1)} %broadcast_in_dim.93), calls=%async_computation.6 | async-start | bytes 524288 | tf_op jit(solution)/shard_map/all_to_all | solution.py:11
  419.5 16.4 %all-to-all-start.3 = ((bf16[8,1536,16]{1,2,0:T(8,128)(2,1)}), bf16[8,1536,16]{1,2,0:T(8,128)(2,1)S(1)}, u32[]{:S(2)}, u32[]{:S(2)}) async-start(bf16[8,1536,16]{1,2,0:T(8,128)(2,1)} %broadcast_in_dim.91), calls=%async_computation.4 | async-start | bytes 786432 | tf_op jit(solution)/shard_map/all_to_all | solution.py:11
  427.3 2.3 copy-start.10
  427.3 4.6 %copy-start.21 = (bf16[8,512,16]{1,2,0:T(8,128)(2,1)S(1)}, bf16[8,512,16]{1,2,0:T(8,128)(2,1)}, u32[]{:S(2)}) copy-start(bf16[8,512,16]{1,2,0:T(8,128)(2,1)} %copy-done.20) | copy-start | bytes 393220
Sparse Core Ops, SparseCore 0:
  193.1 155.2 reduce-scatter.6
  350.9 65.6 reduce-scatter.4
where the time goes:
time: 445 us; the launch traced here: 443 us
  waiting for transfers between devices  161 us (36%)
  blocking collectives  72.1 us (16%)
  other arithmetic  69 us (16%)
  local copies, waits for them, and re-layouts  61.7 us (14%)
  starting transfers between devices  44.9 us (10%)
  matrix products  19.9 us (4%)
  between operations  14.6 us (3%)
    unnamed x3, waiting for transfers between devices  95.6 us
    all_to_all x5, waiting for transfers between devices, copy_for_each(): return lax.all_to_all(copies, axis, split_axis=0, concat_axis=0, tiled=True)  55.6 us
    all_to_all x1, blocking collectives, copy_for_each(): return lax.all_to_all(copies, axis, split_axis=0, concat_axis=0, tiled=True)  40.1 us
    all_to_all x1, blocking collectives, summed_on_arrival(): blocks = lax.all_to_all(split_up(x, dim, size), axis, 0, 0, tiled=True)  32 us
    all_to_all x5, starting transfers between devices, copy_for_each(): return lax.all_to_all(copies, axis, split_axis=0, concat_axis=0, tiled=True)  27.4 us
    unnamed x85, local copies, waits for them, and re-layouts  19.7 us
    ppermute x2, starting transfers between devices, padded(): lax.ppermute(lax.slice_in_dim(block, block.shape[dim] - width, None, axis...  12.5 us
    scatter-add x1, other arithmetic, body(): jax.ops.segment_sum(d_edge[:, 2 * width:], receivers, num_segments=patch_...  10.2 us
  transfers between devices with their start and end apart: 11, of which 7 were waited for; matrix products, arithmetic and copies ran while one was open for 17% of the time, Pallas kernels for 0%

commit v1 on v0

v1 whole, which is shorter than its diff:
```python
import functools

import jax
import jax.numpy as jnp
from jax import lax
from jax.experimental import pallas as pl
from jax.experimental.pallas import tpu as pltpu
from jax.sharding import PartitionSpec as P

epsilon = 1e-05
F32 = jnp.float32
BF16 = jnp.bfloat16
MIB = 1 << 20


def over_ring(x, by):
    count = lax.axis_size("shard")
    return lax.ppermute(x, "shard", [(i, (i + 2 * by) % count) for i in range(count)])


def to_partner(x):
    count = lax.axis_size("shard")
    return lax.ppermute(x, "shard", [(i, i ^ 1) for i in range(count)])


def to_patch(x, by):
    count = lax.axis_size("patch")
    return lax.ppermute(x, "patch", [(i, (i + by) % count) for i in range(count)])


def spread_over_shard(own):
    after = over_ring(own, -1)
    before = over_ring(own, 1)
    across = over_ring(own, 2)
    mine = [own, after, across, before]
    return mine + [to_partner(b) for b in mine]


def ring_sum_parts(chunks):
    return [over_ring(chunks[0], 1), over_ring(chunks[1], 2), over_ring(chunks[2], -1)]


def dot(a, b):
    return jnp.dot(a, b, preferred_element_type=F32)


def dot_nt(a, b):
    return lax.dot_general(a, b, (((1,), (1,)), ((), ())), preferred_element_type=F32)


def dot_tn(a, b):
    return lax.dot_general(a, b, (((0,), (0,)), ((), ())), preferred_element_type=F32)


def pick_rows(index_column, count, first=0):
    places = lax.broadcasted_iota(jnp.int32, (index_column.shape[0], count), 1) + first
    return jnp.where(places == index_column, 1.0, 0.0).astype(BF16)


def add_rows(index_row, count, first=0):
    places = lax.broadcasted_iota(jnp.int32, (count, index_row.shape[1]), 0) + first
    return jnp.where(places == index_row, 1.0, 0.0).astype(BF16)


def normalised(out):
    center = out - jnp.mean(out, axis=-1, keepdims=True)
    inv = lax.rsqrt(jnp.mean(center * center, axis=-1, keepdims=True) + epsilon)
    return center * inv, inv


def norm_backward(g, normed, inv):
    d = inv * (
        g
        - jnp.mean(g, axis=-1, keepdims=True)
        - normed * jnp.mean(g * normed, axis=-1, keepdims=True)
    )
    return d.astype(BF16)


def call(kernel, out_shapes, args, *, grid=None, in_specs=None, out_specs=None, scratch=(),
         flops=0, moved=0, vmem=32 * MIB):
    extra = {}
    if grid is not None:
        extra = dict(grid=grid, in_specs=in_specs, out_specs=out_specs)
    else:
        full = pl.BlockSpec(memory_space=pltpu.VMEM)
        extra = dict(in_specs=in_specs or [full] * len(args), out_specs=[full] * len(out_shapes))
    return pl.pallas_call(
        kernel,
        out_shape=out_shapes,
        scratch_shapes=list(scratch),
        compiler_params=pltpu.CompilerParams(vmem_limit_bytes=vmem),
        cost_estimate=pl.CostEstimate(flops=flops, bytes_accessed=moved, transcendentals=0),
        **extra,
    )(*args)


def shape(dims, dtype):
    return jax.ShapeDtypeStruct(dims, dtype)


def halo_rows_kernel(index, *refs):
    blocks, (low, high) = refs[:-2], refs[-2:]
    total = None
    for k, block in enumerate(blocks):
        part = dot(pick_rows(index[...], 128, 128 * k), block[...])
        total = part if total is None else total + part
    low[...] = total[:128].astype(BF16)
    high[...] = total[128:].astype(BF16)


def edge_forward_kernel(n_blocks, s_col, r_col, r_row, edge, *refs):
    blocks = refs[:n_blocks]
    (w1, w2, from_s, from_r, act_o, slope_o, normed_o, inv_o, keep_o, send_o, table, total) = refs[
        n_blocks:
    ]
    step = pl.program_id(0)

    @pl.when(step == 0)
    def _():
        for k, block in enumerate(blocks):
            table[pl.ds(128 * k, 128), :] = block[...]
        total[...] = jnp.zeros_like(total)

    rows_s = dot(pick_rows(s_col[...], 1536), table[...]).astype(BF16)
    rows_r = dot(pick_rows(r_col[...], 1024), table[pl.ds(0, 1024), :]).astype(BF16)
    from_s[...] = rows_s
    from_r[...] = rows_r
    pre = (
        dot(edge[...], w1[pl.ds(0, 512), :])
        + dot(rows_s, w1[pl.ds(512, 512), :])
        + dot(rows_r, w1[pl.ds(1024, 512), :])
    )
    sig = jax.nn.sigmoid(pre)
    act = (pre * sig).astype(BF16)
    act_o[...] = act
    slope_o[...] = sig * (1.0 + pre * (1.0 - sig))
    normed, inv = normalised(dot(act, w2[...]))
    normed_o[...] = normed
    inv_o[...] = inv
    edge_new = (edge[...].astype(F32) + normed).astype(BF16)
    total[...] += dot(add_rows(r_row[...], 1024), edge_new)

    @pl.when(step == pl.num_programs(0) - 1)
    def _():
        keep_o[...] = total[pl.ds(0, 512), :]
        send_o[...] = total[pl.ds(512, 512), :].astype(BF16)


def pair_sum_kernel(keep, came, own, one, two, three):
    both = keep[...] + came[...].astype(F32)
    own[...] = both[0:128]
    one[...] = both[128:256].astype(BF16)
    two[...] = both[256:384].astype(BF16)
    three[...] = both[384:512].astype(BF16)


def node_kernel(core, own, got1, got2, got3, node, grad, w1, w2, d_agg_o, part_o, keep_o, send_o, agg_s, act_s):
    agg = (
        own[...] + got1[...].astype(F32) + got2[...].astype(F32) + got3[...].astype(F32)
    ).astype(BF16)
    x = node[...]
    pre = dot(x, w1[pl.ds(0, 512), :]) + dot(agg, w1[pl.ds(512, 512), :])
    sig = jax.nn.sigmoid(pre)
    act = (pre * sig).astype(BF16)
    normed, inv = normalised(dot(act, w2[...]))
    g = grad[...].astype(F32)
    d_out = norm_backward(g, normed, inv)
    d_act = dot_nt(d_out, w2[...])
    d_pre = (d_act * (sig * (1.0 + pre * (1.0 - sig)))).astype(BF16)
    d_agg_o[...] = dot_nt(d_pre, w1[pl.ds(512, 512), :]).astype(BF16)
    part_o[...] = g + dot_nt(d_pre, w1[pl.ds(0, 512), :])
    agg_s[...] = agg
    act_s[...] = act
    mine = pl.multiple_of(core[0] * 256, 256)
    theirs = pl.multiple_of(256 - core[0] * 256, 256)
    for k, (left, right) in enumerate(((d_pre, node), (d_pre, agg_s), (d_out, act_s))):
        keep_o[:, pl.ds(256 * k, 256)] = dot_tn(left, right[:, pl.ds(mine, 256)])
        send_o[:, pl.ds(256 * k, 256)] = dot_tn(left, right[:, pl.ds(theirs, 256)]).astype(BF16)


def edge_backward_kernel(n_blocks, r_col, s_row, grad, normed, inv, slope, *refs):
    blocks = refs[:n_blocks]
    (w1, w2, d_out_o, d_pre_o, dxs_o, grad_o, keep_o, send_o, table, total) = refs[n_blocks:]
    step = pl.program_id(0)

    @pl.when(step == 0)
    def _():
        for k, block in enumerate(blocks):
            table[pl.ds(128 * k, 128), :] = block[...]
        total[...] = jnp.zeros_like(total)

    g = grad[...].astype(F32) + dot(pick_rows(r_col[...], 1024), table[...])
    d_out = norm_backward(g, normed[...], inv[...])
    d_out_o[...] = d_out
    d_pre = (dot_nt(d_out, w2[...]) * slope[...]).astype(BF16)
    d_pre_o[...] = d_pre
    dxs = dot_nt(d_pre, w1[pl.ds(512, 512), :]).astype(BF16)
    dxs_o[...] = dxs
    total[...] += dot(add_rows(s_row[...], 512, 1024), dxs)
    grad_o[...] = (g + dot_nt(d_pre, w1[pl.ds(0, 512), :])).astype(BF16)

    @pl.when(step == pl.num_programs(0) - 1)
    def _():
        keep_o[pl.ds(0, 128), :] = total[pl.ds(0, 128), :]
        keep_o[pl.ds(128, 128), :] = total[pl.ds(256, 128), :]
        send_o[pl.ds(0, 128), :] = total[pl.ds(128, 128), :].astype(BF16)
        send_o[pl.ds(128, 128), :] = total[pl.ds(384, 128), :].astype(BF16)


def edge_weights_kernel(core, d_pre, d_out, edge, from_s, from_r, act, keep_o, send_o):
    mine = pl.multiple_of(core[0] * 256, 256)
    theirs = pl.multiple_of(256 - core[0] * 256, 256)
    for k, (left, right) in enumerate(
        ((d_pre, edge), (d_pre, from_s), (d_pre, from_r), (d_out, act))
    ):
        keep_o[:, pl.ds(256 * k, 256)] = dot_tn(left[...], right[:, pl.ds(mine, 256)])
        send_o[:, pl.ds(256 * k, 256)] = dot_tn(
            left[...], right[:, pl.ds(theirs, 256)]
        ).astype(BF16)


def node_sums_kernel(s_row, r_row, d_pre, dxs, w_r, out, dxr):
    dxr[...] = dot_nt(d_pre[...], w_r[...]).astype(BF16)
    for k in range(4):
        out[pl.ds(256 * k, 256), :] = dot(add_rows(s_row[...], 256, 256 * k), dxs[...]) + dot(
            add_rows(r_row[...], 256, 256 * k), dxr[...]
        )


def pair_add_kernel(keep, came, low, high):
    both = keep[...] + came[...].astype(F32)
    low[...] = both[:128].astype(BF16)
    high[...] = both[128:].astype(BF16)


def returned_kernel(index, sums, low, high, keep_o, send_o):
    for k in range(4):
        rows = (
            sums[pl.ds(256 * k, 256), :]
            + dot(add_rows(index[:, pl.ds(0, 128)], 256, 256 * k), low[...])
            + dot(add_rows(index[:, pl.ds(128, 128)], 256, 256 * k), high[...])
        )
        if k < 2:
            keep_o[pl.ds(256 * k, 256), :] = rows
        else:
            send_o[pl.ds(256 * (k - 2), 256), :] = rows.astype(BF16)


def node_total_kernel(own, got1, got2, got3, part, out):
    out[...] = (
        own[...]
        + got1[...].astype(F32)
        + got2[...].astype(F32)
        + got3[...].astype(F32)
        + part[...]
    ).astype(BF16)


def weight_sum(keep, came):
    patches = lax.axis_size("patch")
    both = (keep + came.astype(F32)).astype(BF16)
    units, lanes = both.shape
    blocks = lax.all_to_all(
        both.reshape(patches, units // patches, lanes), "patch", 0, 0, tiled=True
    )
    return jnp.sum(blocks.astype(F32), axis=0)


def body(
    node_latent,
    edge_latent,
    senders,
    receivers,
    halo_list,
    w_edge_first,
    w_edge_second,
    w_node_first,
    w_node_second,
    grad_node_new,
    grad_edge_new,
):
    place = lax.axis_index("shard")
    core = place & 1
    chip = place >> 1

    table_blocks = spread_over_shard(node_latent)

    def relative(n):
        return (((n >> 7) & 1) ^ core) * 512 + (((n >> 8) - chip) & 3) * 128 + (n & 127)

    s_index = jnp.where(
        senders < 256,
        1024 + ((senders >> 7) ^ core) * 128 + (senders & 127),
        jnp.where(
            senders >= 1280,
            1280 + (((senders - 1280) >> 7) ^ core) * 128 + (senders & 127),
            relative(senders - 256),
        ),
    )
    r_index = relative(receivers)
    listed = relative(halo_list[0])
    half = jnp.concatenate(
        [
            lax.dynamic_slice(listed, (core * 128,), (128,)),
            lax.dynamic_slice(listed, (256 + core * 128,), (128,)),
        ]
    )
    s_col, s_row = s_index.reshape(1024, 1), s_index.reshape(1, 1024)
    r_col, r_row = r_index.reshape(1024, 1), r_index.reshape(1, 1024)
    core_word = core.reshape(1).astype(jnp.int32)

    to_prev, to_next = call(
        halo_rows_kernel,
        [shape((128, 512), BF16)] * 2,
        [half.reshape(256, 1)] + table_blocks,
        flops=2 * 256 * 1024 * 512,
        moved=2 * MIB,
        vmem=8 * MIB,
    )
    prev_mine = to_patch(to_next, 1)
    next_mine = to_patch(to_prev, -1)
    halo_blocks = [prev_mine, to_partner(prev_mine), next_mine, to_partner(next_mine)]

    tile = 256
    steps = 1024 // tile
    rows = lambda lanes: pl.BlockSpec((tile, lanes), lambda i: (i, 0))
    lanes_row = pl.BlockSpec((1, tile), lambda i: (0, i))
    fixed = lambda a, b: pl.BlockSpec((a, b), lambda i: (0, 0))
    from_s, from_r, act, slope, normed, inv, agg_keep, agg_send = call(
        functools.partial(edge_forward_kernel, 12),
        [
            shape((1024, 512), BF16),
            shape((1024, 512), BF16),
            shape((1024, 512), BF16),
            shape((1024, 512), F32),
            shape((1024, 512), F32),
            shape((1024, 1), F32),
            shape((512, 512), F32),
            shape((512, 512), BF16),
        ],
        [s_col, r_col, r_row, edge_latent]
        + table_blocks
        + halo_blocks
        + [w_edge_first, w_edge_second],
        grid=(steps,),
        in_specs=[rows(1), rows(1), lanes_row, rows(512)]
        + [fixed(128, 512)] * 12
        + [fixed(1536, 512), fixed(512, 512)],
        out_specs=[
            rows(512),
            rows(512),
            rows(512),
            rows(512),
            rows(512),
            rows(1),
            fixed(512, 512),
            fixed(512, 512),
        ],
        scratch=[pltpu.VMEM((1536, 512), BF16), pltpu.VMEM((1024, 512), F32)],
        flops=6_000_000_000,
        moved=12 * MIB,
    )
    agg_came = to_partner(agg_send)
    agg_own, agg_1, agg_2, agg_3 = call(
        pair_sum_kernel,
        [shape((128, 512), F32)] + [shape((128, 512), BF16)] * 3,
        [agg_keep, agg_came],
        moved=2 * MIB,
        vmem=8 * MIB,
    )
    smem = pl.BlockSpec(memory_space=pltpu.SMEM)
    vmem = pl.BlockSpec(memory_space=pltpu.VMEM)
    d_agg, node_part, n_keep, n_send = call(
        node_kernel,
        [
            shape((128, 512), BF16),
            shape((128, 512), F32),
            shape((512, 768), F32),
            shape((512, 768), BF16),
        ],
        [core_word, agg_own]
        + ring_sum_parts([agg_1, agg_2, agg_3])
        + [node_latent, grad_node_new, w_node_first, w_node_second],
        in_specs=[smem] + [vmem] * 8,
        scratch=[pltpu.VMEM((128, 512), BF16), pltpu.VMEM((128, 512), BF16)],
        flops=800_000_000,
        moved=5 * MIB,
        vmem=16 * MIB,
    )
    d_blocks = spread_over_shard(d_agg)
    n_came = to_partner(n_send)
    node_rows = weight_sum(n_keep, n_came)

    d_out, d_pre, dxs, grad_edge_latent, back_keep, back_send = call(
        functools.partial(edge_backward_kernel, 8),
        [
            shape((1024, 512), BF16),
            shape((1024, 512), BF16),
            shape((1024, 512), BF16),
            shape((1024, 512), BF16),
            shape((256, 512), F32),
            shape((256, 512), BF16),
        ],
        [r_col, s_row, grad_edge_new, normed, inv, slope]
        + d_blocks
        + [w_edge_first, w_edge_second],
        grid=(steps,),
        in_specs=[rows(1), lanes_row, rows(512), rows(512), rows(1), rows(512)]
        + [fixed(128, 512)] * 8
        + [fixed(1536, 512), fixed(512, 512)],
        out_specs=[rows(512)] * 4 + [fixed(256, 512)] * 2,
        scratch=[pltpu.VMEM((1024, 512), BF16), pltpu.VMEM((512, 512), F32)],
        flops=3_300_000_000,
        moved=12 * MIB,
    )
    back_came = to_partner(back_send)
    w_keep, w_send = call(
        edge_weights_kernel,
        [shape((512, 1024), F32), shape((512, 1024), BF16)],
        [core_word, d_pre, d_out, edge_latent, from_s, from_r, act],
        in_specs=[smem] + [vmem] * 6,
        flops=2_200_000_000,
        moved=9 * MIB,
    )
    w_came = to_partner(w_send)
    back_prev, back_next = call(
        pair_add_kernel,
        [shape((128, 512), BF16)] * 2,
        [back_keep, back_came],
        moved=MIB,
        vmem=8 * MIB,
    )
    got_next = to_patch(back_prev, -1)
    got_prev = to_patch(back_next, 1)
    (sums,) = call(
        node_sums_kernel,
        [shape((1024, 512), F32)],
        [s_row, r_row, d_pre, dxs, lax.slice_in_dim(w_edge_first, 1024, 1536, axis=0)],
        scratch=[pltpu.VMEM((1024, 512), BF16)],
        flops=2_700_000_000,
        moved=5 * MIB,
    )
    edge_rows = weight_sum(w_keep, w_came)
    node_keep, node_send = call(
        returned_kernel,
        [shape((512, 512), F32), shape((512, 512), BF16)],
        [half.reshape(1, 256), sums, got_prev, got_next],
        flops=300_000_000,
        moved=4 * MIB,
        vmem=16 * MIB,
    )
    node_came = to_partner(node_send)
    t_own, t_1, t_2, t_3 = call(
        pair_sum_kernel,
        [shape((128, 512), F32)] + [shape((128, 512), BF16)] * 3,
        [node_keep, node_came],
        moved=2 * MIB,
        vmem=8 * MIB,
    )
    (grad_node_latent,) = call(
        node_total_kernel,
        [shape((128, 512), BF16)],
        [t_own] + ring_sum_parts([t_1, t_2, t_3]) + [node_part],
        moved=MIB,
        vmem=8 * MIB,
    )

    weight_rows = jnp.concatenate([edge_rows, node_rows], axis=1)
    sent = weight_rows.astype(BF16)
    for by in (1, 2, 3):
        weight_rows = weight_rows + over_ring(sent, by).astype(F32)
    other = to_partner(weight_rows.astype(BF16)).astype(F32)
    low = jnp.where(core == 0, weight_rows, other)
    high = jnp.where(core == 0, other, weight_rows)

    def joined(first, count):
        parts = []
        for k in range(first, first + count):
            parts += [low[:, 256 * k : 256 * k + 256], high[:, 256 * k : 256 * k + 256]]
        return jnp.concatenate(parts, axis=1).T

    return (
        grad_node_latent,
        grad_edge_latent,
        joined(0, 3),
        joined(3, 1),
        joined(4, 2),
        joined(6, 1),
    )


def solution(mesh):
    split = P(("patch", "shard"), None)
    ids = P(("patch", "shard"))
    in_specs = (split, split, ids, ids, P("patch", None), P(), P(), P(), P(), split, split)
    out_specs = (split, split) + (P(None, "patch"),) * 4
    return jax.shard_map(body, mesh=mesh, in_specs=in_specs, out_specs=out_specs, check_vma=False)
```

time: 445 us -> 186 us (0.42)
  waiting for transfers between devices: 161 us -> 49.8 us
  blocking collectives: 72.1 us -> 0 us
  other arithmetic: 69 us -> 8.5 us
  local copies, waits for them, and re-layouts: 61.7 us -> 15.9 us
  starting transfers between devices: 44.9 us -> 83.2 us
  Pallas kernels: 0 us -> 27 us
  matrix products: 19.9 us -> 0 us
  between operations: 14.6 us -> 1 us
    unnamed x3 -> x0, waiting for transfers between devices: 95.6 us -> none
    all_to_all x2 -> x0, blocking collectives: 72.1 us -> none  [the longest x1 40.1 us: copy_for_each(): return lax.all_to_all(copies, axis, split_axis=0, concat_axis=0, tiled=True)]
    ppermute x4 -> x35, starting transfers between devices: 17.2 us -> 72.1 us  [the longest x15 37.2 us: over_ring(): lax.ppermute(x, 'shard', [(i, (i + 2 * by) % count) for i in range(count)])]
    all_to_all x5 -> x2, waiting for transfers between devices: 55.6 us -> 1.73 us  [weight_sum(): lax.all_to_all(both.reshape(patches, units // patches, lanes), 'patch', 0...]
    scatter-add x5 -> x0, other arithmetic: 38.6 us -> none  [the longest x1 10.2 us: body(): jax.ops.segment_sum(d_edge[:, 2 * width:], receivers, num_segments=patch_...]
    ppermute x4 -> x35, waiting for transfers between devices: 10.1 us -> 48.1 us  [the longest x15 27.6 us: over_ring(): lax.ppermute(x, 'shard', [(i, (i + 2 * by) % count) for i in range(count)])]
    pallas_call x0 -> x11, Pallas kernels: none -> 27 us  [call(): pl.pallas_call(kernel, out_shape=out_shapes, scratch_shapes=list(scratch)...]
    gather x7 -> x0, local copies, waits for them, and re-layouts: 26 us -> none  [the longest x2 9.81 us: body(): jnp.take(spread, receivers, axis=0)]
  transfers between devices with their start and end apart: 11 -> 37, of which waited for: 7 -> 19; matrix products, arithmetic and copies ran while one was open for 17% -> 3% of each run, Pallas kernels for 0% -> 7%
where the time goes in v1:
time: 186 us; the launch traced here: 185 us
  starting transfers between devices  83.2 us (45%)
  waiting for transfers between devices  49.8 us (27%)
  Pallas kernels  27 us (15%)
  local copies, waits for them, and re-layouts  15.9 us (9%)
  other arithmetic  8.5 us (5%)
    ppermute x15, starting transfers between devices, over_ring(): lax.ppermute(x, 'shard', [(i, (i + 2 * by) % count) for i in range(count)])  37.2 us
    ppermute x15, waiting for transfers between devices, over_ring(): lax.ppermute(x, 'shard', [(i, (i + 2 * by) % count) for i in range(count)])  27.6 us
    pallas_call x11, Pallas kernels, call(): pl.pallas_call(kernel, out_shape=out_shapes, scratch_shapes=list(scratch)...  27 us
    ppermute x16, starting transfers between devices, to_partner(): return lax.ppermute(x, 'shard', [(i, i ^ 1) for i in range(count)])  23.1 us
    unnamed x62, local copies, waits for them, and re-layouts  15.2 us
    ppermute x4, waiting for transfers between devices, to_patch(): lax.ppermute(x, 'patch', [(i, (i + by) % count) for i in range(count)])  12.9 us
    ppermute x4, starting transfers between devices, to_patch(): lax.ppermute(x, 'patch', [(i, (i + by) % count) for i in range(count)])  11.8 us
    all_to_all x2, starting transfers between devices, weight_sum(): lax.all_to_all(both.reshape(patches, units // patches, lanes), 'patch', 0...  11.1 us
  transfers between devices with their start and end apart: 37, of which 19 were waited for; matrix products, arithmetic and copies ran while one was open for 3% of the time, Pallas kernels for 7%

profile of v1, /device:TPU:1, one launch (start us, length us, event | category | flops | bytes accessed | tf_op | source)
XLA Modules:
  0.0 185.5 jit_solution(11479407572024739636)
XLA Ops:
  0.6 6.9 %collective-permute-start = (bf16[128,512]{1,0:T(8,128)(2,1)}, bf16[128,512]{1,0:T(8,128)(2,1)S(1)}, u32[]{:S(2)}, u32[]{:S(2)}) collective-permute-start(bf16[128,512]{1,0:T(8,128)(2,1)} %node.1), channel_id=1, source_target_pairs={{0,6},{1,7},{2,0},{3,1},{4,2},{5,3},{6,4},{7,5},{8,14},{9,15},{10,... | collective-permute-start | bytes 393224 | tf_op jit(solution)/shard_map/ppermute | solution.py:18
  7.6 1.0 collective-permute-start.1
  8.5 2.3 %collective-permute-start.2 = (bf16[128,512]{1,0:T(8,128)(2,1)}, bf16[128,512]{1,0:T(8,128)(2,1)S(1)}, u32[]{:S(2)}, u32[]{:S(2)}) collective-permute-start(bf16[128,512]{1,0:T(8,128)(2,1)} %node.1), channel_id=1, source_target_pairs={{0,2},{1,3},{2,4},{3,5},{4,6},{5,7},{6,0},{7,1},{8,10},{9,11},{10,... | collective-permute-start | bytes 393224 | tf_op jit(solution)/shard_map/ppermute | solution.py:18
  10.8 1.5 collective-permute-start.3
  13.0 7.0 %collective-permute-start.4 = (bf16[128,512]{1,0:T(8,128)(2,1)S(1)}, bf16[128,512]{1,0:T(8,128)(2,1)S(1)}, u32[]{:S(2)}, u32[]{:S(2)}) collective-permute-start(bf16[128,512]{1,0:T(8,128)(2,1)S(1)} %collective-permute-done.refs_1_), channel_id=1, source_target_pairs={{0,1},{1,0},{2,3},{3,2},{4,5},{5,4},{6,7},{7,6},{8,9},{9,8},{10,11... | collective-permute-start | bytes 393224 | tf_op jit(solution)/shard_map/ppermute | solution.py:23
  20.0 1.7 collective-permute-start.5
  24.8 5.9 %collective-permute-start.9 = (bf16[128,512]{1,0:T(8,128)(2,1)S(1)}, bf16[128,512]{1,0:T(8,128)(2,1)}, u32[]{:S(2)}, u32[]{:S(2)}) collective-permute-start(bf16[128,512]{1,0:T(8,128)(2,1)S(1)} %get-tuple-element.41), channel_id=1, source_target_pairs={{0,248},{8,0},{16,8},{24,16},{32,24},{40,32},{48,40},{56,48},{64,5... | collective-permute-start | bytes 393224 | tf_op jit(solution)/shard_map/ppermute | solution.py:28
  30.7 2.5 %collective-permute-done.9.refs_10_ = bf16[128,512]{1,0:T(8,128)(2,1)} collective-permute-done((bf16[128,512]{1,0:T(8,128)(2,1)S(1)}, bf16[128,512]{1,0:T(8,128)(2,1)}, u32[]{:S(2)}, u32[]{:S(2)}) %collective-permute-start.9) | collective-permute-done | bytes 131104 | tf_op jit(solution)/shard_map/ppermute | solution.py:28
  33.2 2.0 %collective-permute-start.10 = (bf16[128,512]{1,0:T(8,128)(2,1)}, bf16[128,512]{1,0:T(8,128)(2,1)}, u32[]{:S(2)}, u32[]{:S(2)}) collective-permute-start(bf16[128,512]{1,0:T(8,128)(2,1)} %collective-permute-done.9.refs_10_), channel_id=1, source_target_pairs={{0,1},{1,0},{2,3},{3,2},{4,5},{5,4},{6,7},{7,6},{8,9},{9,8},{10,11... | collective-permute-start | bytes 393224 | tf_op jit(solution)/shard_map/ppermute | solution.py:23
  35.2 4.2 %collective-permute-done.7.refs_8_ = bf16[128,512]{1,0:T(8,128)(2,1)} collective-permute-done((bf16[128,512]{1,0:T(8,128)(2,1)S(1)}, bf16[128,512]{1,0:T(8,128)(2,1)}, u32[]{:S(2)}, u32[]{:S(2)}) %collective-permute-start.7) | collective-permute-done | bytes 131104 | tf_op jit(solution)/shard_map/ppermute | solution.py:28
  39.5 1.5 collective-permute-start.8
  42.3 0.9 copy-done.4
  43.2 1.2 copy-done.7
  44.4 1.0 copy-done.10
  45.5 10.5 %shard_map.155 = (bf16[1024,512]{1,0:T(8,128)(2,1)S(1)}, bf16[1024,512]{1,0:T(8,128)(2,1)S(1)}, bf16[1024,512]{1,0:T(8,128)(2,1)S(1)}, f32[1024,512]{1,0:T(8,128...) custom-call(s32[1024,1]{1,0:T(8,128)S(1)} %copy.18.s_col, ...), custom_call_target="tpu_custom_call" | custom-call | flops 6000000000 | bytes 12582912 | tf_op jit(solution)/shard_map/pallas_call | solution.py:88
  56.0 1.0 copy-done.19
  57.4 1.5 collective-permute-done.11.came
  59.1 1.9 %collective-permute-start.12 = (bf16[128,512]{1,0:T(8,128)(2,1)S(1)}, bf16[128,512]{1,0:T(8,128)(2,1)S(1)}, u32[]{:S(2)}, u32[]{:S(2)}) collective-permute-start(bf16[128,512]{1,0:T(8,128)(2,1)S(1)} %get-tuple-element.48), channel_id=1, source_target_pairs={{0,2},{1,3},{2,4},{3,5},{4,6},{5,7},{6,0},{7,1},{8,10},{9,11},{10,... | collective-permute-start | bytes 393224 | tf_op jit(solution)/shard_map/ppermute | solution.py:18
  61.0 4.1 %collective-permute-start.13 = (bf16[128,512]{1,0:T(8,128)(2,1)S(1)}, bf16[128,512]{1,0:T(8,128)(2,1)S(1)}, u32[]{:S(2)}, u32[]{:S(2)}) collective-permute-start(bf16[128,512]{1,0:T(8,128)(2,1)S(1)} %get-tuple-element.49), channel_id=1, source_target_pairs={{0,4},{1,5},{2,6},{3,7},{4,0},{5,1},{6,2},{7,3},{8,12},{9,13},{10,... | collective-permute-start | bytes 393224 | tf_op jit(solution)/shard_map/ppermute | solution.py:18
  65.0 2.8 %collective-permute-start.14 = (bf16[128,512]{1,0:T(8,128)(2,1)S(1)}, bf16[128,512]{1,0:T(8,128)(2,1)S(1)}, u32[]{:S(2)}, u32[]{:S(2)}) collective-permute-start(bf16[128,512]{1,0:T(8,128)(2,1)S(1)} %get-tuple-element.50), channel_id=1, source_target_pairs={{0,6},{1,7},{2,0},{3,1},{4,2},{5,3},{6,4},{7,5},{8,14},{9,15},{10,... | collective-permute-start | bytes 393224 | tf_op jit(solution)/shard_map/ppermute | solution.py:18
  67.8 1.5 collective-permute-done.12.got1
  69.2 8.1 %collective-permute-done.13.got2 = bf16[128,512]{1,0:T(8,128)(2,1)S(1)} collective-permute-done((bf16[128,512]{1,0:T(8,128)(2,1)S(1)}, bf16[128,512]{1,0:T(8,128)(2,1)S(1)}, u32[]{:S(2)}, u32[]{:S(2)}) %collective-permute-start.13) | collective-permute-done | bytes 131104 | tf_op jit(solution)/shard_map/ppermute | solution.py:18
  77.3 1.8 shard_map.157
  79.8 1.9 %collective-permute-start.15 = (bf16[128,512]{1,0:T(8,128)(2,1)S(1)}, bf16[128,512]{1,0:T(8,128)(2,1)S(1)}, u32[]{:S(2)}, u32[]{:S(2)}) collective-permute-start(bf16[128,512]{1,0:T(8,128)(2,1)S(1)} %get-tuple-element.51.refs_0_), channel_id=1, source_target_pairs={{0,6},{1,7},{2,0},{3,1},{4,2},{5,3},{6,4},{7,5},{8,14},{9,15},{10,... | collective-permute-start | bytes 393224 | tf_op jit(solution)/shard_map/ppermute | solution.py:18
  81.6 1.4 collective-permute-start.16
  83.1 2.3 %collective-permute-start.17 = (bf16[128,512]{1,0:T(8,128)(2,1)S(1)}, bf16[128,512]{1,0:T(8,128)(2,1)S(1)}, u32[]{:S(2)}, u32[]{:S(2)}) collective-permute-start(bf16[128,512]{1,0:T(8,128)(2,1)S(1)} %get-tuple-element.51.refs_0_), channel_id=1, source_target_pairs={{0,2},{1,3},{2,4},{3,5},{4,6},{5,7},{6,0},{7,1},{8,10},{9,11},{10,... | collective-permute-start | bytes 393224 | tf_op jit(solution)/shard_map/ppermute | solution.py:18
  85.4 0.9 collective-permute-start.18
  86.3 2.8 %collective-permute-done.15.refs_1_ = bf16[128,512]{1,0:T(8,128)(2,1)S(1)} collective-permute-done((bf16[128,512]{1,0:T(8,128)(2,1)S(1)}, bf16[128,512]{1,0:T(8,128)(2,1)S(1)}, u32[]{:S(2)}, u32[]{:S(2)}) %collective-permute-start.15) | collective-permute-done | bytes 131104 | tf_op jit(solution)/shard_map/ppermute | solution.py:18
  89.2 1.0 collective-permute-start.19
  90.1 6.2 %collective-permute-done.16.refs_2_ = bf16[128,512]{1,0:T(8,128)(2,1)S(1)} collective-permute-done((bf16[128,512]{1,0:T(8,128)(2,1)S(1)}, bf16[128,512]{1,0:T(8,128)(2,1)S(1)}, u32[]{:S(2)}, u32[]{:S(2)}) %collective-permute-start.16) | collective-permute-done | bytes 131104 | tf_op jit(solution)/shard_map/ppermute | solution.py:18
  96.9 1.0 collective-permute-done.20.refs_6_
  98.2 6.9 %shard_map.158 = (bf16[1024,512]{1,0:T(8,128)(2,1)S(1)}, bf16[1024,512]{1,0:T(8,128)(2,1)S(1)}, bf16[1024,512]{1,0:T(8,128)(2,1)S(1)}, bf16[1024,512]{1,0:T(8,12...) custom-call(s32[1024,1]{1,0:T(8,128)S(1)} %copy.20.r_col, s32[1,1024]{1,0:T(1,128)S(1)} %bitcast.24, ...), custom_call_target="tpu_custom_call" | custom-call | flops 3300000000 | bytes 12582912 | tf_op jit(solution)/shard_map/pallas_call | solution.py:88
  105.1 1.0 copy-done.26
  106.1 1.1 add_convert_fusion.1
  107.8 4.6 %all-to-all-start.1 = ((bf16[32,16,768]{2,1,0:T(8,128)(2,1)}), bf16[32,16,768]{2,1,0:T(8,128)(2,1)}, u32[]{:S(2)}, u32[]{:S(2)}) async-start(bf16[32,16,768]{2,1,0:T(8,128)(2,1)} %bitcast.29), calls=%async_computation.1 | async-start | bytes 1572864 | tf_op jit(solution)/shard_map/all_to_all | solution.py:264
  112.4 1.2 copy-done.16
  113.7 1.2 copy-done.18
  114.9 1.2 copy-done.20
  116.1 1.2 copy-done.22
  117.3 1.2 copy-done.25
  118.6 2.4 %shard_map.164 = (f32[512,1024]{1,0:T(8,128)S(1)}, bf16[512,1024]{1,0:T(8,128)(2,1)S(1)}) custom-call(s32[1]{0:T(128)} %bitcast.8.core, bf16[1024,512]{1,0:T(8,128)(2,1)S(1)} %copy-done.22, bf16[1024,512]{1,0:T(8,128)(2,1)S(1)} %copy-done.25, bf16[1024,512]{1,0:T(8,128)(2,1)S(1)} %copy-done.8, bf16[1024,512]{1,0:T(8,128)(2,1)S(1)} %copy-done.16, ...), custom_call_target="tpu_custom_call" | custom-call | flops 2200000000 | bytes 9437184 | tf_op jit(solution)/shard_map/pallas_call | solution.py:88
  121.4 2.3 %collective-permute-done.29 = bf16[512,1024]{1,0:T(8,128)(2,1)S(1)} collective-permute-done((bf16[512,1024]{1,0:T(8,128)(2,1)S(1)}, bf16[512,1024]{1,0:T(8,128)(2,1)S(1)}, u32[]{:S(2)}, u32[]{:S(2)}) %collective-permute-start.29) | collective-permute-done | bytes 1048608 | tf_op jit(solution)/shard_map/ppermute | solution.py:23
  123.7 1.4 add_convert_fusion
  125.1 1.7 all-to-all-done.1
  126.8 6.5 %all-to-all-start = ((bf16[32,16,1024]{2,1,0:T(8,128)(2,1)}), bf16[32,16,1024]{2,1,0:T(8,128)(2,1)}, u32[]{:S(2)}, u32[]{:S(2)}) async-start(bf16[32,16,1024]{2,1,0:T(8,128)(2,1)} %bitcast.28), calls=%async_computation | async-start | bytes 2097152 | tf_op jit(solution)/shard_map/all_to_all | solution.py:264
  133.3 1.0 collective-permute-start.22
  134.3 1.1 collective-permute-done.22.came
  135.5 1.5 collective-permute-start.23
  137.0 4.4 %collective-permute-start.24 = (bf16[128,512]{1,0:T(8,128)(2,1)S(1)}, bf16[128,512]{1,0:T(8,128)(2,1)S(1)}, u32[]{:S(2)}, u32[]{:S(2)}) collective-permute-start(bf16[128,512]{1,0:T(8,128)(2,1)S(1)} %get-tuple-element.57), channel_id=1, source_target_pairs={{0,248},{8,0},{16,8},{24,16},{32,24},{40,32},{48,40},{56,48},{64,5... | collective-permute-start | bytes 393224 | tf_op jit(solution)/shard_map/ppermute | solution.py:28
  141.4 1.2 copy-done.23
  142.7 1.2 copy-done.27
  143.9 2.9 %shard_map.159.sums = f32[1024,512]{1,0:T(8,128)S(1)} custom-call(s32[1,1024]{1,0:T(1,128)S(1)} %bitcast.25, s32[1,1024]{1,0:T(1,128)S(1)} %bitcast.22, bf16[1024,512]{1,0:T(8,128)(2,1)S(1)} %copy-done.23, bf16[1024,512]{1,0:T(8,128)(2,1)S(1)} %copy-done.27, bf16[512,512]{1,0:T(8,128)(2,1)S(1)} %slice.45.w_r), custom_call_target="tpu_custom_call" | custom-call | flops 2700000000 | bytes 5242880 | tf_op jit(solution)/shard_map/pallas_call | solution.py:88
  146.8 6.2 %collective-permute-done.23.low = bf16[128,512]{1,0:T(8,128)(2,1)S(1)} collective-permute-done((bf16[128,512]{1,0:T(8,128)(2,1)S(1)}, bf16[128,512]{1,0:T(8,128)(2,1)S(1)}, u32[]{:S(2)}, u32[]{:S(2)}) %collective-permute-start.23) | collective-permute-done | bytes 131104 | tf_op jit(solution)/shard_map/ppermute | solution.py:28
  153.7 2.7 %collective-permute-start.25 = (bf16[512,512]{1,0:T(8,128)(2,1)S(1)}, bf16[512,512]{1,0:T(8,128)(2,1)S(1)}, u32[]{:S(2)}, u32[]{:S(2)}) collective-permute-start(bf16[512,512]{1,0:T(8,128)(2,1)S(1)} %get-tuple-element.59), channel_id=1, source_target_pairs={{0,1},{1,0},{2,3},{3,2},{4,5},{5,4},{6,7},{7,6},{8,9},{9,8},{10,11... | collective-permute-start | bytes 1572872 | tf_op jit(solution)/shard_map/ppermute | solution.py:23
  156.4 1.3 convert_reduce_fusion.1
  157.7 1.4 convert_reduce_fusion
  159.6 4.4 %collective-permute-start.32 = (bf16[16,1792]{1,0:T(8,128)(2,1)S(1)}, bf16[16,1792]{1,0:T(8,128)(2,1)S(1)}, u32[]{:S(2)}, u32[]{:S(2)}) collective-permute-start(bf16[16,1792]{1,0:T(8,128)(2,1)S(1)} %fusion), channel_id=1, source_target_pairs={{0,4},{1,5},{2,6},{3,7},{4,0},{5,1},{6,2},{7,3},{8,12},{9,13},{10,... | collective-permute-start | bytes 172040 | tf_op jit(solution)/shard_map/ppermute | solution.py:18
  164.0 2.2 %collective-permute-start.33 = (bf16[16,1792]{1,0:T(8,128)(2,1)S(1)}, bf16[16,1792]{1,0:T(8,128)(2,1)S(1)}, u32[]{:S(2)}, u32[]{:S(2)}) collective-permute-start(bf16[16,1792]{1,0:T(8,128)(2,1)S(1)} %fusion), channel_id=1, source_target_pairs={{0,6},{1,7},{2,0},{3,1},{4,2},{5,3},{6,4},{7,5},{8,14},{9,15},{10,... | collective-permute-start | bytes 172040 | tf_op jit(solution)/shard_map/ppermute | solution.py:18
  166.5 1.9 %collective-permute-start.27 = (bf16[128,512]{1,0:T(8,128)(2,1)S(1)}, bf16[128,512]{1,0:T(8,128)(2,1)S(1)}, u32[]{:S(2)}, u32[]{:S(2)}) collective-permute-start(bf16[128,512]{1,0:T(8,128)(2,1)S(1)} %get-tuple-element.62), channel_id=1, source_target_pairs={{0,4},{1,5},{2,6},{3,7},{4,0},{5,1},{6,2},{7,3},{8,12},{9,13},{10,... | collective-permute-start | bytes 393224 | tf_op jit(solution)/shard_map/ppermute | solution.py:18
  168.5 3.4 %collective-permute-start.28 = (bf16[128,512]{1,0:T(8,128)(2,1)S(1)}, bf16[128,512]{1,0:T(8,128)(2,1)S(1)}, u32[]{:S(2)}, u32[]{:S(2)}) collective-permute-start(bf16[128,512]{1,0:T(8,128)(2,1)S(1)} %get-tuple-element.63), channel_id=1, source_target_pairs={{0,6},{1,7},{2,0},{3,1},{4,2},{5,3},{6,4},{7,5},{8,14},{9,15},{10,... | collective-permute-start | bytes 393224 | tf_op jit(solution)/shard_map/ppermute | solution.py:18
  171.9 1.8 collective-permute-start.34
  173.7 1.9 %collective-permute-done.26.got1 = bf16[128,512]{1,0:T(8,128)(2,1)S(1)} collective-permute-done((bf16[128,512]{1,0:T(8,128)(2,1)S(1)}, bf16[128,512]{1,0:T(8,128)(2,1)S(1)}, u32[]{:S(2)}, u32[]{:S(2)}) %collective-permute-start.26) | collective-permute-done | bytes 131104 | tf_op jit(solution)/shard_map/ppermute | solution.py:18
  175.6 5.6 %collective-permute-done.27.got2 = bf16[128,512]{1,0:T(8,128)(2,1)S(1)} collective-permute-done((bf16[128,512]{1,0:T(8,128)(2,1)S(1)}, bf16[128,512]{1,0:T(8,128)(2,1)S(1)}, u32[]{:S(2)}, u32[]{:S(2)}) %collective-permute-start.27) | collective-permute-done | bytes 131104 | tf_op jit(solution)/shard_map/ppermute | solution.py:18
  181.2 1.6 collective-permute-done.28.got3
  (103 shorter events, 12.4 us)
Async XLA Ops:
  0.6 41.7 %copy-start = (bf16[1536,512]{1,0:T(8,128)(2,1)S(1)}, bf16[1536,512]{1,0:T(8,128)(2,1)}, u32[]{:S(2)}) copy-start(bf16[1536,512]{1,0:T(8,128)(2,1)} %refs_8_.1) | copy-start | bytes 4718596
  0.6 12.4 %collective-permute-start = (bf16[128,512]{1,0:T(8,128)(2,1)}, bf16[128,512]{1,0:T(8,128)(2,1)S(1)}, u32[]{:S(2)}, u32[]{:S(2)}) collective-permute-start(bf16[128,512]{1,0:T(8,128)(2,1)} %node.1), channel_id=1, source_target_pairs={{0,6},{1,7},{2,0},{3,1},{4,2},{5,3},{6,4},{7,5},{8,14},{9,15},{10,... | collective-permute-start | bytes 393224 | tf_op jit(solution)/shard_map/ppermute | solution.py:18
  7.6 12.5 %collective-permute-start.1 = (bf16[128,512]{1,0:T(8,128)(2,1)}, bf16[128,512]{1,0:T(8,128)(2,1)S(1)}, u32[]{:S(2)}, u32[]{:S(2)}) collective-permute-start(bf16[128,512]{1,0:T(8,128)(2,1)} %node.1), channel_id=1, source_target_pairs={{0,4},{1,5},{2,6},{3,7},{4,0},{5,1},{6,2},{7,3},{8,12},{9,13},{10,... | collective-permute-start | bytes 393224 | tf_op jit(solution)/shard_map/ppermute | solution.py:18
  8.5 13.2 %collective-permute-start.2 = (bf16[128,512]{1,0:T(8,128)(2,1)}, bf16[128,512]{1,0:T(8,128)(2,1)S(1)}, u32[]{:S(2)}, u32[]{:S(2)}) collective-permute-start(bf16[128,512]{1,0:T(8,128)(2,1)} %node.1), channel_id=1, source_target_pairs={{0,2},{1,3},{2,4},{3,5},{4,6},{5,7},{6,0},{7,1},{8,10},{9,11},{10,... | collective-permute-start | bytes 393224 | tf_op jit(solution)/shard_map/ppermute | solution.py:18
  10.8 11.1 %collective-permute-start.3 = (bf16[128,512]{1,0:T(8,128)(2,1)}, bf16[128,512]{1,0:T(8,128)(2,1)S(1)}, u32[]{:S(2)}, u32[]{:S(2)}) collective-permute-start(bf16[128,512]{1,0:T(8,128)(2,1)} %node.1), channel_id=1, source_target_pairs={{0,1},{1,0},{2,3},{3,2},{4,5},{5,4},{6,7},{7,6},{8,9},{9,8},{10,11... | collective-permute-start | bytes 393224 | tf_op jit(solution)/shard_map/ppermute | solution.py:23
  13.0 8.9 %collective-permute-start.4 = (bf16[128,512]{1,0:T(8,128)(2,1)S(1)}, bf16[128,512]{1,0:T(8,128)(2,1)S(1)}, u32[]{:S(2)}, u32[]{:S(2)}) collective-permute-start(bf16[128,512]{1,0:T(8,128)(2,1)S(1)} %collective-permute-done.refs_1_), channel_id=1, source_target_pairs={{0,1},{1,0},{2,3},{3,2},{4,5},{5,4},{6,7},{7,6},{8,9},{9,8},{10,11... | collective-permute-start | bytes 393224 | tf_op jit(solution)/shard_map/ppermute | solution.py:23
  20.0 2.7 %collective-permute-start.5 = (bf16[128,512]{1,0:T(8,128)(2,1)S(1)}, bf16[128,512]{1,0:T(8,128)(2,1)S(1)}, u32[]{:S(2)}, u32[]{:S(2)}) collective-permute-start(bf16[128,512]{1,0:T(8,128)(2,1)S(1)} %collective-permute-done.1.refs_2_), channel_id=1, source_target_pairs={{0,1},{1,0},{2,3},{3,2},{4,5},{5,4},{6,7},{7,6},{8,9},{9,8},{10,11... | collective-permute-start | bytes 393224 | tf_op jit(solution)/shard_map/ppermute | solution.py:23
  21.7 1.3 collective-permute-start.6
  24.0 17.9 %copy-start.3 = (bf16[128,512]{1,0:T(8,128)(2,1)}, bf16[128,512]{1,0:T(8,128)(2,1)S(1)}, u32[]{:S(2)}) copy-start(bf16[128,512]{1,0:T(8,128)(2,1)S(1)} %collective-permute-done.6.refs_7_) | copy-start | bytes 393220
  24.0 18.3 %copy-start.2 = (bf16[128,512]{1,0:T(8,128)(2,1)S(1)}, bf16[128,512]{1,0:T(8,128)(2,1)}, u32[]{:S(2)}) copy-start(bf16[128,512]{1,0:T(8,128)(2,1)} %node.1) | copy-start | bytes 393220
  24.8 8.4 %collective-permute-start.9 = (bf16[128,512]{1,0:T(8,128)(2,1)S(1)}, bf16[128,512]{1,0:T(8,128)(2,1)}, u32[]{:S(2)}, u32[]{:S(2)}) collective-permute-start(bf16[128,512]{1,0:T(8,128)(2,1)S(1)} %get-tuple-element.41), channel_id=1, source_target_pairs={{0,248},{8,0},{16,8},{24,16},{32,24},{40,32},{48,40},{56,48},{64,5... | collective-permute-start | bytes 393224 | tf_op jit(solution)/shard_map/ppermute | solution.py:28
  30.7 8.7 %collective-permute-start.7 = (bf16[128,512]{1,0:T(8,128)(2,1)S(1)}, bf16[128,512]{1,0:T(8,128)(2,1)}, u32[]{:S(2)}, u32[]{:S(2)}) collective-permute-start(bf16[128,512]{1,0:T(8,128)(2,1)S(1)} %get-tuple-element.40), channel_id=1, source_target_pairs={{0,8},{8,16},{16,24},{24,32},{32,40},{40,48},{48,56},{56,64},{64,7... | collective-permute-start | bytes 393224 | tf_op jit(solution)/shard_map/ppermute | solution.py:28
  33.2 8.9 %collective-permute-start.10 = (bf16[128,512]{1,0:T(8,128)(2,1)}, bf16[128,512]{1,0:T(8,128)(2,1)}, u32[]{:S(2)}, u32[]{:S(2)}) collective-permute-start(bf16[128,512]{1,0:T(8,128)(2,1)} %collective-permute-done.9.refs_10_), channel_id=1, source_target_pairs={{0,1},{1,0},{2,3},{3,2},{4,5},{5,4},{6,7},{7,6},{8,9},{9,8},{10,11... | collective-permute-start | bytes 393224 | tf_op jit(solution)/shard_map/ppermute | solution.py:23
  39.5 2.8 %collective-permute-start.8 = (bf16[128,512]{1,0:T(8,128)(2,1)}, bf16[128,512]{1,0:T(8,128)(2,1)}, u32[]{:S(2)}, u32[]{:S(2)}) collective-permute-start(bf16[128,512]{1,0:T(8,128)(2,1)} %collective-permute-done.7.refs_8_), channel_id=1, source_target_pairs={{0,1},{1,0},{2,3},{3,2},{4,5},{5,4},{6,7},{7,6},{8,9},{9,8},{10,11... | collective-permute-start | bytes 393224 | tf_op jit(solution)/shard_map/ppermute | solution.py:23
  43.2 1.2 copy-start.7
  44.4 1.0 copy-start.10
  45.5 31.8 %copy-start.5 = (bf16[1024,512]{1,0:T(8,128)(2,1)S(1)}, bf16[1024,512]{1,0:T(8,128)(2,1)}, u32[]{:S(2)}) copy-start(bf16[1024,512]{1,0:T(8,128)(2,1)} %w1.1) | copy-start | bytes 3145732
  45.5 31.8 %copy-start.9 = (bf16[512,512]{1,0:T(8,128)(2,1)S(1)}, bf16[512,512]{1,0:T(8,128)(2,1)}, u32[]{:S(2)}) copy-start(bf16[512,512]{1,0:T(8,128)(2,1)} %w2.1) | copy-start | bytes 1572868
  45.5 31.9 %copy-start.14 = (bf16[128,512]{1,0:T(8,128)(2,1)S(1)}, bf16[128,512]{1,0:T(8,128)(2,1)}, u32[]{:S(2)}) copy-start(bf16[128,512]{1,0:T(8,128)(2,1)} %grad.2) | copy-start | bytes 393220
  56.0 1.0 copy-start.19
  57.0 22.2 %copy-start.15 = (bf16[1024,512]{1,0:T(8,128)(2,1)}, bf16[1024,512]{1,0:T(8,128)(2,1)S(1)}, u32[]{:S(2)}) copy-start(bf16[1024,512]{1,0:T(8,128)(2,1)S(1)} %get-tuple-element.67.from_s) | copy-start | bytes 3145732
  57.0 22.2 %copy-start.17 = (bf16[1024,512]{1,0:T(8,128)(2,1)}, bf16[1024,512]{1,0:T(8,128)(2,1)S(1)}, u32[]{:S(2)}) copy-start(bf16[1024,512]{1,0:T(8,128)(2,1)S(1)} %get-tuple-element.68.from_r) | copy-start | bytes 3145732
  57.0 1.9 %collective-permute-start.11 = (bf16[512,512]{1,0:T(8,128)(2,1)S(1)}, bf16[512,512]{1,0:T(8,128)(2,1)S(1)}, u32[]{:S(2)}, u32[]{:S(2)}) collective-permute-start(bf16[512,512]{1,0:T(8,128)(2,1)S(1)} %get-tuple-element.46), channel_id=1, source_target_pairs={{0,1},{1,0},{2,3},{3,2},{4,5},{5,4},{6,7},{7,6},{8,9},{9,8},{10,11... | collective-permute-start | bytes 1572872 | tf_op jit(solution)/shard_map/ppermute | solution.py:23
  58.9 39.3 %copy-start.6 = (bf16[1024,512]{1,0:T(8,128)(2,1)S(1)}, bf16[1024,512]{1,0:T(8,128)(2,1)}, u32[]{:S(2)}) copy-start(bf16[1024,512]{1,0:T(8,128)(2,1)} %grad.3) | copy-start | bytes 3145732
  58.9 39.3 %copy-start.11 = (bf16[512,512]{1,0:T(8,128)(2,1)S(1)}, bf16[512,512]{1,0:T(8,128)(2,1)}, u32[]{:S(2)}) copy-start(bf16[512,512]{1,0:T(8,128)(2,1)} %refs_9_.1) | copy-start | bytes 1572868
  59.1 10.2 %collective-permute-start.12 = (bf16[128,512]{1,0:T(8,128)(2,1)S(1)}, bf16[128,512]{1,0:T(8,128)(2,1)S(1)}, u32[]{:S(2)}, u32[]{:S(2)}) collective-permute-start(bf16[128,512]{1,0:T(8,128)(2,1)S(1)} %get-tuple-element.48), channel_id=1, source_target_pairs={{0,2},{1,3},{2,4},{3,5},{4,6},{5,7},{6,0},{7,1},{8,10},{9,11},{10,... | collective-permute-start | bytes 393224 | tf_op jit(solution)/shard_map/ppermute | solution.py:18
  61.0 16.3 %collective-permute-start.13 = (bf16[128,512]{1,0:T(8,128)(2,1)S(1)}, bf16[128,512]{1,0:T(8,128)(2,1)S(1)}, u32[]{:S(2)}, u32[]{:S(2)}) collective-permute-start(bf16[128,512]{1,0:T(8,128)(2,1)S(1)} %get-tuple-element.49), channel_id=1, source_target_pairs={{0,4},{1,5},{2,6},{3,7},{4,0},{5,1},{6,2},{7,3},{8,12},{9,13},{10,... | collective-permute-start | bytes 393224 | tf_op jit(solution)/shard_map/ppermute | solution.py:18
  65.0 12.3 %collective-permute-start.14 = (bf16[128,512]{1,0:T(8,128)(2,1)S(1)}, bf16[128,512]{1,0:T(8,128)(2,1)S(1)}, u32[]{:S(2)}, u32[]{:S(2)}) collective-permute-start(bf16[128,512]{1,0:T(8,128)(2,1)S(1)} %get-tuple-element.50), channel_id=1, source_target_pairs={{0,6},{1,7},{2,0},{3,1},{4,2},{5,3},{6,4},{7,5},{8,14},{9,15},{10,... | collective-permute-start | bytes 393224 | tf_op jit(solution)/shard_map/ppermute | solution.py:18
  79.2 26.9 %collective-permute-start.30 = (bf16[512,768]{1,0:T(8,128)(2,1)S(1)}, bf16[512,768]{1,0:T(8,128)(2,1)S(1)}, u32[]{:S(2)}, u32[]{:S(2)}) collective-permute-start(bf16[512,768]{1,0:T(8,128)(2,1)S(1)} %get-tuple-element.73), channel_id=1, source_target_pairs={{0,1},{1,0},{2,3},{3,2},{4,5},{5,4},{6,7},{7,6},{8,9},{9,8},{10,11... | collective-permute-start | bytes 2359304 | tf_op jit(solution)/shard_map/ppermute | solution.py:23
  79.8 9.4 %collective-permute-start.15 = (bf16[128,512]{1,0:T(8,128)(2,1)S(1)}, bf16[128,512]{1,0:T(8,128)(2,1)S(1)}, u32[]{:S(2)}, u32[]{:S(2)}) collective-permute-start(bf16[128,512]{1,0:T(8,128)(2,1)S(1)} %get-tuple-element.51.refs_0_), channel_id=1, source_target_pairs={{0,6},{1,7},{2,0},{3,1},{4,2},{5,3},{6,4},{7,5},{8,14},{9,15},{10,... | collective-permute-start | bytes 393224 | tf_op jit(solution)/shard_map/ppermute | solution.py:18
  81.6 14.6 %collective-permute-start.16 = (bf16[128,512]{1,0:T(8,128)(2,1)S(1)}, bf16[128,512]{1,0:T(8,128)(2,1)S(1)}, u32[]{:S(2)}, u32[]{:S(2)}) collective-permute-start(bf16[128,512]{1,0:T(8,128)(2,1)S(1)} %get-tuple-element.51.refs_0_), channel_id=1, source_target_pairs={{0,4},{1,5},{2,6},{3,7},{4,0},{5,1},{6,2},{7,3},{8,12},{9,13},{10,... | collective-permute-start | bytes 393224 | tf_op jit(solution)/shard_map/ppermute | solution.py:18
  83.1 13.8 %collective-permute-start.17 = (bf16[128,512]{1,0:T(8,128)(2,1)S(1)}, bf16[128,512]{1,0:T(8,128)(2,1)S(1)}, u32[]{:S(2)}, u32[]{:S(2)}) collective-permute-start(bf16[128,512]{1,0:T(8,128)(2,1)S(1)} %get-tuple-element.51.refs_0_), channel_id=1, source_target_pairs={{0,2},{1,3},{2,4},{3,5},{4,6},{5,7},{6,0},{7,1},{8,10},{9,11},{10,... | collective-permute-start | bytes 393224 | tf_op jit(solution)/shard_map/ppermute | solution.py:18
  85.4 11.5 %collective-permute-start.18 = (bf16[128,512]{1,0:T(8,128)(2,1)S(1)}, bf16[128,512]{1,0:T(8,128)(2,1)S(1)}, u32[]{:S(2)}, u32[]{:S(2)}) collective-permute-start(bf16[128,512]{1,0:T(8,128)(2,1)S(1)} %get-tuple-element.51.refs_0_), channel_id=1, source_target_pairs={{0,1},{1,0},{2,3},{3,2},{4,5},{5,4},{6,7},{7,6},{8,9},{9,8},{10,11... | collective-permute-start | bytes 393224 | tf_op jit(solution)/shard_map/ppermute | solution.py:23
  89.2 7.7 %collective-permute-start.19 = (bf16[128,512]{1,0:T(8,128)(2,1)S(1)}, bf16[128,512]{1,0:T(8,128)(2,1)S(1)}, u32[]{:S(2)}, u32[]{:S(2)}) collective-permute-start(bf16[128,512]{1,0:T(8,128)(2,1)S(1)} %collective-permute-done.15.refs_1_), channel_id=1, source_target_pairs={{0,1},{1,0},{2,3},{3,2},{4,5},{5,4},{6,7},{7,6},{8,9},{9,8},{10,11... | collective-permute-start | bytes 393224 | tf_op jit(solution)/shard_map/ppermute | solution.py:23
  96.3 1.5 collective-permute-start.20
  96.8 1.3 collective-permute-start.21
  105.1 1.0 copy-start.26
  106.1 1.1 copy-start.12
  106.1 1.3 copy-start.21
  106.1 1.7 copy-start.24
  106.1 6.3 %copy-start.8 = (bf16[1024,512]{1,0:T(8,128)(2,1)S(1)}, bf16[1024,512]{1,0:T(8,128)(2,1)}, u32[]{:S(2)}) copy-start(bf16[1024,512]{1,0:T(8,128)(2,1)} %edge.3) | copy-start | bytes 3145732
  107.8 19.0 %all-to-all-start.1 = ((bf16[32,16,768]{2,1,0:T(8,128)(2,1)}), bf16[32,16,768]{2,1,0:T(8,128)(2,1)}, u32[]{:S(2)}, u32[]{:S(2)}) async-start(bf16[32,16,768]{2,1,0:T(8,128)(2,1)} %bitcast.29), calls=%async_computation.1 | async-start | bytes 1572864 | tf_op jit(solution)/shard_map/all_to_all | solution.py:264
  112.4 1.2 copy-start.16
  113.7 1.2 copy-start.18
  114.9 1.2 copy-start.20
  116.1 1.2 copy-start.22
  117.3 1.2 copy-start.25
  120.9 2.8 %collective-permute-start.29 = (bf16[512,1024]{1,0:T(8,128)(2,1)S(1)}, bf16[512,1024]{1,0:T(8,128)(2,1)S(1)}, u32[]{:S(2)}, u32[]{:S(2)}) collective-permute-start(bf16[512,1024]{1,0:T(8,128)(2,1)S(1)} %get-tuple-element.71), channel_id=1, source_target_pairs={{0,1},{1,0},{2,3},{3,2},{4,5},{5,4},{6,7},{7,6},{8,9},{9,8},{10,11... | collective-permute-start | bytes 3145736 | tf_op jit(solution)/shard_map/ppermute | solution.py:23
  125.1 8.2 %copy-start.13 = (bf16[256,512]{1,0:T(8,128)(2,1)S(1)}, bf16[256,512]{1,0:T(8,128)(2,1)}, u32[]{:S(2)}) copy-start(bf16[256,512]{1,0:T(8,128)(2,1)} %copy-done.12) | copy-start | bytes 786436
  126.8 30.8 %all-to-all-start = ((bf16[32,16,1024]{2,1,0:T(8,128)(2,1)}), bf16[32,16,1024]{2,1,0:T(8,128)(2,1)}, u32[]{:S(2)}, u32[]{:S(2)}) async-start(bf16[32,16,1024]{2,1,0:T(8,128)(2,1)} %bitcast.28), calls=%async_computation | async-start | bytes 2097152 | tf_op jit(solution)/shard_map/all_to_all | solution.py:264
  133.3 2.1 %collective-permute-start.22 = (bf16[256,512]{1,0:T(8,128)(2,1)S(1)}, bf16[256,512]{1,0:T(8,128)(2,1)S(1)}, u32[]{:S(2)}, u32[]{:S(2)}) collective-permute-start(bf16[256,512]{1,0:T(8,128)(2,1)S(1)} %copy-done.13), channel_id=1, source_target_pairs={{0,1},{1,0},{2,3},{3,2},{4,5},{5,4},{6,7},{7,6},{8,9},{9,8},{10,11... | collective-permute-start | bytes 786440 | tf_op jit(solution)/shard_map/ppermute | solution.py:23
  135.5 17.5 %collective-permute-start.23 = (bf16[128,512]{1,0:T(8,128)(2,1)S(1)}, bf16[128,512]{1,0:T(8,128)(2,1)S(1)}, u32[]{:S(2)}, u32[]{:S(2)}) collective-permute-start(bf16[128,512]{1,0:T(8,128)(2,1)S(1)} %get-tuple-element.56), channel_id=1, source_target_pairs={{0,8},{8,16},{16,24},{24,32},{32,40},{40,48},{48,56},{56,64},{64,7... | collective-permute-start | bytes 393224 | tf_op jit(solution)/shard_map/ppermute | solution.py:28
  137.0 16.0 %collective-permute-start.24 = (bf16[128,512]{1,0:T(8,128)(2,1)S(1)}, bf16[128,512]{1,0:T(8,128)(2,1)S(1)}, u32[]{:S(2)}, u32[]{:S(2)}) collective-permute-start(bf16[128,512]{1,0:T(8,128)(2,1)S(1)} %get-tuple-element.57), channel_id=1, source_target_pairs={{0,248},{8,0},{16,8},{24,16},{32,24},{40,32},{48,40},{56,48},{64,5... | collective-permute-start | bytes 393224 | tf_op jit(solution)/shard_map/ppermute | solution.py:28
  141.4 1.2 copy-start.23
  142.7 1.2 copy-start.27
  153.7 12.5 %collective-permute-start.25 = (bf16[512,512]{1,0:T(8,128)(2,1)S(1)}, bf16[512,512]{1,0:T(8,128)(2,1)S(1)}, u32[]{:S(2)}, u32[]{:S(2)}) collective-permute-start(bf16[512,512]{1,0:T(8,128)(2,1)S(1)} %get-tuple-element.59), channel_id=1, source_target_pairs={{0,1},{1,0},{2,3},{3,2},{4,5},{5,4},{6,7},{7,6},{8,9},{9,8},{10,11... | collective-permute-start | bytes 1572872 | tf_op jit(solution)/shard_map/ppermute | solution.py:23
  159.1 9.4 %collective-permute-start.31 = (bf16[16,1792]{1,0:T(8,128)(2,1)S(1)}, bf16[16,1792]{1,0:T(8,128)(2,1)S(1)}, u32[]{:S(2)}, u32[]{:S(2)}) collective-permute-start(bf16[16,1792]{1,0:T(8,128)(2,1)S(1)} %fusion), channel_id=1, source_target_pairs={{0,2},{1,3},{2,4},{3,5},{4,6},{5,7},{6,0},{7,1},{8,10},{9,11},{10,... | collective-permute-start | bytes 172040 | tf_op jit(solution)/shard_map/ppermute | solution.py:18
  159.6 12.3 %collective-permute-start.32 = (bf16[16,1792]{1,0:T(8,128)(2,1)S(1)}, bf16[16,1792]{1,0:T(8,128)(2,1)S(1)}, u32[]{:S(2)}, u32[]{:S(2)}) collective-permute-start(bf16[16,1792]{1,0:T(8,128)(2,1)S(1)} %fusion), channel_id=1, source_target_pairs={{0,4},{1,5},{2,6},{3,7},{4,0},{5,1},{6,2},{7,3},{8,12},{9,13},{10,... | collective-permute-start | bytes 172040 | tf_op jit(solution)/shard_map/ppermute | solution.py:18
  164.0 7.9 %collective-permute-start.33 = (bf16[16,1792]{1,0:T(8,128)(2,1)S(1)}, bf16[16,1792]{1,0:T(8,128)(2,1)S(1)}, u32[]{:S(2)}, u32[]{:S(2)}) collective-permute-start(bf16[16,1792]{1,0:T(8,128)(2,1)S(1)} %fusion), channel_id=1, source_target_pairs={{0,6},{1,7},{2,0},{3,1},{4,2},{5,3},{6,4},{7,5},{8,14},{9,15},{10,... | collective-permute-start | bytes 172040 | tf_op jit(solution)/shard_map/ppermute | solution.py:18
  166.3 9.3 %collective-permute-start.26 = (bf16[128,512]{1,0:T(8,128)(2,1)S(1)}, bf16[128,512]{1,0:T(8,128)(2,1)S(1)}, u32[]{:S(2)}, u32[]{:S(2)}) collective-permute-start(bf16[128,512]{1,0:T(8,128)(2,1)S(1)} %get-tuple-element.61), channel_id=1, source_target_pairs={{0,2},{1,3},{2,4},{3,5},{4,6},{5,7},{6,0},{7,1},{8,10},{9,11},{10,... | collective-permute-start | bytes 393224 | tf_op jit(solution)/shard_map/ppermute | solution.py:18
  166.5 14.6 %collective-permute-start.27 = (bf16[128,512]{1,0:T(8,128)(2,1)S(1)}, bf16[128,512]{1,0:T(8,128)(2,1)S(1)}, u32[]{:S(2)}, u32[]{:S(2)}) collective-permute-start(bf16[128,512]{1,0:T(8,128)(2,1)S(1)} %get-tuple-element.62), channel_id=1, source_target_pairs={{0,4},{1,5},{2,6},{3,7},{4,0},{5,1},{6,2},{7,3},{8,12},{9,13},{10,... | collective-permute-start | bytes 393224 | tf_op jit(solution)/shard_map/ppermute | solution.py:18
  168.5 14.3 %collective-permute-start.28 = (bf16[128,512]{1,0:T(8,128)(2,1)S(1)}, bf16[128,512]{1,0:T(8,128)(2,1)S(1)}, u32[]{:S(2)}, u32[]{:S(2)}) collective-permute-start(bf16[128,512]{1,0:T(8,128)(2,1)S(1)} %get-tuple-element.63), channel_id=1, source_target_pairs={{0,6},{1,7},{2,0},{3,1},{4,2},{5,3},{6,4},{7,5},{8,14},{9,15},{10,... | collective-permute-start | bytes 393224 | tf_op jit(solution)/shard_map/ppermute | solution.py:18
  171.9 11.5 %collective-permute-start.34 = (bf16[16,1792]{1,0:T(8,128)(2,1)S(1)}, bf16[16,1792]{1,0:T(8,128)(2,1)S(1)}, u32[]{:S(2)}, u32[]{:S(2)}) collective-permute-start(bf16[16,1792]{1,0:T(8,128)(2,1)S(1)} %get-tuple-element.74), channel_id=1, source_target_pairs={{0,1},{1,0},{2,3},{3,2},{4,5},{5,4},{6,7},{7,6},{8,9},{9,8},{10,11... | collective-permute-start | bytes 172040 | tf_op jit(solution)/shard_map/ppermute | solution.py:23
  183.6 1.9 %copy-start.28 = (f32[16,1536]{1,0:T(8,128)}, f32[16,1536]{1,0:T(8,128)S(1)}, u32[]{:S(2)}) copy-start(f32[16,1536]{1,0:T(8,128)S(1)} %get-tuple-element.87) | copy-start | bytes 294916
  (2 other events, 1.8 us)

commit v2 on v1

v2 whole, which is shorter than its diff:
```python
import jax
import jax.numpy as jnp
from jax import lax
from jax.experimental import pallas as pl
from jax.experimental.pallas import tpu as pltpu
from jax.sharding import PartitionSpec as P


epsilon = 1e-05
F32 = jnp.float32
BF16 = jnp.bfloat16
MIB = 1 << 20


def over_ring(x, by):
    count = lax.axis_size("shard")
    return lax.ppermute(x, "shard", [(i, (i + 2 * by) % count) for i in range(count)])


def to_partner(x):
    count = lax.axis_size("shard")
    return lax.ppermute(x, "shard", [(i, i ^ 1) for i in range(count)])


def to_patch(x, by):
    count = lax.axis_size("patch")
    return lax.ppermute(x, "patch", [(i, (i + by) % count) for i in range(count)])


def spread_over_shard(own):
    across = over_ring(own, 2)
    after = over_ring(own, -1)
    before = over_ring(own, 1)
    mine = [own, after, across, before]
    return mine + [to_partner(b) for b in mine]


def ring_sum_parts(chunks):
    return [over_ring(chunks[0], 1), over_ring(chunks[1], 2), over_ring(chunks[2], -1)]


def dot(a, b):
    return jnp.dot(a, b, preferred_element_type=F32)


def dot_nt(a, b):
    return lax.dot_general(a, b, (((1,), (1,)), ((), ())), preferred_element_type=F32)


def dot_tn(a, b):
    return lax.dot_general(a, b, (((0,), (0,)), ((), ())), preferred_element_type=F32)


def pick_rows(index_column, count, first=0):
    places = lax.broadcasted_iota(jnp.int32, (index_column.shape[0], count), 1) + first
    return jnp.where(places == index_column, 1.0, 0.0).astype(BF16)


def add_rows(index_row, count, first=0):
    places = lax.broadcasted_iota(jnp.int32, (count, index_row.shape[1]), 0) + first
    return jnp.where(places == index_row, 1.0, 0.0).astype(BF16)


def normalised(out):
    center = out - jnp.mean(out, axis=-1, keepdims=True)
    inv = lax.rsqrt(jnp.mean(center * center, axis=-1, keepdims=True) + epsilon)
    return center * inv, inv


def norm_backward(g, normed, inv):
    d = inv * (
        g
        - jnp.mean(g, axis=-1, keepdims=True)
        - normed * jnp.mean(g * normed, axis=-1, keepdims=True)
    )
    return d.astype(BF16)


def call(
    kernel, out_shapes, args, *, far=(), words=(), far_out=(), scratch=(), flops=0, moved=0, vmem=16 * MIB
):
    full = pl.BlockSpec(memory_space=pltpu.VMEM)
    hbm = pl.BlockSpec(memory_space=pltpu.HBM)
    smem = pl.BlockSpec(memory_space=pltpu.SMEM)
    in_specs = [hbm if i in far else smem if i in words else full for i in range(len(args))]
    out_specs = [hbm if i in far_out else full for i in range(len(out_shapes))]
    out_shapes = [
        pltpu.HBM(o.shape, o.dtype) if i in far_out else o for i, o in enumerate(out_shapes)
    ]
    args = [
        pltpu.with_memory_space_constraint(a, pltpu.HBM) if i in far else a
        for i, a in enumerate(args)
    ]
    return pl.pallas_call(
        kernel,
        out_shape=out_shapes,
        in_specs=in_specs,
        out_specs=out_specs,
        scratch_shapes=list(scratch),
        compiler_params=pltpu.CompilerParams(vmem_limit_bytes=vmem),
        cost_estimate=pl.CostEstimate(flops=flops, bytes_accessed=moved, transcendentals=0),
    )(*args)


def shape(dims, dtype):
    return jax.ShapeDtypeStruct(dims, dtype)


def begin(src, dst, sem):
    copy = pltpu.make_async_copy(src, dst, sem)
    copy.start()
    return copy


def halo_rows_kernel(index, own, *refs):
    blocks, (low, high, held, sem) = refs[:7], refs[7:]
    arriving = begin(own, held, sem.at[0])
    total = None
    for k, block in enumerate(blocks):
        part = dot(pick_rows(index[...], 128, 128 * (k + 1)), block[...])
        total = part if total is None else total + part
    arriving.wait()
    total = total + dot(pick_rows(index[...], 128), held[...])
    low[...] = total[:128].astype(BF16)
    high[...] = total[128:].astype(BF16)


TILE = 256
TILES = 4


def tiles(body):
    lax.fori_loop(
        0, TILES, lambda i, _: (body(i, pl.ds(pl.multiple_of(i * TILE, TILE), TILE)), 0)[1], 0
    )


def edge_start_kernel(s_col, r_col, edge_h, own_h, *refs):
    blocks = refs[:7]
    (w1_h, from_s, from_r_h, pre_o, table, edge, w1, from_r, sem) = refs[7:]
    got_own = begin(own_h, table.at[pl.ds(0, 128), :], sem.at[0])
    got_w1 = begin(w1_h, w1, sem.at[1])
    got_edge = begin(edge_h, edge, sem.at[2])
    for k, block in enumerate(blocks):
        table[pl.ds(128 * (k + 1), 128), :] = block[...]
    got_own.wait()

    def gather(i, rows):
        from_s[rows, :] = dot(pick_rows(s_col[rows, :], 1024), table[...]).astype(BF16)
        from_r[rows, :] = dot(pick_rows(r_col[rows, :], 1024), table[...]).astype(BF16)
        begin(from_r.at[rows, :], from_r_h.at[rows, :], sem.at[3 + i])

    tiles(gather)
    got_w1.wait()
    got_edge.wait()

    def multiply(i, rows):
        pre_o[rows, :] = (
            dot(edge[rows, :], w1[pl.ds(0, 512), :])
            + dot(from_s[rows, :], w1[pl.ds(512, 512), :])
            + dot(from_r[rows, :], w1[pl.ds(1024, 512), :])
        )

    tiles(multiply)

    def finish(i, rows):
        pltpu.make_async_copy(from_r.at[rows, :], from_r_h.at[rows, :], sem.at[3 + i]).wait()

    tiles(finish)


def edge_forward_kernel(s_col, r_row, edge_h, from_s, pre_i, *refs):
    blocks = refs[:4]
    (w1_h, w2_h, from_s_h, act_h, slope_h, normed_h, inv_h, keep_o, send_o) = refs[4:13]
    (table, news, edge, w1, w2, from_s_o, act_o, slope_o, normed_o, inv_o, sem, out_sem) = refs[13:]
    got_w1 = begin(w1_h.at[pl.ds(512, 512), :], w1, sem.at[0])
    got_w2 = begin(w2_h, w2, sem.at[1])
    got_edge = begin(edge_h, edge, sem.at[2])
    for k, block in enumerate(blocks):
        table[pl.ds(128 * k, 128), :] = block[...]
    got_w1.wait()
    got_w2.wait()
    got_edge.wait()
    leaving = (
        (from_s_o, from_s_h),
        (act_o, act_h),
        (slope_o, slope_h),
        (normed_o, normed_h),
        (inv_o, inv_h),
    )

    def tile(i, rows):
        halo = dot(pick_rows(s_col[rows, :], 512, 1024), table[...]).astype(BF16)
        from_s_o[rows, :] = from_s[rows, :] + halo
        pre = pre_i[rows, :] + dot(halo, w1[...])
        sig = jax.nn.sigmoid(pre)
        act = (pre * sig).astype(BF16)
        act_o[rows, :] = act
        slope_o[rows, :] = sig * (1.0 + pre * (1.0 - sig))
        normed, inv = normalised(dot(act, w2[...]))
        normed_o[rows, :] = normed
        inv_o[rows, :] = inv
        news[rows, :] = (edge[rows, :].astype(F32) + normed).astype(BF16)
        for k, (here, there) in enumerate(leaving):
            begin(here.at[rows, :], there.at[rows, :], out_sem.at[k, i])

    tiles(tile)
    for k in (2, 3, 0, 1):
        sums = dot(add_rows(r_row[...], 256, 256 * k), news[...])
        if k < 2:
            keep_o[pl.ds(256 * k, 256), :] = sums
        else:
            send_o[pl.ds(256 * (k - 2), 256), :] = sums.astype(BF16)

    def finish(i, rows):
        for k, (here, there) in enumerate(leaving):
            pltpu.make_async_copy(here.at[rows, :], there.at[rows, :], out_sem.at[k, i]).wait()

    tiles(finish)


def pair_sum_kernel(keep, came, own, one, two, three):
    both = keep[...] + came[...].astype(F32)
    own[...] = both[0:128]
    one[...] = both[128:256].astype(BF16)
    two[...] = both[256:384].astype(BF16)
    three[...] = both[384:512].astype(BF16)


def node_kernel(core, own, got1, got2, got3, node, grad, w1, w2, d_agg_o, part_o, keep_o, send_o, agg_s, act_s):
    agg = (
        own[...] + got1[...].astype(F32) + got2[...].astype(F32) + got3[...].astype(F32)
    ).astype(BF16)
    x = node[...]
    pre = dot(x, w1[pl.ds(0, 512), :]) + dot(agg, w1[pl.ds(512, 512), :])
    sig = jax.nn.sigmoid(pre)
    act = (pre * sig).astype(BF16)
    normed, inv = normalised(dot(act, w2[...]))
    g = grad[...].astype(F32)
    d_out = norm_backward(g, normed, inv)
    d_act = dot_nt(d_out, w2[...])
    d_pre = (d_act * (sig * (1.0 + pre * (1.0 - sig)))).astype(BF16)
    d_agg_o[...] = dot_nt(d_pre, w1[pl.ds(512, 512), :]).astype(BF16)
    part_o[...] = g + dot_nt(d_pre, w1[pl.ds(0, 512), :])
    agg_s[...] = agg
    act_s[...] = act
    mine = pl.multiple_of(core[0] * 256, 256)
    theirs = pl.multiple_of(256 - core[0] * 256, 256)
    for k, (left, right) in enumerate(((d_pre, node), (d_pre, agg_s), (d_out, act_s))):
        keep_o[:, pl.ds(256 * k, 256)] = dot_tn(left, right[:, pl.ds(mine, 256)])
        send_o[:, pl.ds(256 * k, 256)] = dot_tn(left, right[:, pl.ds(theirs, 256)]).astype(BF16)


def edge_backward_kernel(core, r_col, s_row, grad_h, normed_h, inv_h, slope_h, edge_h, from_s_h, from_r_h, act_h, *refs):
    blocks = refs[:8]
    (w1_h, w2_h, d_pre_h, dxs_h, grad_o_h, back_keep, back_send, keep_o, send_o) = refs[8:17]
    (table, d_outs, d_pres, dxss, grad_o, grad, normed, inv, slope) = refs[17:26]
    (edge, from_s, from_r, act, w1, w2, tile_sem, sem, out_sem) = refs[26:]
    streams = ((grad_h, grad), (normed_h, normed), (inv_h, inv), (slope_h, slope))
    leaving = ((d_pres, d_pre_h), (dxss, dxs_h), (grad_o, grad_o_h))
    got_w2 = begin(w2_h, w2, sem.at[0])
    got_w1 = begin(w1_h.at[pl.ds(0, 1024), :], w1, sem.at[1])

    def ask(i, rows):
        for k, (there, here) in enumerate(streams):
            begin(there.at[rows, :], here.at[rows, :], tile_sem.at[k, i])

    tiles(ask)
    late = [
        begin(there, here, sem.at[2 + k])
        for k, (there, here) in enumerate(
            ((edge_h, edge), (from_s_h, from_s), (from_r_h, from_r), (act_h, act))
        )
    ]
    for k, block in enumerate(blocks):
        table[pl.ds(128 * k, 128), :] = block[...]
    got_w2.wait()
    got_w1.wait()

    def tile(i, rows):
        for k, (there, here) in enumerate(streams):
            pltpu.make_async_copy(there.at[rows, :], here.at[rows, :], tile_sem.at[k, i]).wait()
        g = grad[rows, :].astype(F32) + dot(pick_rows(r_col[rows, :], 1024), table[...])
        d_out = norm_backward(g, normed[rows, :], inv[rows, :])
        d_outs[rows, :] = d_out
        d_pre = (dot_nt(d_out, w2[...]) * slope[rows, :]).astype(BF16)
        d_pres[rows, :] = d_pre
        dxss[rows, :] = dot_nt(d_pre, w1[pl.ds(512, 512), :]).astype(BF16)
        grad_o[rows, :] = (g + dot_nt(d_pre, w1[pl.ds(0, 512), :])).astype(BF16)
        for k, (here, there) in enumerate(leaving):
            begin(here.at[rows, :], there.at[rows, :], out_sem.at[k, i])

    tiles(tile)
    for k in range(4):
        sums = dot(add_rows(s_row[...], 128, 1024 + 128 * k), dxss[...])
        to = pl.ds(128 * (k // 2), 128)
        if k % 2 == 0:
            back_keep[to, :] = sums
        else:
            back_send[to, :] = sums.astype(BF16)
    mine = pl.multiple_of(core[0] * 256, 256)
    theirs = pl.multiple_of(256 - core[0] * 256, 256)
    for copy in late:
        copy.wait()
    for k, (left, right) in enumerate(
        ((d_pres, edge), (d_pres, from_s), (d_pres, from_r), (d_outs, act))
    ):
        keep_o[:, pl.ds(256 * k, 256)] = dot_tn(left[...], right[:, pl.ds(mine, 256)])
        send_o[:, pl.ds(256 * k, 256)] = dot_tn(
            left[...], right[:, pl.ds(theirs, 256)]
        ).astype(BF16)

    def finish(i, rows):
        for k, (here, there) in enumerate(leaving):
            pltpu.make_async_copy(here.at[rows, :], there.at[rows, :], out_sem.at[k, i]).wait()

    tiles(finish)


def add_kernel(keep, came, out):
    out[...] = (keep[...] + came[...].astype(F32)).astype(BF16)


def node_sums_kernel(s_row, r_row, d_pre_h, dxs_h, w1_h, out, dxr, d_pre, dxs, w_r, sem):
    got_w = begin(w1_h.at[pl.ds(1024, 512), :], w_r, sem.at[0])
    got_d = begin(d_pre_h, d_pre, sem.at[1])
    got_x = begin(dxs_h, dxs, sem.at[2])
    got_w.wait()
    got_d.wait()
    dxr[...] = dot_nt(d_pre[...], w_r[...]).astype(BF16)
    got_x.wait()
    for k in range(4):
        out[pl.ds(256 * k, 256), :] = dot(add_rows(s_row[...], 256, 256 * k), dxs[...]) + dot(
            add_rows(r_row[...], 256, 256 * k), dxr[...]
        )


def blocks_total_kernel(edge, node_h, sum_o, send_o, node, sem):
    got_n = begin(node_h, node, sem.at[0])
    edge_part = jnp.sum(edge[...].astype(F32), axis=0)
    sum_o[:, pl.ds(0, 1024)] = edge_part
    send_o[:, pl.ds(0, 1024)] = edge_part.astype(BF16)
    got_n.wait()
    node_part = jnp.sum(node[...].astype(F32), axis=0)
    sum_o[:, pl.ds(1024, 768)] = node_part
    send_o[:, pl.ds(1024, 768)] = node_part.astype(BF16)


def ring_total_kernel(own, got1, got2, got3, sum_o, send_o):
    total = own[...] + got1[...].astype(F32) + got2[...].astype(F32) + got3[...].astype(F32)
    sum_o[...] = total
    send_o[...] = total.astype(BF16)


def both_halves_kernel(core, mine, theirs, *outs):
    here = pl.multiple_of(core[0] * 256, 256)
    there = pl.multiple_of(256 - core[0] * 256, 256)
    k = 0
    for out in outs:
        for j in range(out.shape[1] // 512):
            out[:, pl.ds(512 * j + here, 256)] = mine[:, pl.ds(256 * k, 256)]
            out[:, pl.ds(512 * j + there, 256)] = theirs[:, pl.ds(256 * k, 256)].astype(F32)
            k += 1


def pair_add_kernel(keep, came, low, high):
    both = keep[...] + came[...].astype(F32)
    low[...] = both[:128].astype(BF16)
    high[...] = both[128:].astype(BF16)


def returned_kernel(index, sums, low, high, keep_o, send_o):
    for k in range(4):
        rows = (
            sums[pl.ds(256 * k, 256), :]
            + dot(add_rows(index[:, pl.ds(0, 128)], 256, 256 * k), low[...])
            + dot(add_rows(index[:, pl.ds(128, 128)], 256, 256 * k), high[...])
        )
        if k < 2:
            keep_o[pl.ds(256 * k, 256), :] = rows
        else:
            send_o[pl.ds(256 * (k - 2), 256), :] = rows.astype(BF16)


def node_total_kernel(own, got1, got2, got3, part, out):
    out[...] = (
        own[...]
        + got1[...].astype(F32)
        + got2[...].astype(F32)
        + got3[...].astype(F32)
        + part[...]
    ).astype(BF16)


def weight_sum(keep, came):
    patches = lax.axis_size("patch")
    units, lanes = keep.shape
    (both,) = call(add_kernel, [shape((units, lanes), BF16)], [keep, came], moved=4 * MIB, vmem=8 * MIB)
    return lax.all_to_all(both.reshape(patches, units // patches, lanes), "patch", 0, 0, tiled=True)


def body(
    node_latent,
    edge_latent,
    senders,
    receivers,
    halo_list,
    w_edge_first,
    w_edge_second,
    w_node_first,
    w_node_second,
    grad_node_new,
    grad_edge_new,
):
    place = lax.axis_index("shard")
    core = place & 1
    chip = place >> 1

    table_blocks = spread_over_shard(node_latent)

    def relative(n):
        return (((n >> 7) & 1) ^ core) * 512 + (((n >> 8) - chip) & 3) * 128 + (n & 127)

    s_index = jnp.where(
        senders < 256,
        1024 + ((senders >> 7) ^ core) * 128 + (senders & 127),
        jnp.where(
            senders >= 1280,
            1280 + (((senders - 1280) >> 7) ^ core) * 128 + (senders & 127),
            relative(senders - 256),
        ),
    )
    r_index = relative(receivers)
    listed = relative(halo_list[0])
    half = jnp.concatenate(
        [
            lax.dynamic_slice(listed, (core * 128,), (128,)),
            lax.dynamic_slice(listed, (256 + core * 128,), (128,)),
        ]
    )
    s_col, s_row = s_index.reshape(1024, 1), s_index.reshape(1, 1024)
    r_col, r_row = r_index.reshape(1024, 1), r_index.reshape(1, 1024)
    core_word = core.reshape(1).astype(jnp.int32)

    to_prev, to_next = call(
        halo_rows_kernel,
        [shape((128, 512), BF16)] * 2,
        [half.reshape(256, 1)] + table_blocks,
        far=(1,),
        scratch=[pltpu.VMEM((128, 512), BF16), pltpu.SemaphoreType.DMA((1,))],
        flops=2 * 256 * 1024 * 512,
        moved=2 * MIB,
        vmem=8 * MIB,
    )
    prev_mine = to_patch(to_next, 1)
    next_mine = to_patch(to_prev, -1)
    halo_blocks = [prev_mine, to_partner(prev_mine), next_mine, to_partner(next_mine)]
    from_s, from_r, pre = call(
        edge_start_kernel,
        [shape((1024, 512), BF16)] * 2 + [shape((1024, 512), F32)],
        [s_col, r_col, edge_latent] + table_blocks + [w_edge_first],
        far=(2, 3, 11),
        far_out=(1,),
        scratch=[
            pltpu.VMEM((1024, 512), BF16),
            pltpu.VMEM((1024, 512), BF16),
            pltpu.VMEM((1536, 512), BF16),
            pltpu.VMEM((1024, 512), BF16),
            pltpu.SemaphoreType.DMA((7,)),
        ],
        flops=3_800_000_000,
        moved=8 * MIB,
    )
    from_s, act, slope, normed, inv, agg_keep, agg_send = call(
        edge_forward_kernel,
        [
            shape((1024, 512), BF16),
            shape((1024, 512), BF16),
            shape((1024, 512), F32),
            shape((1024, 512), F32),
            shape((1024, 1), F32),
            shape((512, 512), F32),
            shape((512, 512), BF16),
        ],
        [s_col, r_row, edge_latent, from_s, pre] + halo_blocks + [w_edge_first, w_edge_second],
        far=(2, 9, 10),
        far_out=(0, 1, 2, 3, 4),
        scratch=[
            pltpu.VMEM((512, 512), BF16),
            pltpu.VMEM((1024, 512), BF16),
            pltpu.VMEM((1024, 512), BF16),
            pltpu.VMEM((512, 512), BF16),
            pltpu.VMEM((512, 512), BF16),
            pltpu.VMEM((1024, 512), BF16),
            pltpu.VMEM((1024, 512), BF16),
            pltpu.VMEM((1024, 512), F32),
            pltpu.VMEM((1024, 512), F32),
            pltpu.VMEM((1024, 1), F32),
            pltpu.SemaphoreType.DMA((3,)),
            pltpu.SemaphoreType.DMA((5, TILES)),
        ],
        flops=2_700_000_000,
        moved=12 * MIB,
        vmem=20 * MIB,
    )
    agg_came = to_partner(agg_send)
    agg_own, agg_1, agg_2, agg_3 = call(
        pair_sum_kernel,
        [shape((128, 512), F32)] + [shape((128, 512), BF16)] * 3,
        [agg_keep, agg_came],
        moved=2 * MIB,
        vmem=8 * MIB,
    )
    d_agg, node_part, n_keep, n_send = call(
        node_kernel,
        [
            shape((128, 512), BF16),
            shape((128, 512), F32),
            shape((512, 768), F32),
            shape((512, 768), BF16),
        ],
        [core_word, agg_own]
        + ring_sum_parts([agg_1, agg_2, agg_3])
        + [node_latent, grad_node_new, w_node_first, w_node_second],
        words=(0,),
        scratch=[pltpu.VMEM((128, 512), BF16), pltpu.VMEM((128, 512), BF16)],
        flops=800_000_000,
        moved=5 * MIB,
        vmem=8 * MIB,
    )
    d_blocks = spread_over_shard(d_agg)
    node_blocks = weight_sum(n_keep, to_partner(n_send))

    d_pre, dxs, grad_edge_latent, back_keep, back_send, w_keep, w_send = call(
        edge_backward_kernel,
        [
            shape((1024, 512), BF16),
            shape((1024, 512), BF16),
            shape((1024, 512), BF16),
            shape((256, 512), F32),
            shape((256, 512), BF16),
            shape((512, 1024), F32),
            shape((512, 1024), BF16),
        ],
        [core_word, r_col, s_row, grad_edge_new, normed, inv, slope, edge_latent, from_s, from_r, act]
        + d_blocks
        + [w_edge_first, w_edge_second],
        words=(0,),
        far=(3, 4, 5, 6, 7, 8, 9, 10, 19, 20),
        far_out=(0, 1, 2),
        scratch=[pltpu.VMEM((1024, 512), BF16)] * 6
        + [
            pltpu.VMEM((1024, 512), F32),
            pltpu.VMEM((1024, 1), F32),
            pltpu.VMEM((1024, 512), F32),
        ]
        + [pltpu.VMEM((1024, 512), BF16)] * 5
        + [
            pltpu.VMEM((512, 512), BF16),
            pltpu.SemaphoreType.DMA((4, TILES)),
            pltpu.SemaphoreType.DMA((6,)),
            pltpu.SemaphoreType.DMA((3, TILES)),
        ],
        flops=5_500_000_000,
        moved=16 * MIB,
        vmem=28 * MIB,
    )
    back_prev, back_next = call(
        pair_add_kernel,
        [shape((128, 512), BF16)] * 2,
        [back_keep, to_partner(back_send)],
        moved=MIB,
        vmem=8 * MIB,
    )
    got_next = to_patch(back_prev, -1)
    got_prev = to_patch(back_next, 1)
    edge_blocks = weight_sum(w_keep, to_partner(w_send))
    (sums,) = call(
        node_sums_kernel,
        [shape((1024, 512), F32)],
        [s_row, r_row, d_pre, dxs, w_edge_first],
        far=(2, 3, 4),
        scratch=[pltpu.VMEM((1024, 512), BF16)] * 3
        + [pltpu.VMEM((512, 512), BF16), pltpu.SemaphoreType.DMA((3,))],
        flops=2_700_000_000,
        moved=5 * MIB,
    )
    node_keep, node_send = call(
        returned_kernel,
        [shape((512, 512), F32), shape((512, 512), BF16)],
        [half.reshape(1, 256), sums, got_prev, got_next],
        flops=300_000_000,
        moved=4 * MIB,
        vmem=8 * MIB,
    )
    t_own, t_1, t_2, t_3 = call(
        pair_sum_kernel,
        [shape((128, 512), F32)] + [shape((128, 512), BF16)] * 3,
        [node_keep, to_partner(node_send)],
        moved=2 * MIB,
        vmem=8 * MIB,
    )
    (grad_node_latent,) = call(
        node_total_kernel,
        [shape((128, 512), BF16)],
        [t_own] + ring_sum_parts([t_1, t_2, t_3]) + [node_part],
        moved=MIB,
        vmem=8 * MIB,
    )

    w_rows, w_out = call(
        blocks_total_kernel,
        [shape((16, 1792), F32), shape((16, 1792), BF16)],
        [edge_blocks, node_blocks],
        far=(1,),
        scratch=[pltpu.VMEM((32, 16, 768), BF16), pltpu.SemaphoreType.DMA((1,))],
        moved=2 * MIB,
        vmem=8 * MIB,
    )
    w_rows, w_out = call(
        ring_total_kernel,
        [shape((16, 1792), F32), shape((16, 1792), BF16)],
        [w_rows] + ring_sum_parts([w_out] * 3),
        moved=MIB,
        vmem=4 * MIB,
    )
    rows = call(
        both_halves_kernel,
        [shape((16, lanes), F32) for lanes in (1536, 512, 1024, 512)],
        [core_word, w_rows, to_partner(w_out)],
        words=(0,),
        moved=MIB,
        vmem=4 * MIB,
    )
    return (grad_node_latent, grad_edge_latent) + tuple(r.T for r in rows)


def solution(mesh):
    split = P(("patch", "shard"), None)
    ids = P(("patch", "shard"))
    in_specs = (split, split, ids, ids, P("patch", None), P(), P(), P(), P(), split, split)
    out_specs = (split, split) + (P(None, "patch"),) * 4

    return jax.shard_map(body, mesh=mesh, in_specs=in_specs, out_specs=out_specs, check_vma=False)
```

time: 186 us -> 172 us (0.925)
  local copies, waits for them, and re-layouts: 15.9 us -> 0.61 us
  Pallas kernels: 27 us -> 37.7 us
  other arithmetic: 8.5 us -> 1.41 us
    unnamed x62 -> x8, local copies, waits for them, and re-layouts: 15.2 us -> 0.03 us
    pallas_call x11 -> x16, Pallas kernels: 27 us -> 37.7 us  [call(): pl.pallas_call(kernel, out_shape=out_shapes, in_specs=in_specs, out_specs...]
    reduce_sum x2 -> x0, other arithmetic: 2.64 us -> none  [weight_sum(): return jnp.sum(blocks.astype(F32), axis=0)]
    convert_element_type x4 -> x0, other arithmetic: 2.54 us -> none  [the longest x2 2.5 us: weight_sum(): both = (keep + came.astype(F32)).astype(BF16)]
    transpose x3 -> x0, other arithmetic: 1.89 us -> none  [joined(): return jnp.concatenate(parts, axis=1).T]
  transfers between devices with their start and end apart: 37 -> 37, of which waited for: 19 -> 16; matrix products, arithmetic and copies ran while one was open for 3% -> 1% of each run, Pallas kernels for 7% -> 15%
where the time goes in v2:
time: 172 us; the launch traced here: 171 us
  starting transfers between devices  81.8 us (48%)
  waiting for transfers between devices  48.7 us (28%)
  Pallas kernels  37.7 us (22%)
    pallas_call x16, Pallas kernels, call(): pl.pallas_call(kernel, out_shape=out_shapes, in_specs=in_specs, out_specs...  37.7 us
    ppermute x15, starting transfers between devices, over_ring(): lax.ppermute(x, 'shard', [(i, (i + 2 * by) % count) for i in range(count)])  36 us
    ppermute x15, waiting for transfers between devices, over_ring(): lax.ppermute(x, 'shard', [(i, (i + 2 * by) % count) for i in range(count)])  29.1 us
    ppermute x16, starting transfers between devices, to_partner(): return lax.ppermute(x, 'shard', [(i, i ^ 1) for i in range(count)])  21.5 us
    ppermute x4, waiting for transfers between devices, to_patch(): lax.ppermute(x, 'patch', [(i, (i + by) % count) for i in range(count)])  12.8 us
    all_to_all x2, starting transfers between devices, weight_sum(): lax.all_to_all(both.reshape(patches, units // patches, lanes), 'patch', 0...  12.4 us
    ppermute x4, starting transfers between devices, to_patch(): lax.ppermute(x, 'patch', [(i, (i + by) % count) for i in range(count)])  11.9 us
    ppermute x16, waiting for transfers between devices, to_partner(): return lax.ppermute(x, 'shard', [(i, i ^ 1) for i in range(count)])  6.69 us
  transfers between devices with their start and end apart: 37, of which 16 were waited for; matrix products, arithmetic and copies ran while one was open for 1% of the time, Pallas kernels for 15%

profile of v2, /device:TPU:1, one launch (start us, length us, event | category | flops | bytes accessed | tf_op | source)
XLA Modules:
  0.0 171.1 jit_solution(3969553265679445809)
XLA Ops:
  0.6 6.9 %collective-permute-start = (bf16[128,512]{1,0:T(8,128)(2,1)}, bf16[128,512]{1,0:T(8,128)(2,1)S(1)}, u32[]{:S(2)}, u32[]{:S(2)}) collective-permute-start(bf16[128,512]{1,0:T(8,128)(2,1)} %node.1), channel_id=1, source_target_pairs={{0,6},{1,7},{2,0},{3,1},{4,2},{5,3},{6,4},{7,5},{8,14},{9,15},{10,... | collective-permute-start | bytes 393224 | tf_op jit(solution)/shard_map/ppermute | solution.py:17
  7.5 1.0 collective-permute-start.1
  8.5 2.3 %collective-permute-start.2 = (bf16[128,512]{1,0:T(8,128)(2,1)}, bf16[128,512]{1,0:T(8,128)(2,1)S(1)}, u32[]{:S(2)}, u32[]{:S(2)}) collective-permute-start(bf16[128,512]{1,0:T(8,128)(2,1)} %node.1), channel_id=1, source_target_pairs={{0,2},{1,3},{2,4},{3,5},{4,6},{5,7},{6,0},{7,1},{8,10},{9,11},{10,... | collective-permute-start | bytes 393224 | tf_op jit(solution)/shard_map/ppermute | solution.py:17
  10.8 1.5 collective-permute-start.3
  12.3 0.7 add_add_fusion
  13.0 7.0 %collective-permute-start.4 = (bf16[128,512]{1,0:T(8,128)(2,1)S(1)}, bf16[128,512]{1,0:T(8,128)(2,1)S(1)}, u32[]{:S(2)}, u32[]{:S(2)}) collective-permute-start(bf16[128,512]{1,0:T(8,128)(2,1)S(1)} %collective-permute-done.refs_0_), channel_id=1, source_target_pairs={{0,1},{1,0},{2,3},{3,2},{4,5},{5,4},{6,7},{7,6},{8,9},{9,8},{10,11... | collective-permute-start | bytes 393224 | tf_op jit(solution)/shard_map/ppermute | solution.py:22
  20.0 1.7 collective-permute-start.5
  21.9 0.8 collective-permute-done.5.refs_5_
  22.7 0.4 collective-permute-done.6.refs_6_
  23.1 1.7 shard_map.155
  24.7 5.9 %collective-permute-start.9 = (bf16[128,512]{1,0:T(8,128)(2,1)S(1)}, bf16[128,512]{1,0:T(8,128)(2,1)S(1)}, u32[]{:S(2)}, u32[]{:S(2)}) collective-permute-start(bf16[128,512]{1,0:T(8,128)(2,1)S(1)} %get-tuple-element.52), channel_id=1, source_target_pairs={{0,248},{8,0},{16,8},{24,16},{32,24},{40,32},{48,40},{56,48},{64,5... | collective-permute-start | bytes 393224 | tf_op jit(solution)/shard_map/ppermute | solution.py:27
  30.7 0.7 and_add_fusion
  31.4 0.2 copy.20.s_col
  31.6 0.2 copy.21.r_col
  31.8 1.3 collective-permute-done.9.refs_2_
  33.2 2.0 %collective-permute-start.10 = (bf16[128,512]{1,0:T(8,128)(2,1)S(1)}, bf16[128,512]{1,0:T(8,128)(2,1)S(1)}, u32[]{:S(2)}, u32[]{:S(2)}) collective-permute-start(bf16[128,512]{1,0:T(8,128)(2,1)S(1)} %collective-permute-done.9.refs_2_), channel_id=1, source_target_pairs={{0,1},{1,0},{2,3},{3,2},{4,5},{5,4},{6,7},{7,6},{8,9},{9,8},{10,11... | collective-permute-start | bytes 393224 | tf_op jit(solution)/shard_map/ppermute | solution.py:22
  35.2 4.1 %collective-permute-done.7.refs_0_ = bf16[128,512]{1,0:T(8,128)(2,1)S(1)} collective-permute-done((bf16[128,512]{1,0:T(8,128)(2,1)S(1)}, bf16[128,512]{1,0:T(8,128)(2,1)S(1)}, u32[]{:S(2)}, u32[]{:S(2)}) %collective-permute-start.7) | collective-permute-done | bytes 131104 | tf_op jit(solution)/shard_map/ppermute | solution.py:27
  39.3 1.5 collective-permute-start.8
  40.8 6.5 %shard_map.154 = (bf16[1024,512]{1,0:T(8,128)(2,1)S(1)}, bf16[1024,512]{1,0:T(8,128)(2,1)}, f32[1024,512]{1,0:T(8,128)S(1)}) custom-call(s32[1024,1]{1,0:T(8,128)S(1)} %copy.20.s_col, s32[1024,1]{1,0:T(8,128)S(1)} %copy.21.r_col, bf16[1024,512]{1,0:T(8,128)(2,1)} %edge_h.5, bf16[128,512]{1,0:T(8,128)(2,1)} %node.1, ...), custom_call_target="tpu_custom_call" | custom-call | flops 3800000000 | bytes 8388608 | tf_op jit(solution)/shard_map/pallas_call | solution.py:94
  47.4 7.3 %shard_map.156 = (bf16[1024,512]{1,0:T(8,128)(2,1)}, bf16[1024,512]{1,0:T(8,128)(2,1)}, f32[1024,512]{1,0:T(8,128)}, f32[1024,512]{1,0:T(8,128)}, f32[1024,1]{1,...) custom-call(s32[1024,1]{1,0:T(8,128)S(1)} %copy.20.s_col, s32[1,1024]{1,0:T(1,128)S(1)} %bitcast.18, ...), custom_call_target="tpu_custom_call" | custom-call | flops 2700000000 | bytes 12582912 | tf_op jit(solution)/shard_map/pallas_call | solution.py:94
  54.8 1.9 %collective-permute-done.11.came = bf16[512,512]{1,0:T(8,128)(2,1)S(1)} collective-permute-done((bf16[512,512]{1,0:T(8,128)(2,1)S(1)}, bf16[512,512]{1,0:T(8,128)(2,1)S(1)}, u32[]{:S(2)}, u32[]{:S(2)}) %collective-permute-start.11) | collective-permute-done | bytes 524320 | tf_op jit(solution)/shard_map/ppermute | solution.py:22
  56.8 1.9 %collective-permute-start.12 = (bf16[128,512]{1,0:T(8,128)(2,1)S(1)}, bf16[128,512]{1,0:T(8,128)(2,1)S(1)}, u32[]{:S(2)}, u32[]{:S(2)}) collective-permute-start(bf16[128,512]{1,0:T(8,128)(2,1)S(1)} %get-tuple-element.62), channel_id=1, source_target_pairs={{0,2},{1,3},{2,4},{3,5},{4,6},{5,7},{6,0},{7,1},{8,10},{9,11},{10,... | collective-permute-start | bytes 393224 | tf_op jit(solution)/shard_map/ppermute | solution.py:17
  58.7 4.0 %collective-permute-start.13 = (bf16[128,512]{1,0:T(8,128)(2,1)S(1)}, bf16[128,512]{1,0:T(8,128)(2,1)S(1)}, u32[]{:S(2)}, u32[]{:S(2)}) collective-permute-start(bf16[128,512]{1,0:T(8,128)(2,1)S(1)} %get-tuple-element.63), channel_id=1, source_target_pairs={{0,4},{1,5},{2,6},{3,7},{4,0},{5,1},{6,2},{7,3},{8,12},{9,13},{10,... | collective-permute-start | bytes 393224 | tf_op jit(solution)/shard_map/ppermute | solution.py:17
  62.7 2.8 %collective-permute-start.14 = (bf16[128,512]{1,0:T(8,128)(2,1)S(1)}, bf16[128,512]{1,0:T(8,128)(2,1)S(1)}, u32[]{:S(2)}, u32[]{:S(2)}) collective-permute-start(bf16[128,512]{1,0:T(8,128)(2,1)S(1)} %get-tuple-element.64), channel_id=1, source_target_pairs={{0,6},{1,7},{2,0},{3,1},{4,2},{5,3},{6,4},{7,5},{8,14},{9,15},{10,... | collective-permute-start | bytes 393224 | tf_op jit(solution)/shard_map/ppermute | solution.py:17
  65.5 1.5 collective-permute-done.12.got1
  67.0 8.1 %collective-permute-done.13.got2 = bf16[128,512]{1,0:T(8,128)(2,1)S(1)} collective-permute-done((bf16[128,512]{1,0:T(8,128)(2,1)S(1)}, bf16[128,512]{1,0:T(8,128)(2,1)S(1)}, u32[]{:S(2)}, u32[]{:S(2)}) %collective-permute-start.13) | collective-permute-done | bytes 131104 | tf_op jit(solution)/shard_map/ppermute | solution.py:17
  75.1 1.8 %shard_map.158 = (bf16[128,512]{1,0:T(8,128)(2,1)S(1)}, f32[128,512]{1,0:T(8,128)S(1)}, f32[512,768]{1,0:T(8,128)S(1)}, bf16[512,768]{1,0:T(8,128)(2,1)S(1)}) custom-call(s32[1]{0:T(128)} %bitcast.5.core, f32[128,512]{1,0:T(8,128)S(1)} %get-tuple-element.61.own, bf16[128,512]{1,0:T(8,128)(2,1)S(1)} %collective-permute-done.12.got1, ...), custom_call_target="tpu_custom_call" | custom-call | flops 800000000 | bytes 5242880 | tf_op jit(solution)/shard_map/pallas_call | solution.py:94
  76.9 0.5 collective-permute-start.30
  77.5 2.0 %collective-permute-start.15 = (bf16[128,512]{1,0:T(8,128)(2,1)S(1)}, bf16[128,512]{1,0:T(8,128)(2,1)S(1)}, u32[]{:S(2)}, u32[]{:S(2)}) collective-permute-start(bf16[128,512]{1,0:T(8,128)(2,1)S(1)} %get-tuple-element.65.refs_0_), channel_id=1, source_target_pairs={{0,6},{1,7},{2,0},{3,1},{4,2},{5,3},{6,4},{7,5},{8,14},{9,15},{10,... | collective-permute-start | bytes 393224 | tf_op jit(solution)/shard_map/ppermute | solution.py:17
  79.5 1.3 collective-permute-start.16
  80.8 2.3 %collective-permute-start.17 = (bf16[128,512]{1,0:T(8,128)(2,1)S(1)}, bf16[128,512]{1,0:T(8,128)(2,1)S(1)}, u32[]{:S(2)}, u32[]{:S(2)}) collective-permute-start(bf16[128,512]{1,0:T(8,128)(2,1)S(1)} %get-tuple-element.65.refs_0_), channel_id=1, source_target_pairs={{0,2},{1,3},{2,4},{3,5},{4,6},{5,7},{6,0},{7,1},{8,10},{9,11},{10,... | collective-permute-start | bytes 393224 | tf_op jit(solution)/shard_map/ppermute | solution.py:17
  83.1 0.9 collective-permute-start.18
  84.0 3.1 %collective-permute-done.15.refs_1_ = bf16[128,512]{1,0:T(8,128)(2,1)S(1)} collective-permute-done((bf16[128,512]{1,0:T(8,128)(2,1)S(1)}, bf16[128,512]{1,0:T(8,128)(2,1)S(1)}, u32[]{:S(2)}, u32[]{:S(2)}) %collective-permute-start.15) | collective-permute-done | bytes 131104 | tf_op jit(solution)/shard_map/ppermute | solution.py:17
  87.1 0.9 collective-permute-start.19
  88.1 6.1 %collective-permute-done.16.refs_2_ = bf16[128,512]{1,0:T(8,128)(2,1)S(1)} collective-permute-done((bf16[128,512]{1,0:T(8,128)(2,1)S(1)}, bf16[128,512]{1,0:T(8,128)(2,1)S(1)}, u32[]{:S(2)}, u32[]{:S(2)}) %collective-permute-start.16) | collective-permute-done | bytes 131104 | tf_op jit(solution)/shard_map/ppermute | solution.py:17
  94.2 0.6 collective-permute-start.20
  94.7 1.1 shard_map.166
  95.8 4.6 %all-to-all-start.1 = ((bf16[32,16,768]{2,1,0:T(8,128)(2,1)}), bf16[32,16,768]{2,1,0:T(8,128)(2,1)}, u32[]{:S(2)}, u32[]{:S(2)}) async-start(bf16[32,16,768]{2,1,0:T(8,128)(2,1)} %bitcast.10), calls=%async_computation.1 | async-start | bytes 1572864 | tf_op jit(solution)/shard_map/all_to_all | solution.py:399
  100.5 10.0 %shard_map.159 = (bf16[1024,512]{1,0:T(8,128)(2,1)}, bf16[1024,512]{1,0:T(8,128)(2,1)}, bf16[1024,512]{1,0:T(8,128)(2,1)}, f32[256,512]{1,0:T(8,128)S(1)}, bf16[...) custom-call(s32[1]{0:T(128)} %bitcast.5.core, s32[1024,1]{1,0:T(8,128)S(1)} %copy.21.r_col, ...), custom_call_target="tpu_custom_call" | custom-call | flops 5500000256 | bytes 16777216 | tf_op jit(solution)/shard_map/pallas_call | solution.py:94
  110.5 0.6 collective-permute-start.29
  111.1 2.3 %collective-permute-done.29.came = bf16[512,1024]{1,0:T(8,128)(2,1)S(1)} collective-permute-done((bf16[512,1024]{1,0:T(8,128)(2,1)S(1)}, bf16[512,1024]{1,0:T(8,128)(2,1)S(1)}, u32[]{:S(2)}, u32[]{:S(2)}) %collective-permute-start.29) | collective-permute-done | bytes 1048608 | tf_op jit(solution)/shard_map/ppermute | solution.py:22
  113.4 1.2 shard_map.165
  114.6 0.2 all-to-all-done.1.node_h
  114.7 7.8 %all-to-all-start = ((bf16[32,16,1024]{2,1,0:T(8,128)(2,1)}), bf16[32,16,1024]{2,1,0:T(8,128)(2,1)S(1)}, u32[]{:S(2)}, u32[]{:S(2)}) async-start(bf16[32,16,1024]{2,1,0:T(8,128)(2,1)} %bitcast.9), calls=%async_computation | async-start | bytes 2097152 | tf_op jit(solution)/shard_map/all_to_all | solution.py:399
  122.5 0.7 collective-permute-start.22
  123.3 1.2 collective-permute-done.22.came
  124.5 1.6 collective-permute-start.23
  126.1 4.4 %collective-permute-start.24 = (bf16[128,512]{1,0:T(8,128)(2,1)S(1)}, bf16[128,512]{1,0:T(8,128)(2,1)S(1)}, u32[]{:S(2)}, u32[]{:S(2)}) collective-permute-start(bf16[128,512]{1,0:T(8,128)(2,1)S(1)} %get-tuple-element.71), channel_id=1, source_target_pairs={{0,248},{8,0},{16,8},{24,16},{32,24},{40,32},{48,40},{56,48},{64,5... | collective-permute-start | bytes 393224 | tf_op jit(solution)/shard_map/ppermute | solution.py:27
  130.5 4.5 %shard_map.160.sums = f32[1024,512]{1,0:T(8,128)S(1)} custom-call(s32[1,1024]{1,0:T(1,128)S(1)} %bitcast.22, s32[1,1024]{1,0:T(1,128)S(1)} %bitcast.19, bf16[1024,512]{1,0:T(8,128)(2,1)} %get-tuple-element.66.d_pre_h, bf16[1024,512]{1,0:T(8,128)(2,1)} %get-tuple-element.67.dxs_h, bf16[1536,512]{1,0:T(8,128)(2,1)} %w1_h.1), custom_call_target="tpu_custom_call" | custom-call | flops 2700000000 | bytes 5242880 | tf_op jit(solution)/shard_map/pallas_call | solution.py:94
  135.0 7.4 %collective-permute-done.23.low = bf16[128,512]{1,0:T(8,128)(2,1)S(1)} collective-permute-done((bf16[128,512]{1,0:T(8,128)(2,1)S(1)}, bf16[128,512]{1,0:T(8,128)(2,1)S(1)}, u32[]{:S(2)}, u32[]{:S(2)}) %collective-permute-start.23) | collective-permute-done | bytes 131104 | tf_op jit(solution)/shard_map/ppermute | solution.py:27
  142.3 0.7 shard_map.162
  143.0 2.7 %collective-permute-start.25 = (bf16[512,512]{1,0:T(8,128)(2,1)S(1)}, bf16[512,512]{1,0:T(8,128)(2,1)S(1)}, u32[]{:S(2)}, u32[]{:S(2)}) collective-permute-start(bf16[512,512]{1,0:T(8,128)(2,1)S(1)} %get-tuple-element.73), channel_id=1, source_target_pairs={{0,1},{1,0},{2,3},{3,2},{4,5},{5,4},{6,7},{7,6},{8,9},{9,8},{10,11... | collective-permute-start | bytes 1572872 | tf_op jit(solution)/shard_map/ppermute | solution.py:22
  145.8 1.3 shard_map.167
  147.0 0.3 collective-permute-start.31
  147.4 3.3 %collective-permute-start.26 = (bf16[128,512]{1,0:T(8,128)(2,1)S(1)}, bf16[128,512]{1,0:T(8,128)(2,1)S(1)}, u32[]{:S(2)}, u32[]{:S(2)}) collective-permute-start(bf16[128,512]{1,0:T(8,128)(2,1)S(1)} %get-tuple-element.75), channel_id=1, source_target_pairs={{0,2},{1,3},{2,4},{3,5},{4,6},{5,7},{6,0},{7,1},{8,10},{9,11},{10,... | collective-permute-start | bytes 393224 | tf_op jit(solution)/shard_map/ppermute | solution.py:17
  150.7 2.3 %collective-permute-start.27 = (bf16[128,512]{1,0:T(8,128)(2,1)S(1)}, bf16[128,512]{1,0:T(8,128)(2,1)S(1)}, u32[]{:S(2)}, u32[]{:S(2)}) collective-permute-start(bf16[128,512]{1,0:T(8,128)(2,1)S(1)} %get-tuple-element.76), channel_id=1, source_target_pairs={{0,4},{1,5},{2,6},{3,7},{4,0},{5,1},{6,2},{7,3},{8,12},{9,13},{10,... | collective-permute-start | bytes 393224 | tf_op jit(solution)/shard_map/ppermute | solution.py:17
  152.9 2.5 %collective-permute-start.28 = (bf16[128,512]{1,0:T(8,128)(2,1)S(1)}, bf16[128,512]{1,0:T(8,128)(2,1)S(1)}, u32[]{:S(2)}, u32[]{:S(2)}) collective-permute-start(bf16[128,512]{1,0:T(8,128)(2,1)S(1)} %get-tuple-element.77), channel_id=1, source_target_pairs={{0,6},{1,7},{2,0},{3,1},{4,2},{5,3},{6,4},{7,5},{8,14},{9,15},{10,... | collective-permute-start | bytes 393224 | tf_op jit(solution)/shard_map/ppermute | solution.py:17
  155.5 0.9 collective-permute-start.32
  156.4 2.2 %collective-permute-start.33 = (bf16[16,1792]{1,0:T(8,128)(2,1)S(1)}, bf16[16,1792]{1,0:T(8,128)(2,1)S(1)}, u32[]{:S(2)}, u32[]{:S(2)}) collective-permute-start(bf16[16,1792]{1,0:T(8,128)(2,1)S(1)} %get-tuple-element.85), channel_id=1, source_target_pairs={{0,6},{1,7},{2,0},{3,1},{4,2},{5,3},{6,4},{7,5},{8,14},{9,15},{10,... | collective-permute-start | bytes 172040 | tf_op jit(solution)/shard_map/ppermute | solution.py:17
  158.6 8.1 %collective-permute-done.32.got2 = bf16[16,1792]{1,0:T(8,128)(2,1)S(1)} collective-permute-done((bf16[16,1792]{1,0:T(8,128)(2,1)S(1)}, bf16[16,1792]{1,0:T(8,128)(2,1)S(1)}, u32[]{:S(2)}, u32[]{:S(2)}) %collective-permute-start.32) | collective-permute-done | bytes 57376 | tf_op jit(solution)/shard_map/ppermute | solution.py:17
  166.7 2.2 %collective-permute-done.33.got3 = bf16[16,1792]{1,0:T(8,128)(2,1)S(1)} collective-permute-done((bf16[16,1792]{1,0:T(8,128)(2,1)S(1)}, bf16[16,1792]{1,0:T(8,128)(2,1)S(1)}, u32[]{:S(2)}, u32[]{:S(2)}) %collective-permute-start.33) | collective-permute-done | bytes 57376 | tf_op jit(solution)/shard_map/ppermute | solution.py:17
  169.0 0.6 collective-permute-start.34
  169.5 0.7 shard_map.164
  170.4 0.7 shard_map.169
  (41 shorter events, 0.8 us)
Async XLA Ops:
  0.6 12.4 %collective-permute-start = (bf16[128,512]{1,0:T(8,128)(2,1)}, bf16[128,512]{1,0:T(8,128)(2,1)S(1)}, u32[]{:S(2)}, u32[]{:S(2)}) collective-permute-start(bf16[128,512]{1,0:T(8,128)(2,1)} %node.1), channel_id=1, source_target_pairs={{0,6},{1,7},{2,0},{3,1},{4,2},{5,3},{6,4},{7,5},{8,14},{9,15},{10,... | collective-permute-start | bytes 393224 | tf_op jit(solution)/shard_map/ppermute | solution.py:17
  7.5 12.5 %collective-permute-start.1 = (bf16[128,512]{1,0:T(8,128)(2,1)}, bf16[128,512]{1,0:T(8,128)(2,1)S(1)}, u32[]{:S(2)}, u32[]{:S(2)}) collective-permute-start(bf16[128,512]{1,0:T(8,128)(2,1)} %node.1), channel_id=1, source_target_pairs={{0,4},{1,5},{2,6},{3,7},{4,0},{5,1},{6,2},{7,3},{8,12},{9,13},{10,... | collective-permute-start | bytes 393224 | tf_op jit(solution)/shard_map/ppermute | solution.py:17
  8.5 13.2 %collective-permute-start.2 = (bf16[128,512]{1,0:T(8,128)(2,1)}, bf16[128,512]{1,0:T(8,128)(2,1)S(1)}, u32[]{:S(2)}, u32[]{:S(2)}) collective-permute-start(bf16[128,512]{1,0:T(8,128)(2,1)} %node.1), channel_id=1, source_target_pairs={{0,2},{1,3},{2,4},{3,5},{4,6},{5,7},{6,0},{7,1},{8,10},{9,11},{10,... | collective-permute-start | bytes 393224 | tf_op jit(solution)/shard_map/ppermute | solution.py:17
  10.8 11.1 %collective-permute-start.3 = (bf16[128,512]{1,0:T(8,128)(2,1)}, bf16[128,512]{1,0:T(8,128)(2,1)S(1)}, u32[]{:S(2)}, u32[]{:S(2)}) collective-permute-start(bf16[128,512]{1,0:T(8,128)(2,1)} %node.1), channel_id=1, source_target_pairs={{0,1},{1,0},{2,3},{3,2},{4,5},{5,4},{6,7},{7,6},{8,9},{9,8},{10,11... | collective-permute-start | bytes 393224 | tf_op jit(solution)/shard_map/ppermute | solution.py:22
  13.0 8.9 %collective-permute-start.4 = (bf16[128,512]{1,0:T(8,128)(2,1)S(1)}, bf16[128,512]{1,0:T(8,128)(2,1)S(1)}, u32[]{:S(2)}, u32[]{:S(2)}) collective-permute-start(bf16[128,512]{1,0:T(8,128)(2,1)S(1)} %collective-permute-done.refs_0_), channel_id=1, source_target_pairs={{0,1},{1,0},{2,3},{3,2},{4,5},{5,4},{6,7},{7,6},{8,9},{9,8},{10,11... | collective-permute-start | bytes 393224 | tf_op jit(solution)/shard_map/ppermute | solution.py:22
  20.0 2.7 %collective-permute-start.5 = (bf16[128,512]{1,0:T(8,128)(2,1)S(1)}, bf16[128,512]{1,0:T(8,128)(2,1)S(1)}, u32[]{:S(2)}, u32[]{:S(2)}) collective-permute-start(bf16[128,512]{1,0:T(8,128)(2,1)S(1)} %collective-permute-done.1.refs_1_), channel_id=1, source_target_pairs={{0,1},{1,0},{2,3},{3,2},{4,5},{5,4},{6,7},{7,6},{8,9},{9,8},{10,11... | collective-permute-start | bytes 393224 | tf_op jit(solution)/shard_map/ppermute | solution.py:22
  21.7 1.3 collective-permute-start.6
  24.7 8.4 %collective-permute-start.9 = (bf16[128,512]{1,0:T(8,128)(2,1)S(1)}, bf16[128,512]{1,0:T(8,128)(2,1)S(1)}, u32[]{:S(2)}, u32[]{:S(2)}) collective-permute-start(bf16[128,512]{1,0:T(8,128)(2,1)S(1)} %get-tuple-element.52), channel_id=1, source_target_pairs={{0,248},{8,0},{16,8},{24,16},{32,24},{40,32},{48,40},{56,48},{64,5... | collective-permute-start | bytes 393224 | tf_op jit(solution)/shard_map/ppermute | solution.py:27
  30.7 8.6 %collective-permute-start.7 = (bf16[128,512]{1,0:T(8,128)(2,1)S(1)}, bf16[128,512]{1,0:T(8,128)(2,1)S(1)}, u32[]{:S(2)}, u32[]{:S(2)}) collective-permute-start(bf16[128,512]{1,0:T(8,128)(2,1)S(1)} %get-tuple-element.51), channel_id=1, source_target_pairs={{0,8},{8,16},{16,24},{24,32},{32,40},{40,48},{48,56},{56,64},{64,7... | collective-permute-start | bytes 393224 | tf_op jit(solution)/shard_map/ppermute | solution.py:27
  33.2 14.1 %collective-permute-start.10 = (bf16[128,512]{1,0:T(8,128)(2,1)S(1)}, bf16[128,512]{1,0:T(8,128)(2,1)S(1)}, u32[]{:S(2)}, u32[]{:S(2)}) collective-permute-start(bf16[128,512]{1,0:T(8,128)(2,1)S(1)} %collective-permute-done.9.refs_2_), channel_id=1, source_target_pairs={{0,1},{1,0},{2,3},{3,2},{4,5},{5,4},{6,7},{7,6},{8,9},{9,8},{10,11... | collective-permute-start | bytes 393224 | tf_op jit(solution)/shard_map/ppermute | solution.py:22
  39.3 8.0 %collective-permute-start.8 = (bf16[128,512]{1,0:T(8,128)(2,1)S(1)}, bf16[128,512]{1,0:T(8,128)(2,1)S(1)}, u32[]{:S(2)}, u32[]{:S(2)}) collective-permute-start(bf16[128,512]{1,0:T(8,128)(2,1)S(1)} %collective-permute-done.7.refs_0_), channel_id=1, source_target_pairs={{0,1},{1,0},{2,3},{3,2},{4,5},{5,4},{6,7},{7,6},{8,9},{9,8},{10,11... | collective-permute-start | bytes 393224 | tf_op jit(solution)/shard_map/ppermute | solution.py:22
  47.3 27.7 %copy-start = (bf16[128,512]{1,0:T(8,128)(2,1)S(1)}, bf16[128,512]{1,0:T(8,128)(2,1)}, u32[]{:S(2)}) copy-start(bf16[128,512]{1,0:T(8,128)(2,1)} %node.1) | copy-start | bytes 393220
  47.3 27.7 %copy-start.1 = (bf16[1024,512]{1,0:T(8,128)(2,1)S(1)}, bf16[1024,512]{1,0:T(8,128)(2,1)}, u32[]{:S(2)}) copy-start(bf16[1024,512]{1,0:T(8,128)(2,1)} %w1.1) | copy-start | bytes 3145732
  47.3 27.7 %copy-start.2 = (bf16[512,512]{1,0:T(8,128)(2,1)S(1)}, bf16[512,512]{1,0:T(8,128)(2,1)}, u32[]{:S(2)}) copy-start(bf16[512,512]{1,0:T(8,128)(2,1)} %w2.1) | copy-start | bytes 1572868
  47.4 27.7 %copy-start.3 = (bf16[128,512]{1,0:T(8,128)(2,1)S(1)}, bf16[128,512]{1,0:T(8,128)(2,1)}, u32[]{:S(2)}) copy-start(bf16[128,512]{1,0:T(8,128)(2,1)} %grad.1) | copy-start | bytes 393220
  54.7 2.0 %collective-permute-start.11 = (bf16[512,512]{1,0:T(8,128)(2,1)S(1)}, bf16[512,512]{1,0:T(8,128)(2,1)S(1)}, u32[]{:S(2)}, u32[]{:S(2)}) collective-permute-start(bf16[512,512]{1,0:T(8,128)(2,1)S(1)} %get-tuple-element.60), channel_id=1, source_target_pairs={{0,1},{1,0},{2,3},{3,2},{4,5},{5,4},{6,7},{7,6},{8,9},{9,8},{10,11... | collective-permute-start | bytes 1572872 | tf_op jit(solution)/shard_map/ppermute | solution.py:22
  56.8 10.2 %collective-permute-start.12 = (bf16[128,512]{1,0:T(8,128)(2,1)S(1)}, bf16[128,512]{1,0:T(8,128)(2,1)S(1)}, u32[]{:S(2)}, u32[]{:S(2)}) collective-permute-start(bf16[128,512]{1,0:T(8,128)(2,1)S(1)} %get-tuple-element.62), channel_id=1, source_target_pairs={{0,2},{1,3},{2,4},{3,5},{4,6},{5,7},{6,0},{7,1},{8,10},{9,11},{10,... | collective-permute-start | bytes 393224 | tf_op jit(solution)/shard_map/ppermute | solution.py:17
  58.7 16.3 %collective-permute-start.13 = (bf16[128,512]{1,0:T(8,128)(2,1)S(1)}, bf16[128,512]{1,0:T(8,128)(2,1)S(1)}, u32[]{:S(2)}, u32[]{:S(2)}) collective-permute-start(bf16[128,512]{1,0:T(8,128)(2,1)S(1)} %get-tuple-element.63), channel_id=1, source_target_pairs={{0,4},{1,5},{2,6},{3,7},{4,0},{5,1},{6,2},{7,3},{8,12},{9,13},{10,... | collective-permute-start | bytes 393224 | tf_op jit(solution)/shard_map/ppermute | solution.py:17
  62.7 12.3 %collective-permute-start.14 = (bf16[128,512]{1,0:T(8,128)(2,1)S(1)}, bf16[128,512]{1,0:T(8,128)(2,1)S(1)}, u32[]{:S(2)}, u32[]{:S(2)}) collective-permute-start(bf16[128,512]{1,0:T(8,128)(2,1)S(1)} %get-tuple-element.64), channel_id=1, source_target_pairs={{0,6},{1,7},{2,0},{3,1},{4,2},{5,3},{6,4},{7,5},{8,14},{9,15},{10,... | collective-permute-start | bytes 393224 | tf_op jit(solution)/shard_map/ppermute | solution.py:17
  76.9 17.8 %collective-permute-start.30 = (bf16[512,768]{1,0:T(8,128)(2,1)S(1)}, bf16[512,768]{1,0:T(8,128)(2,1)S(1)}, u32[]{:S(2)}, u32[]{:S(2)}) collective-permute-start(bf16[512,768]{1,0:T(8,128)(2,1)S(1)} %get-tuple-element.83), channel_id=1, source_target_pairs={{0,1},{1,0},{2,3},{3,2},{4,5},{5,4},{6,7},{7,6},{8,9},{9,8},{10,11... | collective-permute-start | bytes 2359304 | tf_op jit(solution)/shard_map/ppermute | solution.py:22
  77.5 9.7 %collective-permute-start.15 = (bf16[128,512]{1,0:T(8,128)(2,1)S(1)}, bf16[128,512]{1,0:T(8,128)(2,1)S(1)}, u32[]{:S(2)}, u32[]{:S(2)}) collective-permute-start(bf16[128,512]{1,0:T(8,128)(2,1)S(1)} %get-tuple-element.65.refs_0_), channel_id=1, source_target_pairs={{0,6},{1,7},{2,0},{3,1},{4,2},{5,3},{6,4},{7,5},{8,14},{9,15},{10,... | collective-permute-start | bytes 393224 | tf_op jit(solution)/shard_map/ppermute | solution.py:17
  79.5 14.6 %collective-permute-start.16 = (bf16[128,512]{1,0:T(8,128)(2,1)S(1)}, bf16[128,512]{1,0:T(8,128)(2,1)S(1)}, u32[]{:S(2)}, u32[]{:S(2)}) collective-permute-start(bf16[128,512]{1,0:T(8,128)(2,1)S(1)} %get-tuple-element.65.refs_0_), channel_id=1, source_target_pairs={{0,4},{1,5},{2,6},{3,7},{4,0},{5,1},{6,2},{7,3},{8,12},{9,13},{10,... | collective-permute-start | bytes 393224 | tf_op jit(solution)/shard_map/ppermute | solution.py:17
  80.8 13.9 %collective-permute-start.17 = (bf16[128,512]{1,0:T(8,128)(2,1)S(1)}, bf16[128,512]{1,0:T(8,128)(2,1)S(1)}, u32[]{:S(2)}, u32[]{:S(2)}) collective-permute-start(bf16[128,512]{1,0:T(8,128)(2,1)S(1)} %get-tuple-element.65.refs_0_), channel_id=1, source_target_pairs={{0,2},{1,3},{2,4},{3,5},{4,6},{5,7},{6,0},{7,1},{8,10},{9,11},{10,... | collective-permute-start | bytes 393224 | tf_op jit(solution)/shard_map/ppermute | solution.py:17
  83.1 17.4 %collective-permute-start.18 = (bf16[128,512]{1,0:T(8,128)(2,1)S(1)}, bf16[128,512]{1,0:T(8,128)(2,1)S(1)}, u32[]{:S(2)}, u32[]{:S(2)}) collective-permute-start(bf16[128,512]{1,0:T(8,128)(2,1)S(1)} %get-tuple-element.65.refs_0_), channel_id=1, source_target_pairs={{0,1},{1,0},{2,3},{3,2},{4,5},{5,4},{6,7},{7,6},{8,9},{9,8},{10,11... | collective-permute-start | bytes 393224 | tf_op jit(solution)/shard_map/ppermute | solution.py:22
  87.1 13.3 %collective-permute-start.19 = (bf16[128,512]{1,0:T(8,128)(2,1)S(1)}, bf16[128,512]{1,0:T(8,128)(2,1)S(1)}, u32[]{:S(2)}, u32[]{:S(2)}) collective-permute-start(bf16[128,512]{1,0:T(8,128)(2,1)S(1)} %collective-permute-done.15.refs_1_), channel_id=1, source_target_pairs={{0,1},{1,0},{2,3},{3,2},{4,5},{5,4},{6,7},{7,6},{8,9},{9,8},{10,11... | collective-permute-start | bytes 393224 | tf_op jit(solution)/shard_map/ppermute | solution.py:22
  94.2 6.3 %collective-permute-start.20 = (bf16[128,512]{1,0:T(8,128)(2,1)S(1)}, bf16[128,512]{1,0:T(8,128)(2,1)S(1)}, u32[]{:S(2)}, u32[]{:S(2)}) collective-permute-start(bf16[128,512]{1,0:T(8,128)(2,1)S(1)} %collective-permute-done.16.refs_2_), channel_id=1, source_target_pairs={{0,1},{1,0},{2,3},{3,2},{4,5},{5,4},{6,7},{7,6},{8,9},{9,8},{10,11... | collective-permute-start | bytes 393224 | tf_op jit(solution)/shard_map/ppermute | solution.py:22
  94.7 5.7 %collective-permute-start.21 = (bf16[128,512]{1,0:T(8,128)(2,1)S(1)}, bf16[128,512]{1,0:T(8,128)(2,1)S(1)}, u32[]{:S(2)}, u32[]{:S(2)}) collective-permute-start(bf16[128,512]{1,0:T(8,128)(2,1)S(1)} %collective-permute-done.17.refs_3_), channel_id=1, source_target_pairs={{0,1},{1,0},{2,3},{3,2},{4,5},{5,4},{6,7},{7,6},{8,9},{9,8},{10,11... | collective-permute-start | bytes 393224 | tf_op jit(solution)/shard_map/ppermute | solution.py:22
  95.8 19.0 %all-to-all-start.1 = ((bf16[32,16,768]{2,1,0:T(8,128)(2,1)}), bf16[32,16,768]{2,1,0:T(8,128)(2,1)}, u32[]{:S(2)}, u32[]{:S(2)}) async-start(bf16[32,16,768]{2,1,0:T(8,128)(2,1)} %bitcast.10), calls=%async_computation.1 | async-start | bytes 1572864 | tf_op jit(solution)/shard_map/all_to_all | solution.py:399
  110.5 2.9 %collective-permute-start.29 = (bf16[512,1024]{1,0:T(8,128)(2,1)S(1)}, bf16[512,1024]{1,0:T(8,128)(2,1)S(1)}, u32[]{:S(2)}, u32[]{:S(2)}) collective-permute-start(bf16[512,1024]{1,0:T(8,128)(2,1)S(1)} %get-tuple-element.81), channel_id=1, source_target_pairs={{0,1},{1,0},{2,3},{3,2},{4,5},{5,4},{6,7},{7,6},{8,9},{9,8},{10,11... | collective-permute-start | bytes 3145736 | tf_op jit(solution)/shard_map/ppermute | solution.py:22
  114.7 31.0 %all-to-all-start = ((bf16[32,16,1024]{2,1,0:T(8,128)(2,1)}), bf16[32,16,1024]{2,1,0:T(8,128)(2,1)S(1)}, u32[]{:S(2)}, u32[]{:S(2)}) async-start(bf16[32,16,1024]{2,1,0:T(8,128)(2,1)} %bitcast.9), calls=%async_computation | async-start | bytes 2097152 | tf_op jit(solution)/shard_map/all_to_all | solution.py:399
  122.5 1.9 %collective-permute-start.22 = (bf16[256,512]{1,0:T(8,128)(2,1)S(1)}, bf16[256,512]{1,0:T(8,128)(2,1)S(1)}, u32[]{:S(2)}, u32[]{:S(2)}) collective-permute-start(bf16[256,512]{1,0:T(8,128)(2,1)S(1)} %get-tuple-element.69), channel_id=1, source_target_pairs={{0,1},{1,0},{2,3},{3,2},{4,5},{5,4},{6,7},{7,6},{8,9},{9,8},{10,11... | collective-permute-start | bytes 786440 | tf_op jit(solution)/shard_map/ppermute | solution.py:22
  124.5 17.9 %collective-permute-start.23 = (bf16[128,512]{1,0:T(8,128)(2,1)S(1)}, bf16[128,512]{1,0:T(8,128)(2,1)S(1)}, u32[]{:S(2)}, u32[]{:S(2)}) collective-permute-start(bf16[128,512]{1,0:T(8,128)(2,1)S(1)} %get-tuple-element.70), channel_id=1, source_target_pairs={{0,8},{8,16},{16,24},{24,32},{32,40},{40,48},{48,56},{56,64},{64,7... | collective-permute-start | bytes 393224 | tf_op jit(solution)/shard_map/ppermute | solution.py:27
  126.1 16.3 %collective-permute-start.24 = (bf16[128,512]{1,0:T(8,128)(2,1)S(1)}, bf16[128,512]{1,0:T(8,128)(2,1)S(1)}, u32[]{:S(2)}, u32[]{:S(2)}) collective-permute-start(bf16[128,512]{1,0:T(8,128)(2,1)S(1)} %get-tuple-element.71), channel_id=1, source_target_pairs={{0,248},{8,0},{16,8},{24,16},{32,24},{40,32},{48,40},{56,48},{64,5... | collective-permute-start | bytes 393224 | tf_op jit(solution)/shard_map/ppermute | solution.py:27
  143.0 4.3 %collective-permute-start.25 = (bf16[512,512]{1,0:T(8,128)(2,1)S(1)}, bf16[512,512]{1,0:T(8,128)(2,1)S(1)}, u32[]{:S(2)}, u32[]{:S(2)}) collective-permute-start(bf16[512,512]{1,0:T(8,128)(2,1)S(1)} %get-tuple-element.73), channel_id=1, source_target_pairs={{0,1},{1,0},{2,3},{3,2},{4,5},{5,4},{6,7},{7,6},{8,9},{9,8},{10,11... | collective-permute-start | bytes 1572872 | tf_op jit(solution)/shard_map/ppermute | solution.py:22
  147.0 9.4 %collective-permute-start.31 = (bf16[16,1792]{1,0:T(8,128)(2,1)S(1)}, bf16[16,1792]{1,0:T(8,128)(2,1)S(1)}, u32[]{:S(2)}, u32[]{:S(2)}) collective-permute-start(bf16[16,1792]{1,0:T(8,128)(2,1)S(1)} %get-tuple-element.85), channel_id=1, source_target_pairs={{0,2},{1,3},{2,4},{3,5},{4,6},{5,7},{6,0},{7,1},{8,10},{9,11},{10,... | collective-permute-start | bytes 172040 | tf_op jit(solution)/shard_map/ppermute | solution.py:17
  147.4 22.2 %collective-permute-start.26 = (bf16[128,512]{1,0:T(8,128)(2,1)S(1)}, bf16[128,512]{1,0:T(8,128)(2,1)S(1)}, u32[]{:S(2)}, u32[]{:S(2)}) collective-permute-start(bf16[128,512]{1,0:T(8,128)(2,1)S(1)} %get-tuple-element.75), channel_id=1, source_target_pairs={{0,2},{1,3},{2,4},{3,5},{4,6},{5,7},{6,0},{7,1},{8,10},{9,11},{10,... | collective-permute-start | bytes 393224 | tf_op jit(solution)/shard_map/ppermute | solution.py:17
  150.7 18.9 %collective-permute-start.27 = (bf16[128,512]{1,0:T(8,128)(2,1)S(1)}, bf16[128,512]{1,0:T(8,128)(2,1)S(1)}, u32[]{:S(2)}, u32[]{:S(2)}) collective-permute-start(bf16[128,512]{1,0:T(8,128)(2,1)S(1)} %get-tuple-element.76), channel_id=1, source_target_pairs={{0,4},{1,5},{2,6},{3,7},{4,0},{5,1},{6,2},{7,3},{8,12},{9,13},{10,... | collective-permute-start | bytes 393224 | tf_op jit(solution)/shard_map/ppermute | solution.py:17
  152.9 16.6 %collective-permute-start.28 = (bf16[128,512]{1,0:T(8,128)(2,1)S(1)}, bf16[128,512]{1,0:T(8,128)(2,1)S(1)}, u32[]{:S(2)}, u32[]{:S(2)}) collective-permute-start(bf16[128,512]{1,0:T(8,128)(2,1)S(1)} %get-tuple-element.77), channel_id=1, source_target_pairs={{0,6},{1,7},{2,0},{3,1},{4,2},{5,3},{6,4},{7,5},{8,14},{9,15},{10,... | collective-permute-start | bytes 393224 | tf_op jit(solution)/shard_map/ppermute | solution.py:17
  155.5 11.3 %collective-permute-start.32 = (bf16[16,1792]{1,0:T(8,128)(2,1)S(1)}, bf16[16,1792]{1,0:T(8,128)(2,1)S(1)}, u32[]{:S(2)}, u32[]{:S(2)}) collective-permute-start(bf16[16,1792]{1,0:T(8,128)(2,1)S(1)} %get-tuple-element.85), channel_id=1, source_target_pairs={{0,4},{1,5},{2,6},{3,7},{4,0},{5,1},{6,2},{7,3},{8,12},{9,13},{10,... | collective-permute-start | bytes 172040 | tf_op jit(solution)/shard_map/ppermute | solution.py:17
  156.4 12.5 %collective-permute-start.33 = (bf16[16,1792]{1,0:T(8,128)(2,1)S(1)}, bf16[16,1792]{1,0:T(8,128)(2,1)S(1)}, u32[]{:S(2)}, u32[]{:S(2)}) collective-permute-start(bf16[16,1792]{1,0:T(8,128)(2,1)S(1)} %get-tuple-element.85), channel_id=1, source_target_pairs={{0,6},{1,7},{2,0},{3,1},{4,2},{5,3},{6,4},{7,5},{8,14},{9,15},{10,... | collective-permute-start | bytes 172040 | tf_op jit(solution)/shard_map/ppermute | solution.py:17
  169.0 1.5 collective-permute-start.34

commit v3 on v2

--- a/solution.py
+++ b/solution.py
@@ -125,8 +125,8 @@
     high[...] = total[128:].astype(BF16)
 
 
-TILE = 256
-TILES = 4
+TILE = 512
+TILES = 2
 
 
 def tiles(body):
@@ -205,12 +205,8 @@
             begin(here.at[rows, :], there.at[rows, :], out_sem.at[k, i])
 
     tiles(tile)
-    for k in (2, 3, 0, 1):
-        sums = dot(add_rows(r_row[...], 256, 256 * k), news[...])
-        if k < 2:
-            keep_o[pl.ds(256 * k, 256), :] = sums
-        else:
-            send_o[pl.ds(256 * (k - 2), 256), :] = sums.astype(BF16)
+    keep_o[...] = dot(add_rows(r_row[...], 512), news[...])
+    send_o[...] = dot(add_rows(r_row[...], 512, 512), news[...]).astype(BF16)
 
     def finish(i, rows):
         for k, (here, there) in enumerate(leaving):
@@ -251,15 +247,22 @@
         send_o[:, pl.ds(256 * k, 256)] = dot_tn(left, right[:, pl.ds(theirs, 256)]).astype(BF16)
 
 
-def edge_backward_kernel(core, r_col, s_row, grad_h, normed_h, inv_h, slope_h, edge_h, from_s_h, from_r_h, act_h, *refs):
+def mask_kernel(index, out):
+    def tile(i, rows):
+        out[rows, :] = pick_rows(index[rows, :], 1024)
+
+    tiles(tile)
+
+
+def edge_backward_kernel(core, r_mask, s_row, r_row, grad_h, normed_h, inv_h, slope_h, edge_h, from_s_h, from_r_h, act_h, *refs):
     blocks = refs[:8]
-    (w1_h, w2_h, d_pre_h, dxs_h, grad_o_h, back_keep, back_send, keep_o, send_o) = refs[8:17]
-    (table, d_outs, d_pres, dxss, grad_o, grad, normed, inv, slope) = refs[17:26]
-    (edge, from_s, from_r, act, w1, w2, tile_sem, sem, out_sem) = refs[26:]
+    (w1_h, w2_h, grad_o_h, back_keep, back_send, keep_o, send_o, sums_o) = refs[8:16]
+    (table, lefts, rights, dxss, dxrs, grad_o, grad, normed, inv, slope) = refs[16:26]
+    (w1, w2, tile_sem, sem, out_sem) = refs[26:]
     streams = ((grad_h, grad), (normed_h, normed), (inv_h, inv), (slope_h, slope))
-    leaving = ((d_pres, d_pre_h), (dxss, dxs_h), (grad_o, grad_o_h))
+    got_block = begin(blocks[4], table.at[pl.ds(512, 128), :], sem.at[6])
     got_w2 = begin(w2_h, w2, sem.at[0])
-    got_w1 = begin(w1_h.at[pl.ds(0, 1024), :], w1, sem.at[1])
+    got_w1 = begin(w1_h, w1, sem.at[1])
 
     def ask(i, rows):
         for k, (there, here) in enumerate(streams):
@@ -267,28 +270,28 @@
 
     tiles(ask)
     late = [
-        begin(there, here, sem.at[2 + k])
-        for k, (there, here) in enumerate(
-            ((edge_h, edge), (from_s_h, from_s), (from_r_h, from_r), (act_h, act))
-        )
+        begin(there, rights.at[k], sem.at[2 + k])
+        for k, there in enumerate((edge_h, from_s_h, from_r_h, act_h))
     ]
     for k, block in enumerate(blocks):
-        table[pl.ds(128 * k, 128), :] = block[...]
+        if k != 4:
+            table[pl.ds(128 * k, 128), :] = block[...]
     got_w2.wait()
     got_w1.wait()
+    got_block.wait()
 
     def tile(i, rows):
         for k, (there, here) in enumerate(streams):
             pltpu.make_async_copy(there.at[rows, :], here.at[rows, :], tile_sem.at[k, i]).wait()
-        g = grad[rows, :].astype(F32) + dot(pick_rows(r_col[rows, :], 1024), table[...])
+        g = grad[rows, :].astype(F32) + dot(r_mask[rows, :], table[...])
         d_out = norm_backward(g, normed[rows, :], inv[rows, :])
-        d_outs[rows, :] = d_out
+        lefts[1, :, rows] = d_out.T
         d_pre = (dot_nt(d_out, w2[...]) * slope[rows, :]).astype(BF16)
-        d_pres[rows, :] = d_pre
+        lefts[0, :, rows] = d_pre.T
         dxss[rows, :] = dot_nt(d_pre, w1[pl.ds(512, 512), :]).astype(BF16)
+        dxrs[rows, :] = dot_nt(d_pre, w1[pl.ds(1024, 512), :]).astype(BF16)
         grad_o[rows, :] = (g + dot_nt(d_pre, w1[pl.ds(0, 512), :])).astype(BF16)
-        for k, (here, there) in enumerate(leaving):
-            begin(here.at[rows, :], there.at[rows, :], out_sem.at[k, i])
+        begin(grad_o.at[rows, :], grad_o_h.at[rows, :], out_sem.at[i])
 
     tiles(tile)
     for k in range(4):
@@ -298,41 +301,35 @@
             back_keep[to, :] = sums
         else:
             back_send[to, :] = sums.astype(BF16)
+
+    def node_sums(i, rows):
+        sums_o[rows, :] = dot(add_rows(s_row[...], TILE, TILE * i), dxss[...]) + dot(
+            add_rows(r_row[...], TILE, TILE * i), dxrs[...]
+        )
+
+    tiles(node_sums)
     mine = pl.multiple_of(core[0] * 256, 256)
     theirs = pl.multiple_of(256 - core[0] * 256, 256)
     for copy in late:
         copy.wait()
-    for k, (left, right) in enumerate(
-        ((d_pres, edge), (d_pres, from_s), (d_pres, from_r), (d_outs, act))
-    ):
-        keep_o[:, pl.ds(256 * k, 256)] = dot_tn(left[...], right[:, pl.ds(mine, 256)])
-        send_o[:, pl.ds(256 * k, 256)] = dot_tn(
-            left[...], right[:, pl.ds(theirs, 256)]
-        ).astype(BF16)
+
+    def product(k, carry):
+        left = lefts[k // 3]
+        to = pl.ds(pl.multiple_of(256 * k, 256), 256)
+        keep_o[:, to] = dot(left, rights[k, :, pl.ds(mine, 256)])
+        send_o[:, to] = dot(left, rights[k, :, pl.ds(theirs, 256)]).astype(BF16)
+        return carry
+
+    lax.fori_loop(0, 4, product, 0)
 
     def finish(i, rows):
-        for k, (here, there) in enumerate(leaving):
-            pltpu.make_async_copy(here.at[rows, :], there.at[rows, :], out_sem.at[k, i]).wait()
+        pltpu.make_async_copy(grad_o.at[rows, :], grad_o_h.at[rows, :], out_sem.at[i]).wait()
 
     tiles(finish)
 
 
 def add_kernel(keep, came, out):
     out[...] = (keep[...] + came[...].astype(F32)).astype(BF16)
-
-
-def node_sums_kernel(s_row, r_row, d_pre_h, dxs_h, w1_h, out, dxr, d_pre, dxs, w_r, sem):
-    got_w = begin(w1_h.at[pl.ds(1024, 512), :], w_r, sem.at[0])
-    got_d = begin(d_pre_h, d_pre, sem.at[1])
-    got_x = begin(dxs_h, dxs, sem.at[2])
-    got_w.wait()
-    got_d.wait()
-    dxr[...] = dot_nt(d_pre[...], w_r[...]).astype(BF16)
-    got_x.wait()
-    for k in range(4):
-        out[pl.ds(256 * k, 256), :] = dot(add_rows(s_row[...], 256, 256 * k), dxs[...]) + dot(
-            add_rows(r_row[...], 256, 256 * k), dxr[...]
-        )
 
 
 def blocks_total_kernel(edge, node_h, sum_o, send_o, node, sem):
@@ -369,17 +366,21 @@
     high[...] = both[128:].astype(BF16)
 
 
-def returned_kernel(index, sums, low, high, keep_o, send_o):
-    for k in range(4):
-        rows = (
-            sums[pl.ds(256 * k, 256), :]
-            + dot(add_rows(index[:, pl.ds(0, 128)], 256, 256 * k), low[...])
-            + dot(add_rows(index[:, pl.ds(128, 128)], 256, 256 * k), high[...])
-        )
-        if k < 2:
-            keep_o[pl.ds(256 * k, 256), :] = rows
-        else:
-            send_o[pl.ds(256 * (k - 2), 256), :] = rows.astype(BF16)
+def returned_kernel(index, sums, low, high, keep_o, send_o, both):
+    both[pl.ds(0, 128), :] = low[...]
+    both[pl.ds(128, 128), :] = high[...]
+
+    def rows_at(k, first):
+        at = pl.multiple_of(first + 256 * k, 256)
+        return sums[pl.ds(at, 256), :] + dot(add_rows(index[...], 256, at), both[...])
+
+    def part(k, carry):
+        to = pl.ds(pl.multiple_of(256 * k, 256), 256)
+        send_o[to, :] = rows_at(k, 512).astype(BF16)
+        keep_o[to, :] = rows_at(k, 0)
+        return carry
+
+    lax.fori_loop(0, 2, part, 0)
 
 
 def node_total_kernel(own, got1, got2, got3, part, out):
@@ -466,7 +467,7 @@
             pltpu.VMEM((1024, 512), BF16),
             pltpu.VMEM((1536, 512), BF16),
             pltpu.VMEM((1024, 512), BF16),
-            pltpu.SemaphoreType.DMA((7,)),
+            pltpu.SemaphoreType.DMA((3 + TILES,)),
         ],
         flops=3_800_000_000,
         moved=8 * MIB,
@@ -531,39 +532,42 @@
     d_blocks = spread_over_shard(d_agg)
     node_blocks = weight_sum(n_keep, to_partner(n_send))
 
-    d_pre, dxs, grad_edge_latent, back_keep, back_send, w_keep, w_send = call(
+    (r_mask,) = call(mask_kernel, [shape((1024, 1024), BF16)], [r_col], moved=2 * MIB, vmem=8 * MIB)
+    grad_edge_latent, back_keep, back_send, w_keep, w_send, sums = call(
         edge_backward_kernel,
         [
-            shape((1024, 512), BF16),
-            shape((1024, 512), BF16),
             shape((1024, 512), BF16),
             shape((256, 512), F32),
             shape((256, 512), BF16),
             shape((512, 1024), F32),
             shape((512, 1024), BF16),
+            shape((1024, 512), F32),
         ],
-        [core_word, r_col, s_row, grad_edge_new, normed, inv, slope, edge_latent, from_s, from_r, act]
+        [core_word, r_mask, s_row, r_row, grad_edge_new, normed, inv, slope, edge_latent, from_s, from_r, act]
         + d_blocks
         + [w_edge_first, w_edge_second],
         words=(0,),
-        far=(3, 4, 5, 6, 7, 8, 9, 10, 19, 20),
-        far_out=(0, 1, 2),
-        scratch=[pltpu.VMEM((1024, 512), BF16)] * 6
+        far=(4, 5, 6, 7, 8, 9, 10, 11, 16, 20, 21),
+        far_out=(0,),
+        scratch=[
+            pltpu.VMEM((1024, 512), BF16),
+            pltpu.VMEM((2, 512, 1024), BF16),
+            pltpu.VMEM((4, 1024, 512), BF16),
+        ]
+        + [pltpu.VMEM((1024, 512), BF16)] * 4
         + [
             pltpu.VMEM((1024, 512), F32),
             pltpu.VMEM((1024, 1), F32),
             pltpu.VMEM((1024, 512), F32),
-        ]
-        + [pltpu.VMEM((1024, 512), BF16)] * 5
-        + [
+            pltpu.VMEM((1536, 512), BF16),
             pltpu.VMEM((512, 512), BF16),
             pltpu.SemaphoreType.DMA((4, TILES)),
-            pltpu.SemaphoreType.DMA((6,)),
-            pltpu.SemaphoreType.DMA((3, TILES)),
+            pltpu.SemaphoreType.DMA((7,)),
+            pltpu.SemaphoreType.DMA((TILES,)),
         ],
-        flops=5_500_000_000,
+        flops=8_200_000_000,
         moved=16 * MIB,
-        vmem=28 * MIB,
+        vmem=22 * MIB,
     )
     back_prev, back_next = call(
         pair_add_kernel,
@@ -575,20 +579,11 @@
     got_next = to_patch(back_prev, -1)
     got_prev = to_patch(back_next, 1)
     edge_blocks = weight_sum(w_keep, to_partner(w_send))
-    (sums,) = call(
-        node_sums_kernel,
-        [shape((1024, 512), F32)],
-        [s_row, r_row, d_pre, dxs, w_edge_first],
-        far=(2, 3, 4),
-        scratch=[pltpu.VMEM((1024, 512), BF16)] * 3
-        + [pltpu.VMEM((512, 512), BF16), pltpu.SemaphoreType.DMA((3,))],
-        flops=2_700_000_000,
-        moved=5 * MIB,
-    )
     node_keep, node_send = call(
         returned_kernel,
         [shape((512, 512), F32), shape((512, 512), BF16)],
         [half.reshape(1, 256), sums, got_prev, got_next],
+        scratch=[pltpu.VMEM((256, 512), BF16)],
         flops=300_000_000,
         moved=4 * MIB,
         vmem=8 * MIB,

time: 172 us -> 179 us (1.041)
  local copies, waits for them, and re-layouts: 0.61 us -> 5.53 us
  waiting for transfers between devices: 48.7 us -> 52.1 us
    unnamed x8 -> x22, local copies, waits for them, and re-layouts: 0.03 us -> 4.95 us
    ppermute x4, waiting for transfers between devices: 12.8 us -> 16 us  [to_patch(): lax.ppermute(x, 'patch', [(i, (i + by) % count) for i in range(count)])]
  transfers between devices with their start and end apart: 37 -> 37, of which waited for: 16 -> 15; matrix products, arithmetic and copies ran while one was open for 1% -> 1% of each run, Pallas kernels for 15% -> 15%
where the time goes in v3:
time: 179 us; the launch traced here: 178 us
  starting transfers between devices  82.1 us (46%)
  waiting for transfers between devices  52.1 us (29%)
  Pallas kernels  36.2 us (20%)
  local copies, waits for them, and re-layouts  5.53 us (3%)
    pallas_call x16, Pallas kernels, call(): pl.pallas_call(kernel, out_shape=out_shapes, in_specs=in_specs, out_specs...  36.2 us
    ppermute x15, starting transfers between devices, over_ring(): lax.ppermute(x, 'shard', [(i, (i + 2 * by) % count) for i in range(count)])  36.2 us
    ppermute x15, waiting for transfers between devices, over_ring(): lax.ppermute(x, 'shard', [(i, (i + 2 * by) % count) for i in range(count)])  29.1 us
    ppermute x16, starting transfers between devices, to_partner(): return lax.ppermute(x, 'shard', [(i, i ^ 1) for i in range(count)])  21.1 us
    ppermute x4, waiting for transfers between devices, to_patch(): lax.ppermute(x, 'patch', [(i, (i + by) % count) for i in range(count)])  16 us
    all_to_all x2, starting transfers between devices, weight_sum(): lax.all_to_all(both.reshape(patches, units // patches, lanes), 'patch', 0...  12.9 us
    ppermute x4, starting transfers between devices, to_patch(): lax.ppermute(x, 'patch', [(i, (i + by) % count) for i in range(count)])  11.9 us
    ppermute x16, waiting for transfers between devices, to_partner(): return lax.ppermute(x, 'shard', [(i, i ^ 1) for i in range(count)])  6.91 us
  transfers between devices with their start and end apart: 37, of which 15 were waited for; matrix products, arithmetic and copies ran while one was open for 1% of the time, Pallas kernels for 15%

profile of v3, /device:TPU:1, one launch (start us, length us, event | category | flops | bytes accessed | tf_op | source)
XLA Modules:
  0.0 178.2 jit_solution(5625138088141146505)
XLA Ops:
  0.6 6.9 %collective-permute-start = (bf16[128,512]{1,0:T(8,128)(2,1)}, bf16[128,512]{1,0:T(8,128)(2,1)S(1)}, u32[]{:S(2)}, u32[]{:S(2)}) collective-permute-start(bf16[128,512]{1,0:T(8,128)(2,1)} %node.1), channel_id=1, source_target_pairs={{0,6},{1,7},{2,0},{3,1},{4,2},{5,3},{6,4},{7,5},{8,14},{9,15},{10,... | collective-permute-start | bytes 393224 | tf_op jit(solution)/shard_map/ppermute | solution.py:17
  7.5 1.0 collective-permute-start.1
  8.5 2.3 %collective-permute-start.2 = (bf16[128,512]{1,0:T(8,128)(2,1)}, bf16[128,512]{1,0:T(8,128)(2,1)S(1)}, u32[]{:S(2)}, u32[]{:S(2)}) collective-permute-start(bf16[128,512]{1,0:T(8,128)(2,1)} %node.1), channel_id=1, source_target_pairs={{0,2},{1,3},{2,4},{3,5},{4,6},{5,7},{6,0},{7,1},{8,10},{9,11},{10,... | collective-permute-start | bytes 393224 | tf_op jit(solution)/shard_map/ppermute | solution.py:17
  10.8 1.5 collective-permute-start.3
  12.3 0.7 add_add_fusion
  13.0 7.0 %collective-permute-start.4 = (bf16[128,512]{1,0:T(8,128)(2,1)S(1)}, bf16[128,512]{1,0:T(8,128)(2,1)S(1)}, u32[]{:S(2)}, u32[]{:S(2)}) collective-permute-start(bf16[128,512]{1,0:T(8,128)(2,1)S(1)} %collective-permute-done.refs_0_), channel_id=1, source_target_pairs={{0,1},{1,0},{2,3},{3,2},{4,5},{5,4},{6,7},{7,6},{8,9},{9,8},{10,11... | collective-permute-start | bytes 393224 | tf_op jit(solution)/shard_map/ppermute | solution.py:22
  20.0 1.7 collective-permute-start.5
  21.9 0.8 collective-permute-done.5.refs_5_
  23.1 1.7 shard_map.156
  24.7 5.9 %collective-permute-start.9 = (bf16[128,512]{1,0:T(8,128)(2,1)S(1)}, bf16[128,512]{1,0:T(8,128)(2,1)S(1)}, u32[]{:S(2)}, u32[]{:S(2)}) collective-permute-start(bf16[128,512]{1,0:T(8,128)(2,1)S(1)} %get-tuple-element.51), channel_id=1, source_target_pairs={{0,248},{8,0},{16,8},{24,16},{32,24},{40,32},{48,40},{56,48},{64,5... | collective-permute-start | bytes 393224 | tf_op jit(solution)/shard_map/ppermute | solution.py:27
  30.7 0.7 select_select_fusion
  31.9 1.3 collective-permute-done.9.refs_2_
  33.2 2.0 %collective-permute-start.10 = (bf16[128,512]{1,0:T(8,128)(2,1)S(1)}, bf16[128,512]{1,0:T(8,128)(2,1)S(1)}, u32[]{:S(2)}, u32[]{:S(2)}) collective-permute-start(bf16[128,512]{1,0:T(8,128)(2,1)S(1)} %collective-permute-done.9.refs_2_), channel_id=1, source_target_pairs={{0,1},{1,0},{2,3},{3,2},{4,5},{5,4},{6,7},{7,6},{8,9},{9,8},{10,11... | collective-permute-start | bytes 393224 | tf_op jit(solution)/shard_map/ppermute | solution.py:22
  35.2 4.1 %collective-permute-done.7.refs_0_ = bf16[128,512]{1,0:T(8,128)(2,1)S(1)} collective-permute-done((bf16[128,512]{1,0:T(8,128)(2,1)S(1)}, bf16[128,512]{1,0:T(8,128)(2,1)S(1)}, u32[]{:S(2)}, u32[]{:S(2)}) %collective-permute-start.7) | collective-permute-done | bytes 131104 | tf_op jit(solution)/shard_map/ppermute | solution.py:27
  39.3 1.5 collective-permute-start.8
  40.8 5.5 %shard_map.155 = (bf16[1024,512]{1,0:T(8,128)(2,1)S(1)}, bf16[1024,512]{1,0:T(8,128)(2,1)}, f32[1024,512]{1,0:T(8,128)S(1)}) custom-call(s32[1024,1]{1,0:T(8,128)S(1)} %copy.21.s_col, s32[1024,1]{1,0:T(8,128)S(1)} %copy.17.index.r_col, bf16[1024,512]{1,0:T(8,128)(2,1)} %edge_h.5, bf16[128,512]{1,0:T(8,128)(2,1)} %node.1, ...), custom_call_target="tpu_custom_call" | custom-call | flops 3800000000 | bytes 8388608 | tf_op jit(solution)/shard_map/pallas_call | solution.py:94
  46.4 6.0 %shard_map.157 = (bf16[1024,512]{1,0:T(8,128)(2,1)}, bf16[1024,512]{1,0:T(8,128)(2,1)}, f32[1024,512]{1,0:T(8,128)}, f32[1024,512]{1,0:T(8,128)}, f32[1024,1]{1,...) custom-call(s32[1024,1]{1,0:T(8,128)S(1)} %copy.21.s_col, s32[1,1024]{1,0:T(1,128)S(1)} %bitcast.20, ...), custom_call_target="tpu_custom_call" | custom-call | flops 2700000000 | bytes 12582912 | tf_op jit(solution)/shard_map/pallas_call | solution.py:94
  52.5 1.9 %collective-permute-done.11.came = bf16[512,512]{1,0:T(8,128)(2,1)S(1)} collective-permute-done((bf16[512,512]{1,0:T(8,128)(2,1)S(1)}, bf16[512,512]{1,0:T(8,128)(2,1)S(1)}, u32[]{:S(2)}, u32[]{:S(2)}) %collective-permute-start.11) | collective-permute-done | bytes 524320 | tf_op jit(solution)/shard_map/ppermute | solution.py:22
  54.5 2.1 %collective-permute-start.12 = (bf16[128,512]{1,0:T(8,128)(2,1)S(1)}, bf16[128,512]{1,0:T(8,128)(2,1)S(1)}, u32[]{:S(2)}, u32[]{:S(2)}) collective-permute-start(bf16[128,512]{1,0:T(8,128)(2,1)S(1)} %get-tuple-element.61), channel_id=1, source_target_pairs={{0,2},{1,3},{2,4},{3,5},{4,6},{5,7},{6,0},{7,1},{8,10},{9,11},{10,... | collective-permute-start | bytes 393224 | tf_op jit(solution)/shard_map/ppermute | solution.py:17
  56.6 4.0 %collective-permute-start.13 = (bf16[128,512]{1,0:T(8,128)(2,1)S(1)}, bf16[128,512]{1,0:T(8,128)(2,1)S(1)}, u32[]{:S(2)}, u32[]{:S(2)}) collective-permute-start(bf16[128,512]{1,0:T(8,128)(2,1)S(1)} %get-tuple-element.62), channel_id=1, source_target_pairs={{0,4},{1,5},{2,6},{3,7},{4,0},{5,1},{6,2},{7,3},{8,12},{9,13},{10,... | collective-permute-start | bytes 393224 | tf_op jit(solution)/shard_map/ppermute | solution.py:17
  60.6 2.8 %collective-permute-start.14 = (bf16[128,512]{1,0:T(8,128)(2,1)S(1)}, bf16[128,512]{1,0:T(8,128)(2,1)S(1)}, u32[]{:S(2)}, u32[]{:S(2)}) collective-permute-start(bf16[128,512]{1,0:T(8,128)(2,1)S(1)} %get-tuple-element.63), channel_id=1, source_target_pairs={{0,6},{1,7},{2,0},{3,1},{4,2},{5,3},{6,4},{7,5},{8,14},{9,15},{10,... | collective-permute-start | bytes 393224 | tf_op jit(solution)/shard_map/ppermute | solution.py:17
  63.4 1.5 collective-permute-done.12.got1
  64.9 8.1 %collective-permute-done.13.got2 = bf16[128,512]{1,0:T(8,128)(2,1)S(1)} collective-permute-done((bf16[128,512]{1,0:T(8,128)(2,1)S(1)}, bf16[128,512]{1,0:T(8,128)(2,1)S(1)}, u32[]{:S(2)}, u32[]{:S(2)}) %collective-permute-start.13) | collective-permute-done | bytes 131104 | tf_op jit(solution)/shard_map/ppermute | solution.py:17
  73.0 1.8 %shard_map.159 = (bf16[128,512]{1,0:T(8,128)(2,1)S(1)}, f32[128,512]{1,0:T(8,128)S(1)}, f32[512,768]{1,0:T(8,128)S(1)}, bf16[512,768]{1,0:T(8,128)(2,1)S(1)}) custom-call(s32[1]{0:T(128)} %bitcast.3.core, f32[128,512]{1,0:T(8,128)S(1)} %get-tuple-element.60.own, bf16[128,512]{1,0:T(8,128)(2,1)S(1)} %collective-permute-done.12.got1, ...), custom_call_target="tpu_custom_call" | custom-call | flops 800000000 | bytes 5242880 | tf_op jit(solution)/shard_map/pallas_call | solution.py:94
  74.8 0.5 collective-permute-start.30
  75.4 1.9 %collective-permute-start.15 = (bf16[128,512]{1,0:T(8,128)(2,1)S(1)}, bf16[128,512]{1,0:T(8,128)(2,1)S(1)}, u32[]{:S(2)}, u32[]{:S(2)}) collective-permute-start(bf16[128,512]{1,0:T(8,128)(2,1)S(1)} %get-tuple-element.64.refs_0_), channel_id=1, source_target_pairs={{0,6},{1,7},{2,0},{3,1},{4,2},{5,3},{6,4},{7,5},{8,14},{9,15},{10,... | collective-permute-start | bytes 393224 | tf_op jit(solution)/shard_map/ppermute | solution.py:17
  77.2 1.4 collective-permute-start.16
  78.7 2.3 %collective-permute-start.17 = (bf16[128,512]{1,0:T(8,128)(2,1)S(1)}, bf16[128,512]{1,0:T(8,128)(2,1)}, u32[]{:S(2)}, u32[]{:S(2)}) collective-permute-start(bf16[128,512]{1,0:T(8,128)(2,1)S(1)} %get-tuple-element.64.refs_0_), channel_id=1, source_target_pairs={{0,2},{1,3},{2,4},{3,5},{4,6},{5,7},{6,0},{7,1},{8,10},{9,11},{10,... | collective-permute-start | bytes 393224 | tf_op jit(solution)/shard_map/ppermute | solution.py:17
  81.0 0.9 collective-permute-start.18
  81.9 3.2 %collective-permute-done.15.refs_1_ = bf16[128,512]{1,0:T(8,128)(2,1)S(1)} collective-permute-done((bf16[128,512]{1,0:T(8,128)(2,1)S(1)}, bf16[128,512]{1,0:T(8,128)(2,1)S(1)}, u32[]{:S(2)}, u32[]{:S(2)}) %collective-permute-start.15) | collective-permute-done | bytes 131104 | tf_op jit(solution)/shard_map/ppermute | solution.py:17
  85.1 0.9 collective-permute-start.19
  86.0 5.8 %collective-permute-done.16.refs_2_ = bf16[128,512]{1,0:T(8,128)(2,1)S(1)} collective-permute-done((bf16[128,512]{1,0:T(8,128)(2,1)S(1)}, bf16[128,512]{1,0:T(8,128)(2,1)S(1)}, u32[]{:S(2)}, u32[]{:S(2)}) %collective-permute-start.16) | collective-permute-done | bytes 131104 | tf_op jit(solution)/shard_map/ppermute | solution.py:17
  91.9 0.6 collective-permute-start.20
  92.4 0.5 shard_map.154.r_mask
  92.9 1.0 shard_map.166
  93.9 5.0 %all-to-all-start.1 = ((bf16[32,16,768]{2,1,0:T(8,128)(2,1)}), bf16[32,16,768]{2,1,0:T(8,128)(2,1)}, u32[]{:S(2)}, u32[]{:S(2)}) async-start(bf16[32,16,768]{2,1,0:T(8,128)(2,1)} %bitcast.10), calls=%async_computation.1 | async-start | bytes 1572864 | tf_op jit(solution)/shard_map/all_to_all | solution.py:400
  99.0 14.2 %shard_map.160 = (bf16[1024,512]{1,0:T(8,128)(2,1)}, f32[256,512]{1,0:T(8,128)S(1)}, bf16[256,512]{1,0:T(8,128)(2,1)S(1)}, f32[512,1024]{1,0:T(8,128)S(1)}, bf16...) custom-call(s32[1]{0:T(128)} %bitcast.3.core, bf16[1024,1024]{1,0:T(8,128)(2,1)S(1)} %shard_map.154.r_mask, ...), custom_call_target="tpu_custom_call" | custom-call | flops 8200000000 | bytes 16777216 | tf_op jit(solution)/shard_map/pallas_call | solution.py:94
  113.3 1.3 copy-done
  114.6 0.8 copy-done.4
  115.4 0.7 copy-done.9
  116.5 2.3 %collective-permute-done.29.came = bf16[512,1024]{1,0:T(8,128)(2,1)S(1)} collective-permute-done((bf16[512,1024]{1,0:T(8,128)(2,1)S(1)}, bf16[512,1024]{1,0:T(8,128)(2,1)S(1)}, u32[]{:S(2)}, u32[]{:S(2)}) %collective-permute-start.29) | collective-permute-done | bytes 1048608 | tf_op jit(solution)/shard_map/ppermute | solution.py:22
  118.8 1.2 shard_map.165
  119.9 7.8 %all-to-all-start = ((bf16[32,16,1024]{2,1,0:T(8,128)(2,1)}), bf16[32,16,1024]{2,1,0:T(8,128)(2,1)S(1)}, u32[]{:S(2)}, u32[]{:S(2)}) async-start(bf16[32,16,1024]{2,1,0:T(8,128)(2,1)} %bitcast.9), calls=%async_computation | async-start | bytes 2097152 | tf_op jit(solution)/shard_map/all_to_all | solution.py:400
  127.8 0.7 collective-permute-start.22
  128.5 1.4 collective-permute-done.22.came
  129.9 1.0 copy-done.5
  131.0 1.6 collective-permute-start.23
  132.6 4.4 %collective-permute-start.24 = (bf16[128,512]{1,0:T(8,128)(2,1)S(1)}, bf16[128,512]{1,0:T(8,128)(2,1)S(1)}, u32[]{:S(2)}, u32[]{:S(2)}) collective-permute-start(bf16[128,512]{1,0:T(8,128)(2,1)S(1)} %get-tuple-element.69), channel_id=1, source_target_pairs={{0,248},{8,0},{16,8},{24,16},{32,24},{40,32},{48,40},{56,48},{64,5... | collective-permute-start | bytes 393224 | tf_op jit(solution)/shard_map/ppermute | solution.py:27
  137.0 10.6 %collective-permute-done.23.low = bf16[128,512]{1,0:T(8,128)(2,1)S(1)} collective-permute-done((bf16[128,512]{1,0:T(8,128)(2,1)S(1)}, bf16[128,512]{1,0:T(8,128)(2,1)S(1)}, u32[]{:S(2)}, u32[]{:S(2)}) %collective-permute-start.23) | collective-permute-done | bytes 131104 | tf_op jit(solution)/shard_map/ppermute | solution.py:27
  147.6 1.4 shard_map.162
  149.0 1.0 copy-done.2
  150.0 2.6 %collective-permute-start.25 = (bf16[512,512]{1,0:T(8,128)(2,1)}, bf16[512,512]{1,0:T(8,128)(2,1)S(1)}, u32[]{:S(2)}, u32[]{:S(2)}) collective-permute-start(bf16[512,512]{1,0:T(8,128)(2,1)} %get-tuple-element.71), channel_id=1, source_target_pairs={{0,1},{1,0},{2,3},{3,2},{4,5},{5,4},{6,7},{7,6},{8,9},{9,8},{10,11... | collective-permute-start | bytes 1572872 | tf_op jit(solution)/shard_map/ppermute | solution.py:22
  152.6 1.3 shard_map.167
  153.9 0.6 collective-permute-start.31
  154.5 3.3 %collective-permute-start.26 = (bf16[128,512]{1,0:T(8,128)(2,1)S(1)}, bf16[128,512]{1,0:T(8,128)(2,1)S(1)}, u32[]{:S(2)}, u32[]{:S(2)}) collective-permute-start(bf16[128,512]{1,0:T(8,128)(2,1)S(1)} %get-tuple-element.73), channel_id=1, source_target_pairs={{0,2},{1,3},{2,4},{3,5},{4,6},{5,7},{6,0},{7,1},{8,10},{9,11},{10,... | collective-permute-start | bytes 393224 | tf_op jit(solution)/shard_map/ppermute | solution.py:17
  157.8 2.0 %collective-permute-start.27 = (bf16[128,512]{1,0:T(8,128)(2,1)S(1)}, bf16[128,512]{1,0:T(8,128)(2,1)S(1)}, u32[]{:S(2)}, u32[]{:S(2)}) collective-permute-start(bf16[128,512]{1,0:T(8,128)(2,1)S(1)} %get-tuple-element.74), channel_id=1, source_target_pairs={{0,4},{1,5},{2,6},{3,7},{4,0},{5,1},{6,2},{7,3},{8,12},{9,13},{10,... | collective-permute-start | bytes 393224 | tf_op jit(solution)/shard_map/ppermute | solution.py:17
  159.8 2.7 %collective-permute-start.28 = (bf16[128,512]{1,0:T(8,128)(2,1)S(1)}, bf16[128,512]{1,0:T(8,128)(2,1)S(1)}, u32[]{:S(2)}, u32[]{:S(2)}) collective-permute-start(bf16[128,512]{1,0:T(8,128)(2,1)S(1)} %get-tuple-element.75), channel_id=1, source_target_pairs={{0,6},{1,7},{2,0},{3,1},{4,2},{5,3},{6,4},{7,5},{8,14},{9,15},{10,... | collective-permute-start | bytes 393224 | tf_op jit(solution)/shard_map/ppermute | solution.py:17
  162.5 1.0 collective-permute-start.32
  163.6 1.9 %collective-permute-start.33 = (bf16[16,1792]{1,0:T(8,128)(2,1)S(1)}, bf16[16,1792]{1,0:T(8,128)(2,1)S(1)}, u32[]{:S(2)}, u32[]{:S(2)}) collective-permute-start(bf16[16,1792]{1,0:T(8,128)(2,1)S(1)} %get-tuple-element.83), channel_id=1, source_target_pairs={{0,6},{1,7},{2,0},{3,1},{4,2},{5,3},{6,4},{7,5},{8,14},{9,15},{10,... | collective-permute-start | bytes 172040 | tf_op jit(solution)/shard_map/ppermute | solution.py:17
  165.5 8.8 %collective-permute-done.32.got2 = bf16[16,1792]{1,0:T(8,128)(2,1)S(1)} collective-permute-done((bf16[16,1792]{1,0:T(8,128)(2,1)S(1)}, bf16[16,1792]{1,0:T(8,128)(2,1)S(1)}, u32[]{:S(2)}, u32[]{:S(2)}) %collective-permute-start.32) | collective-permute-done | bytes 57376 | tf_op jit(solution)/shard_map/ppermute | solution.py:17
  174.3 1.7 collective-permute-done.33.got3
  176.0 0.6 collective-permute-start.34
  176.6 0.7 shard_map.164
  177.5 0.7 shard_map.169
  (55 shorter events, 1.9 us)
Async XLA Ops:
  0.6 12.4 %collective-permute-start = (bf16[128,512]{1,0:T(8,128)(2,1)}, bf16[128,512]{1,0:T(8,128)(2,1)S(1)}, u32[]{:S(2)}, u32[]{:S(2)}) collective-permute-start(bf16[128,512]{1,0:T(8,128)(2,1)} %node.1), channel_id=1, source_target_pairs={{0,6},{1,7},{2,0},{3,1},{4,2},{5,3},{6,4},{7,5},{8,14},{9,15},{10,... | collective-permute-start | bytes 393224 | tf_op jit(solution)/shard_map/ppermute | solution.py:17
  7.5 12.5 %collective-permute-start.1 = (bf16[128,512]{1,0:T(8,128)(2,1)}, bf16[128,512]{1,0:T(8,128)(2,1)S(1)}, u32[]{:S(2)}, u32[]{:S(2)}) collective-permute-start(bf16[128,512]{1,0:T(8,128)(2,1)} %node.1), channel_id=1, source_target_pairs={{0,4},{1,5},{2,6},{3,7},{4,0},{5,1},{6,2},{7,3},{8,12},{9,13},{10,... | collective-permute-start | bytes 393224 | tf_op jit(solution)/shard_map/ppermute | solution.py:17
  8.5 13.2 %collective-permute-start.2 = (bf16[128,512]{1,0:T(8,128)(2,1)}, bf16[128,512]{1,0:T(8,128)(2,1)S(1)}, u32[]{:S(2)}, u32[]{:S(2)}) collective-permute-start(bf16[128,512]{1,0:T(8,128)(2,1)} %node.1), channel_id=1, source_target_pairs={{0,2},{1,3},{2,4},{3,5},{4,6},{5,7},{6,0},{7,1},{8,10},{9,11},{10,... | collective-permute-start | bytes 393224 | tf_op jit(solution)/shard_map/ppermute | solution.py:17
  10.8 11.1 %collective-permute-start.3 = (bf16[128,512]{1,0:T(8,128)(2,1)}, bf16[128,512]{1,0:T(8,128)(2,1)S(1)}, u32[]{:S(2)}, u32[]{:S(2)}) collective-permute-start(bf16[128,512]{1,0:T(8,128)(2,1)} %node.1), channel_id=1, source_target_pairs={{0,1},{1,0},{2,3},{3,2},{4,5},{5,4},{6,7},{7,6},{8,9},{9,8},{10,11... | collective-permute-start | bytes 393224 | tf_op jit(solution)/shard_map/ppermute | solution.py:22
  13.0 8.9 %collective-permute-start.4 = (bf16[128,512]{1,0:T(8,128)(2,1)S(1)}, bf16[128,512]{1,0:T(8,128)(2,1)S(1)}, u32[]{:S(2)}, u32[]{:S(2)}) collective-permute-start(bf16[128,512]{1,0:T(8,128)(2,1)S(1)} %collective-permute-done.refs_0_), channel_id=1, source_target_pairs={{0,1},{1,0},{2,3},{3,2},{4,5},{5,4},{6,7},{7,6},{8,9},{9,8},{10,11... | collective-permute-start | bytes 393224 | tf_op jit(solution)/shard_map/ppermute | solution.py:22
  20.0 2.7 %collective-permute-start.5 = (bf16[128,512]{1,0:T(8,128)(2,1)S(1)}, bf16[128,512]{1,0:T(8,128)(2,1)S(1)}, u32[]{:S(2)}, u32[]{:S(2)}) collective-permute-start(bf16[128,512]{1,0:T(8,128)(2,1)S(1)} %collective-permute-done.1.refs_1_), channel_id=1, source_target_pairs={{0,1},{1,0},{2,3},{3,2},{4,5},{5,4},{6,7},{7,6},{8,9},{9,8},{10,11... | collective-permute-start | bytes 393224 | tf_op jit(solution)/shard_map/ppermute | solution.py:22
  21.7 1.3 collective-permute-start.6
  24.7 8.4 %collective-permute-start.9 = (bf16[128,512]{1,0:T(8,128)(2,1)S(1)}, bf16[128,512]{1,0:T(8,128)(2,1)S(1)}, u32[]{:S(2)}, u32[]{:S(2)}) collective-permute-start(bf16[128,512]{1,0:T(8,128)(2,1)S(1)} %get-tuple-element.51), channel_id=1, source_target_pairs={{0,248},{8,0},{16,8},{24,16},{32,24},{40,32},{48,40},{56,48},{64,5... | collective-permute-start | bytes 393224 | tf_op jit(solution)/shard_map/ppermute | solution.py:27
  30.7 8.6 %collective-permute-start.7 = (bf16[128,512]{1,0:T(8,128)(2,1)S(1)}, bf16[128,512]{1,0:T(8,128)(2,1)S(1)}, u32[]{:S(2)}, u32[]{:S(2)}) collective-permute-start(bf16[128,512]{1,0:T(8,128)(2,1)S(1)} %get-tuple-element.50), channel_id=1, source_target_pairs={{0,8},{8,16},{16,24},{24,32},{32,40},{40,48},{48,56},{56,64},{64,7... | collective-permute-start | bytes 393224 | tf_op jit(solution)/shard_map/ppermute | solution.py:27
  33.2 13.2 %collective-permute-start.10 = (bf16[128,512]{1,0:T(8,128)(2,1)S(1)}, bf16[128,512]{1,0:T(8,128)(2,1)S(1)}, u32[]{:S(2)}, u32[]{:S(2)}) collective-permute-start(bf16[128,512]{1,0:T(8,128)(2,1)S(1)} %collective-permute-done.9.refs_2_), channel_id=1, source_target_pairs={{0,1},{1,0},{2,3},{3,2},{4,5},{5,4},{6,7},{7,6},{8,9},{9,8},{10,11... | collective-permute-start | bytes 393224 | tf_op jit(solution)/shard_map/ppermute | solution.py:22
  39.3 7.0 %collective-permute-start.8 = (bf16[128,512]{1,0:T(8,128)(2,1)S(1)}, bf16[128,512]{1,0:T(8,128)(2,1)S(1)}, u32[]{:S(2)}, u32[]{:S(2)}) collective-permute-start(bf16[128,512]{1,0:T(8,128)(2,1)S(1)} %collective-permute-done.7.refs_0_), channel_id=1, source_target_pairs={{0,1},{1,0},{2,3},{3,2},{4,5},{5,4},{6,7},{7,6},{8,9},{9,8},{10,11... | collective-permute-start | bytes 393224 | tf_op jit(solution)/shard_map/ppermute | solution.py:22
  46.4 26.6 %copy-start.6 = (bf16[128,512]{1,0:T(8,128)(2,1)S(1)}, bf16[128,512]{1,0:T(8,128)(2,1)}, u32[]{:S(2)}) copy-start(bf16[128,512]{1,0:T(8,128)(2,1)} %node.1) | copy-start | bytes 393220
  46.4 26.6 %copy-start.7 = (bf16[1024,512]{1,0:T(8,128)(2,1)S(1)}, bf16[1024,512]{1,0:T(8,128)(2,1)}, u32[]{:S(2)}) copy-start(bf16[1024,512]{1,0:T(8,128)(2,1)} %w1.1) | copy-start | bytes 3145732
  46.4 26.6 %copy-start.8 = (bf16[512,512]{1,0:T(8,128)(2,1)S(1)}, bf16[512,512]{1,0:T(8,128)(2,1)}, u32[]{:S(2)}) copy-start(bf16[512,512]{1,0:T(8,128)(2,1)} %w2.1) | copy-start | bytes 1572868
  46.4 26.6 %copy-start.10 = (bf16[128,512]{1,0:T(8,128)(2,1)S(1)}, bf16[128,512]{1,0:T(8,128)(2,1)}, u32[]{:S(2)}) copy-start(bf16[128,512]{1,0:T(8,128)(2,1)} %grad.1) | copy-start | bytes 393220
  52.4 2.0 %collective-permute-start.11 = (bf16[512,512]{1,0:T(8,128)(2,1)S(1)}, bf16[512,512]{1,0:T(8,128)(2,1)S(1)}, u32[]{:S(2)}, u32[]{:S(2)}) collective-permute-start(bf16[512,512]{1,0:T(8,128)(2,1)S(1)} %get-tuple-element.59), channel_id=1, source_target_pairs={{0,1},{1,0},{2,3},{3,2},{4,5},{5,4},{6,7},{7,6},{8,9},{9,8},{10,11... | collective-permute-start | bytes 1572872 | tf_op jit(solution)/shard_map/ppermute | solution.py:22
  54.5 10.4 %collective-permute-start.12 = (bf16[128,512]{1,0:T(8,128)(2,1)S(1)}, bf16[128,512]{1,0:T(8,128)(2,1)S(1)}, u32[]{:S(2)}, u32[]{:S(2)}) collective-permute-start(bf16[128,512]{1,0:T(8,128)(2,1)S(1)} %get-tuple-element.61), channel_id=1, source_target_pairs={{0,2},{1,3},{2,4},{3,5},{4,6},{5,7},{6,0},{7,1},{8,10},{9,11},{10,... | collective-permute-start | bytes 393224 | tf_op jit(solution)/shard_map/ppermute | solution.py:17
  56.6 16.3 %collective-permute-start.13 = (bf16[128,512]{1,0:T(8,128)(2,1)S(1)}, bf16[128,512]{1,0:T(8,128)(2,1)S(1)}, u32[]{:S(2)}, u32[]{:S(2)}) collective-permute-start(bf16[128,512]{1,0:T(8,128)(2,1)S(1)} %get-tuple-element.62), channel_id=1, source_target_pairs={{0,4},{1,5},{2,6},{3,7},{4,0},{5,1},{6,2},{7,3},{8,12},{9,13},{10,... | collective-permute-start | bytes 393224 | tf_op jit(solution)/shard_map/ppermute | solution.py:17
  60.6 12.3 %collective-permute-start.14 = (bf16[128,512]{1,0:T(8,128)(2,1)S(1)}, bf16[128,512]{1,0:T(8,128)(2,1)S(1)}, u32[]{:S(2)}, u32[]{:S(2)}) collective-permute-start(bf16[128,512]{1,0:T(8,128)(2,1)S(1)} %get-tuple-element.63), channel_id=1, source_target_pairs={{0,6},{1,7},{2,0},{3,1},{4,2},{5,3},{6,4},{7,5},{8,14},{9,15},{10,... | collective-permute-start | bytes 393224 | tf_op jit(solution)/shard_map/ppermute | solution.py:17
  74.8 18.1 %collective-permute-start.30 = (bf16[512,768]{1,0:T(8,128)(2,1)S(1)}, bf16[512,768]{1,0:T(8,128)(2,1)S(1)}, u32[]{:S(2)}, u32[]{:S(2)}) collective-permute-start(bf16[512,768]{1,0:T(8,128)(2,1)S(1)} %get-tuple-element.81), channel_id=1, source_target_pairs={{0,1},{1,0},{2,3},{3,2},{4,5},{5,4},{6,7},{7,6},{8,9},{9,8},{10,11... | collective-permute-start | bytes 2359304 | tf_op jit(solution)/shard_map/ppermute | solution.py:22
  75.4 9.7 %collective-permute-start.15 = (bf16[128,512]{1,0:T(8,128)(2,1)S(1)}, bf16[128,512]{1,0:T(8,128)(2,1)S(1)}, u32[]{:S(2)}, u32[]{:S(2)}) collective-permute-start(bf16[128,512]{1,0:T(8,128)(2,1)S(1)} %get-tuple-element.64.refs_0_), channel_id=1, source_target_pairs={{0,6},{1,7},{2,0},{3,1},{4,2},{5,3},{6,4},{7,5},{8,14},{9,15},{10,... | collective-permute-start | bytes 393224 | tf_op jit(solution)/shard_map/ppermute | solution.py:17
  77.2 14.6 %collective-permute-start.16 = (bf16[128,512]{1,0:T(8,128)(2,1)S(1)}, bf16[128,512]{1,0:T(8,128)(2,1)S(1)}, u32[]{:S(2)}, u32[]{:S(2)}) collective-permute-start(bf16[128,512]{1,0:T(8,128)(2,1)S(1)} %get-tuple-element.64.refs_0_), channel_id=1, source_target_pairs={{0,4},{1,5},{2,6},{3,7},{4,0},{5,1},{6,2},{7,3},{8,12},{9,13},{10,... | collective-permute-start | bytes 393224 | tf_op jit(solution)/shard_map/ppermute | solution.py:17
  78.7 13.8 %collective-permute-start.17 = (bf16[128,512]{1,0:T(8,128)(2,1)S(1)}, bf16[128,512]{1,0:T(8,128)(2,1)}, u32[]{:S(2)}, u32[]{:S(2)}) collective-permute-start(bf16[128,512]{1,0:T(8,128)(2,1)S(1)} %get-tuple-element.64.refs_0_), channel_id=1, source_target_pairs={{0,2},{1,3},{2,4},{3,5},{4,6},{5,7},{6,0},{7,1},{8,10},{9,11},{10,... | collective-permute-start | bytes 393224 | tf_op jit(solution)/shard_map/ppermute | solution.py:17
  81.0 18.0 %collective-permute-start.18 = (bf16[128,512]{1,0:T(8,128)(2,1)S(1)}, bf16[128,512]{1,0:T(8,128)(2,1)}, u32[]{:S(2)}, u32[]{:S(2)}) collective-permute-start(bf16[128,512]{1,0:T(8,128)(2,1)S(1)} %get-tuple-element.64.refs_0_), channel_id=1, source_target_pairs={{0,1},{1,0},{2,3},{3,2},{4,5},{5,4},{6,7},{7,6},{8,9},{9,8},{10,11... | collective-permute-start | bytes 393224 | tf_op jit(solution)/shard_map/ppermute | solution.py:22
  85.1 13.9 %collective-permute-start.19 = (bf16[128,512]{1,0:T(8,128)(2,1)S(1)}, bf16[128,512]{1,0:T(8,128)(2,1)}, u32[]{:S(2)}, u32[]{:S(2)}) collective-permute-start(bf16[128,512]{1,0:T(8,128)(2,1)S(1)} %collective-permute-done.15.refs_1_), channel_id=1, source_target_pairs={{0,1},{1,0},{2,3},{3,2},{4,5},{5,4},{6,7},{7,6},{8,9},{9,8},{10,11... | collective-permute-start | bytes 393224 | tf_op jit(solution)/shard_map/ppermute | solution.py:22
  91.9 7.1 %collective-permute-start.20 = (bf16[128,512]{1,0:T(8,128)(2,1)S(1)}, bf16[128,512]{1,0:T(8,128)(2,1)}, u32[]{:S(2)}, u32[]{:S(2)}) collective-permute-start(bf16[128,512]{1,0:T(8,128)(2,1)S(1)} %collective-permute-done.16.refs_2_), channel_id=1, source_target_pairs={{0,1},{1,0},{2,3},{3,2},{4,5},{5,4},{6,7},{7,6},{8,9},{9,8},{10,11... | collective-permute-start | bytes 393224 | tf_op jit(solution)/shard_map/ppermute | solution.py:22
  92.4 6.6 %collective-permute-start.21 = (bf16[128,512]{1,0:T(8,128)(2,1)}, bf16[128,512]{1,0:T(8,128)(2,1)}, u32[]{:S(2)}, u32[]{:S(2)}) collective-permute-start(bf16[128,512]{1,0:T(8,128)(2,1)} %collective-permute-done.17.refs_3_), channel_id=1, source_target_pairs={{0,1},{1,0},{2,3},{3,2},{4,5},{5,4},{6,7},{7,6},{8,9},{9,8},{10,11... | collective-permute-start | bytes 393224 | tf_op jit(solution)/shard_map/ppermute | solution.py:22
  93.9 26.0 %all-to-all-start.1 = ((bf16[32,16,768]{2,1,0:T(8,128)(2,1)}), bf16[32,16,768]{2,1,0:T(8,128)(2,1)}, u32[]{:S(2)}, u32[]{:S(2)}) async-start(bf16[32,16,768]{2,1,0:T(8,128)(2,1)} %bitcast.10), calls=%async_computation.1 | async-start | bytes 1572864 | tf_op jit(solution)/shard_map/all_to_all | solution.py:400
  113.2 1.4 copy-start
  114.6 0.8 copy-start.4
  115.4 0.7 copy-start.9
  116.1 2.7 %collective-permute-start.29 = (bf16[512,1024]{1,0:T(8,128)(2,1)S(1)}, bf16[512,1024]{1,0:T(8,128)(2,1)S(1)}, u32[]{:S(2)}, u32[]{:S(2)}) collective-permute-start(bf16[512,1024]{1,0:T(8,128)(2,1)S(1)} %get-tuple-element.79), channel_id=1, source_target_pairs={{0,1},{1,0},{2,3},{3,2},{4,5},{5,4},{6,7},{7,6},{8,9},{9,8},{10,11... | collective-permute-start | bytes 3145736 | tf_op jit(solution)/shard_map/ppermute | solution.py:22
  119.9 27.7 %copy-start.1 = (f32[1024,512]{1,0:T(8,128)S(1)}, f32[1024,512]{1,0:T(8,128)}, u32[]{:S(2)}) copy-start(f32[1024,512]{1,0:T(8,128)} %copy-done) | copy-start | bytes 6291460
  119.9 32.7 %all-to-all-start = ((bf16[32,16,1024]{2,1,0:T(8,128)(2,1)}), bf16[32,16,1024]{2,1,0:T(8,128)(2,1)S(1)}, u32[]{:S(2)}, u32[]{:S(2)}) async-start(bf16[32,16,1024]{2,1,0:T(8,128)(2,1)} %bitcast.9), calls=%async_computation | async-start | bytes 2097152 | tf_op jit(solution)/shard_map/all_to_all | solution.py:400
  127.8 2.1 %collective-permute-start.22 = (bf16[256,512]{1,0:T(8,128)(2,1)}, bf16[256,512]{1,0:T(8,128)(2,1)S(1)}, u32[]{:S(2)}, u32[]{:S(2)}) collective-permute-start(bf16[256,512]{1,0:T(8,128)(2,1)} %copy-done.9), channel_id=1, source_target_pairs={{0,1},{1,0},{2,3},{3,2},{4,5},{5,4},{6,7},{7,6},{8,9},{9,8},{10,11... | collective-permute-start | bytes 786440 | tf_op jit(solution)/shard_map/ppermute | solution.py:22
  129.9 1.0 copy-start.5
  131.0 16.6 %collective-permute-start.23 = (bf16[128,512]{1,0:T(8,128)(2,1)S(1)}, bf16[128,512]{1,0:T(8,128)(2,1)S(1)}, u32[]{:S(2)}, u32[]{:S(2)}) collective-permute-start(bf16[128,512]{1,0:T(8,128)(2,1)S(1)} %get-tuple-element.68), channel_id=1, source_target_pairs={{0,8},{8,16},{16,24},{24,32},{32,40},{40,48},{48,56},{56,64},{64,7... | collective-permute-start | bytes 393224 | tf_op jit(solution)/shard_map/ppermute | solution.py:27
  132.6 15.0 %collective-permute-start.24 = (bf16[128,512]{1,0:T(8,128)(2,1)S(1)}, bf16[128,512]{1,0:T(8,128)(2,1)S(1)}, u32[]{:S(2)}, u32[]{:S(2)}) collective-permute-start(bf16[128,512]{1,0:T(8,128)(2,1)S(1)} %get-tuple-element.69), channel_id=1, source_target_pairs={{0,248},{8,0},{16,8},{24,16},{32,24},{40,32},{48,40},{56,48},{64,5... | collective-permute-start | bytes 393224 | tf_op jit(solution)/shard_map/ppermute | solution.py:27
  148.9 1.0 copy-start.2
  150.0 4.5 %copy-start.3 = (f32[512,512]{1,0:T(8,128)S(1)}, f32[512,512]{1,0:T(8,128)}, u32[]{:S(2)}) copy-start(f32[512,512]{1,0:T(8,128)} %copy-done.2) | copy-start | bytes 3145732
  150.0 4.5 %collective-permute-start.25 = (bf16[512,512]{1,0:T(8,128)(2,1)}, bf16[512,512]{1,0:T(8,128)(2,1)S(1)}, u32[]{:S(2)}, u32[]{:S(2)}) collective-permute-start(bf16[512,512]{1,0:T(8,128)(2,1)} %get-tuple-element.71), channel_id=1, source_target_pairs={{0,1},{1,0},{2,3},{3,2},{4,5},{5,4},{6,7},{7,6},{8,9},{9,8},{10,11... | collective-permute-start | bytes 1572872 | tf_op jit(solution)/shard_map/ppermute | solution.py:22
  153.9 9.7 %collective-permute-start.31 = (bf16[16,1792]{1,0:T(8,128)(2,1)S(1)}, bf16[16,1792]{1,0:T(8,128)(2,1)S(1)}, u32[]{:S(2)}, u32[]{:S(2)}) collective-permute-start(bf16[16,1792]{1,0:T(8,128)(2,1)S(1)} %get-tuple-element.83), channel_id=1, source_target_pairs={{0,2},{1,3},{2,4},{3,5},{4,6},{5,7},{6,0},{7,1},{8,10},{9,11},{10,... | collective-permute-start | bytes 172040 | tf_op jit(solution)/shard_map/ppermute | solution.py:17
  154.5 22.1 %collective-permute-start.26 = (bf16[128,512]{1,0:T(8,128)(2,1)S(1)}, bf16[128,512]{1,0:T(8,128)(2,1)S(1)}, u32[]{:S(2)}, u32[]{:S(2)}) collective-permute-start(bf16[128,512]{1,0:T(8,128)(2,1)S(1)} %get-tuple-element.73), channel_id=1, source_target_pairs={{0,2},{1,3},{2,4},{3,5},{4,6},{5,7},{6,0},{7,1},{8,10},{9,11},{10,... | collective-permute-start | bytes 393224 | tf_op jit(solution)/shard_map/ppermute | solution.py:17
  157.8 18.8 %collective-permute-start.27 = (bf16[128,512]{1,0:T(8,128)(2,1)S(1)}, bf16[128,512]{1,0:T(8,128)(2,1)S(1)}, u32[]{:S(2)}, u32[]{:S(2)}) collective-permute-start(bf16[128,512]{1,0:T(8,128)(2,1)S(1)} %get-tuple-element.74), channel_id=1, source_target_pairs={{0,4},{1,5},{2,6},{3,7},{4,0},{5,1},{6,2},{7,3},{8,12},{9,13},{10,... | collective-permute-start | bytes 393224 | tf_op jit(solution)/shard_map/ppermute | solution.py:17
  159.8 16.8 %collective-permute-start.28 = (bf16[128,512]{1,0:T(8,128)(2,1)S(1)}, bf16[128,512]{1,0:T(8,128)(2,1)S(1)}, u32[]{:S(2)}, u32[]{:S(2)}) collective-permute-start(bf16[128,512]{1,0:T(8,128)(2,1)S(1)} %get-tuple-element.75), channel_id=1, source_target_pairs={{0,6},{1,7},{2,0},{3,1},{4,2},{5,3},{6,4},{7,5},{8,14},{9,15},{10,... | collective-permute-start | bytes 393224 | tf_op jit(solution)/shard_map/ppermute | solution.py:17
  162.5 11.7 %collective-permute-start.32 = (bf16[16,1792]{1,0:T(8,128)(2,1)S(1)}, bf16[16,1792]{1,0:T(8,128)(2,1)S(1)}, u32[]{:S(2)}, u32[]{:S(2)}) collective-permute-start(bf16[16,1792]{1,0:T(8,128)(2,1)S(1)} %get-tuple-element.83), channel_id=1, source_target_pairs={{0,4},{1,5},{2,6},{3,7},{4,0},{5,1},{6,2},{7,3},{8,12},{9,13},{10,... | collective-permute-start | bytes 172040 | tf_op jit(solution)/shard_map/ppermute | solution.py:17
  163.6 12.4 %collective-permute-start.33 = (bf16[16,1792]{1,0:T(8,128)(2,1)S(1)}, bf16[16,1792]{1,0:T(8,128)(2,1)S(1)}, u32[]{:S(2)}, u32[]{:S(2)}) collective-permute-start(bf16[16,1792]{1,0:T(8,128)(2,1)S(1)} %get-tuple-element.83), channel_id=1, source_target_pairs={{0,6},{1,7},{2,0},{3,1},{4,2},{5,3},{6,4},{7,5},{8,14},{9,15},{10,... | collective-permute-start | bytes 172040 | tf_op jit(solution)/shard_map/ppermute | solution.py:17
  176.0 1.5 collective-permute-start.34

commit v4 on v3

--- a/solution.py
+++ b/solution.py
@@ -28,9 +28,9 @@
 
 
 def spread_over_shard(own):
-    across = over_ring(own, 2)
     after = over_ring(own, -1)
     before = over_ring(own, 1)
+    across = over_ring(own, 2)
     mine = [own, after, across, before]
     return mine + [to_partner(b) for b in mine]
 
@@ -59,6 +59,10 @@
 def add_rows(index_row, count, first=0):
     places = lax.broadcasted_iota(jnp.int32, (count, index_row.shape[1]), 0) + first
     return jnp.where(places == index_row, 1.0, 0.0).astype(BF16)
+
+
+def sigmoid(x):
+    return 0.5 * jnp.tanh(0.5 * x) + 0.5
 
 
 def normalised(out):
@@ -113,16 +117,15 @@
 
 
 def halo_rows_kernel(index, own, *refs):
-    blocks, (low, high, held, sem) = refs[:7], refs[7:]
-    arriving = begin(own, held, sem.at[0])
-    total = None
+    blocks, (low, high, table, sem) = refs[:7], refs[7:]
+    arriving = begin(own, table.at[pl.ds(0, 128), :], sem.at[0])
     for k, block in enumerate(blocks):
-        part = dot(pick_rows(index[...], 128, 128 * (k + 1)), block[...])
-        total = part if total is None else total + part
+        table[pl.ds(128 * (k + 1), 128), :] = block[...]
+    mask = pick_rows(index[...], 1024)
     arriving.wait()
-    total = total + dot(pick_rows(index[...], 128), held[...])
-    low[...] = total[:128].astype(BF16)
-    high[...] = total[128:].astype(BF16)
+    total = dot(mask, table[...]).astype(BF16)
+    low[...] = total[:128]
+    high[...] = total[128:]
 
 
 TILE = 512
@@ -135,15 +138,11 @@
     )
 
 
-def edge_start_kernel(s_col, r_col, edge_h, own_h, *refs):
-    blocks = refs[:7]
-    (w1_h, from_s, from_r_h, pre_o, table, edge, w1, from_r, sem) = refs[7:]
-    got_own = begin(own_h, table.at[pl.ds(0, 128), :], sem.at[0])
-    got_w1 = begin(w1_h, w1, sem.at[1])
-    got_edge = begin(edge_h, edge, sem.at[2])
-    for k, block in enumerate(blocks):
-        table[pl.ds(128 * (k + 1), 128), :] = block[...]
-    got_own.wait()
+def edge_start_kernel(s_col, r_col, r_row, table, edge_h, w1_h, w2_h, *refs):
+    (from_s, from_r_h, pre_o, halo_mask, sum_mask, edge, w1, w2, from_r, sem) = refs
+    got_w1 = begin(w1_h, w1, sem.at[0])
+    got_edge = begin(edge_h, edge, sem.at[1])
+    got_w2 = begin(w2_h, w2, sem.at[2])
 
     def gather(i, rows):
         from_s[rows, :] = dot(pick_rows(s_col[rows, :], 1024), table[...]).astype(BF16)
@@ -160,6 +159,8 @@
             + dot(from_s[rows, :], w1[pl.ds(512, 512), :])
             + dot(from_r[rows, :], w1[pl.ds(1024, 512), :])
         )
+        halo_mask[rows, :] = pick_rows(s_col[rows, :], 512, 1024)
+        sum_mask[rows, :] = add_rows(r_row[...], TILE, TILE * i)
 
     tiles(multiply)
 
@@ -167,20 +168,15 @@
         pltpu.make_async_copy(from_r.at[rows, :], from_r_h.at[rows, :], sem.at[3 + i]).wait()
 
     tiles(finish)
-
-
-def edge_forward_kernel(s_col, r_row, edge_h, from_s, pre_i, *refs):
+    got_w2.wait()
+
+
+def edge_forward_kernel(halo_mask, sum_mask, edge, from_s, pre_i, *refs):
     blocks = refs[:4]
-    (w1_h, w2_h, from_s_h, act_h, slope_h, normed_h, inv_h, keep_o, send_o) = refs[4:13]
-    (table, news, edge, w1, w2, from_s_o, act_o, slope_o, normed_o, inv_o, sem, out_sem) = refs[13:]
-    got_w1 = begin(w1_h.at[pl.ds(512, 512), :], w1, sem.at[0])
-    got_w2 = begin(w2_h, w2, sem.at[1])
-    got_edge = begin(edge_h, edge, sem.at[2])
+    (w1, w2, from_s_h, act_h, slope_h, normed_h, inv_h, keep_o, send_o) = refs[4:13]
+    (table, news, from_s_o, act_o, slope_o, normed_o, inv_o, out_sem) = refs[13:]
     for k, block in enumerate(blocks):
         table[pl.ds(128 * k, 128), :] = block[...]
-    got_w1.wait()
-    got_w2.wait()
-    got_edge.wait()
     leaving = (
         (from_s_o, from_s_h),
         (act_o, act_h),
@@ -190,10 +186,10 @@
     )
 
     def tile(i, rows):
-        halo = dot(pick_rows(s_col[rows, :], 512, 1024), table[...]).astype(BF16)
+        halo = dot(halo_mask[rows, :], table[...]).astype(BF16)
         from_s_o[rows, :] = from_s[rows, :] + halo
-        pre = pre_i[rows, :] + dot(halo, w1[...])
-        sig = jax.nn.sigmoid(pre)
+        pre = pre_i[rows, :] + dot(halo, w1[pl.ds(512, 512), :])
+        sig = sigmoid(pre)
         act = (pre * sig).astype(BF16)
         act_o[rows, :] = act
         slope_o[rows, :] = sig * (1.0 + pre * (1.0 - sig))
@@ -205,8 +201,8 @@
             begin(here.at[rows, :], there.at[rows, :], out_sem.at[k, i])
 
     tiles(tile)
-    keep_o[...] = dot(add_rows(r_row[...], 512), news[...])
-    send_o[...] = dot(add_rows(r_row[...], 512, 512), news[...]).astype(BF16)
+    keep_o[...] = dot(sum_mask[pl.ds(0, 512), :], news[...])
+    send_o[...] = dot(sum_mask[pl.ds(512, 512), :], news[...]).astype(BF16)
 
     def finish(i, rows):
         for k, (here, there) in enumerate(leaving):
@@ -229,7 +225,7 @@
     ).astype(BF16)
     x = node[...]
     pre = dot(x, w1[pl.ds(0, 512), :]) + dot(agg, w1[pl.ds(512, 512), :])
-    sig = jax.nn.sigmoid(pre)
+    sig = sigmoid(pre)
     act = (pre * sig).astype(BF16)
     normed, inv = normalised(dot(act, w2[...]))
     g = grad[...].astype(F32)
@@ -247,22 +243,26 @@
         send_o[:, pl.ds(256 * k, 256)] = dot_tn(left, right[:, pl.ds(theirs, 256)]).astype(BF16)
 
 
-def mask_kernel(index, out):
+def mask_kernel(index, w1_h, w2_h, out, w1, w2, sem):
+    got_w1 = begin(w1_h, w1, sem.at[0])
+    got_w2 = begin(w2_h, w2, sem.at[1])
+
     def tile(i, rows):
         out[rows, :] = pick_rows(index[rows, :], 1024)
 
     tiles(tile)
-
-
-def edge_backward_kernel(core, r_mask, s_row, r_row, grad_h, normed_h, inv_h, slope_h, edge_h, from_s_h, from_r_h, act_h, *refs):
+    got_w1.wait()
+    got_w2.wait()
+
+
+def edge_backward_kernel(core, r_mask, s_row, grad_h, normed_h, inv_h, slope_h, edge_h, from_s_h, from_r_h, act_h, *refs):
     blocks = refs[:8]
-    (w1_h, w2_h, grad_o_h, back_keep, back_send, keep_o, send_o, sums_o) = refs[8:16]
-    (table, lefts, rights, dxss, dxrs, grad_o, grad, normed, inv, slope) = refs[16:26]
-    (w1, w2, tile_sem, sem, out_sem) = refs[26:]
+    (w1, w2, grad_o_h, dxs_h, dxr_h, back_keep, back_send, keep_o, send_o) = refs[8:17]
+    (table, lefts, rights, dxss, dxrs, grad_o, grad, normed, inv, slope) = refs[17:27]
+    (tile_sem, sem, out_sem) = refs[27:]
+    leaving = ((grad_o, grad_o_h), (dxss, dxs_h), (dxrs, dxr_h))
     streams = ((grad_h, grad), (normed_h, normed), (inv_h, inv), (slope_h, slope))
-    got_block = begin(blocks[4], table.at[pl.ds(512, 128), :], sem.at[6])
-    got_w2 = begin(w2_h, w2, sem.at[0])
-    got_w1 = begin(w1_h, w1, sem.at[1])
+    got_block = begin(blocks[4], table.at[pl.ds(512, 128), :], sem.at[4])
 
     def ask(i, rows):
         for k, (there, here) in enumerate(streams):
@@ -270,20 +270,19 @@
 
     tiles(ask)
     late = [
-        begin(there, rights.at[k], sem.at[2 + k])
+        begin(there, rights.at[k], sem.at[k])
         for k, there in enumerate((edge_h, from_s_h, from_r_h, act_h))
     ]
     for k, block in enumerate(blocks):
         if k != 4:
             table[pl.ds(128 * k, 128), :] = block[...]
-    got_w2.wait()
-    got_w1.wait()
     got_block.wait()
 
     def tile(i, rows):
+        came = dot(r_mask[rows, :], table[...])
         for k, (there, here) in enumerate(streams):
             pltpu.make_async_copy(there.at[rows, :], here.at[rows, :], tile_sem.at[k, i]).wait()
-        g = grad[rows, :].astype(F32) + dot(r_mask[rows, :], table[...])
+        g = grad[rows, :].astype(F32) + came
         d_out = norm_backward(g, normed[rows, :], inv[rows, :])
         lefts[1, :, rows] = d_out.T
         d_pre = (dot_nt(d_out, w2[...]) * slope[rows, :]).astype(BF16)
@@ -291,7 +290,8 @@
         dxss[rows, :] = dot_nt(d_pre, w1[pl.ds(512, 512), :]).astype(BF16)
         dxrs[rows, :] = dot_nt(d_pre, w1[pl.ds(1024, 512), :]).astype(BF16)
         grad_o[rows, :] = (g + dot_nt(d_pre, w1[pl.ds(0, 512), :])).astype(BF16)
-        begin(grad_o.at[rows, :], grad_o_h.at[rows, :], out_sem.at[i])
+        for k, (here, there) in enumerate(leaving):
+            begin(here.at[rows, :], there.at[rows, :], out_sem.at[k, i])
 
     tiles(tile)
     for k in range(4):
@@ -302,12 +302,6 @@
         else:
             back_send[to, :] = sums.astype(BF16)
 
-    def node_sums(i, rows):
-        sums_o[rows, :] = dot(add_rows(s_row[...], TILE, TILE * i), dxss[...]) + dot(
-            add_rows(r_row[...], TILE, TILE * i), dxrs[...]
-        )
-
-    tiles(node_sums)
     mine = pl.multiple_of(core[0] * 256, 256)
     theirs = pl.multiple_of(256 - core[0] * 256, 256)
     for copy in late:
@@ -323,13 +317,41 @@
     lax.fori_loop(0, 4, product, 0)
 
     def finish(i, rows):
-        pltpu.make_async_copy(grad_o.at[rows, :], grad_o_h.at[rows, :], out_sem.at[i]).wait()
+        for k, (here, there) in enumerate(leaving):
+            pltpu.make_async_copy(here.at[rows, :], there.at[rows, :], out_sem.at[k, i]).wait()
 
     tiles(finish)
 
 
-def add_kernel(keep, came, out):
-    out[...] = (keep[...] + came[...].astype(F32)).astype(BF16)
+def node_sums_kernel(s_row, r_row, dxs_h, dxr_h, out, dxs, dxr, sem):
+    got_s = begin(dxs_h, dxs, sem.at[0])
+    got_r = begin(dxr_h, dxr, sem.at[1])
+    got_s.wait()
+    got_r.wait()
+
+    def tile(i, rows):
+        out[rows, :] = dot(add_rows(s_row[...], TILE, TILE * i), dxs[...]) + dot(
+            add_rows(r_row[...], TILE, TILE * i), dxr[...]
+        )
+
+    tiles(tile)
+
+
+def add_kernel(keep, came, out_h, out, sem):
+    def part(i, carry):
+        rows = pl.ds(pl.multiple_of(i * 128, 128), 128)
+        out[rows, :] = (keep[rows, :] + came[rows, :].astype(F32)).astype(BF16)
+        begin(out.at[rows, :], out_h.at[rows, :], sem.at[i])
+        return carry
+
+    lax.fori_loop(0, 4, part, 0)
+
+    def finish(i, carry):
+        rows = pl.ds(pl.multiple_of(i * 128, 128), 128)
+        pltpu.make_async_copy(out.at[rows, :], out_h.at[rows, :], sem.at[i]).wait()
+        return carry
+
+    lax.fori_loop(0, 4, finish, 0)
 
 
 def blocks_total_kernel(edge, node_h, sum_o, send_o, node, sem):
@@ -396,7 +418,15 @@
 def weight_sum(keep, came):
     patches = lax.axis_size("patch")
     units, lanes = keep.shape
-    (both,) = call(add_kernel, [shape((units, lanes), BF16)], [keep, came], moved=4 * MIB, vmem=8 * MIB)
+    (both,) = call(
+        add_kernel,
+        [shape((units, lanes), BF16)],
+        [keep, came],
+        far_out=(0,),
+        scratch=[pltpu.VMEM((units, lanes), BF16), pltpu.SemaphoreType.DMA((4,))],
+        moved=4 * MIB,
+        vmem=8 * MIB,
+    )
     return lax.all_to_all(both.reshape(patches, units // patches, lanes), "patch", 0, 0, tiled=True)
 
 
@@ -443,12 +473,12 @@
     r_col, r_row = r_index.reshape(1024, 1), r_index.reshape(1, 1024)
     core_word = core.reshape(1).astype(jnp.int32)
 
-    to_prev, to_next = call(
+    to_prev, to_next, table = call(
         halo_rows_kernel,
-        [shape((128, 512), BF16)] * 2,
+        [shape((128, 512), BF16)] * 2 + [shape((1024, 512), BF16)],
         [half.reshape(256, 1)] + table_blocks,
         far=(1,),
-        scratch=[pltpu.VMEM((128, 512), BF16), pltpu.SemaphoreType.DMA((1,))],
+        scratch=[pltpu.SemaphoreType.DMA((1,))],
         flops=2 * 256 * 1024 * 512,
         moved=2 * MIB,
         vmem=8 * MIB,
@@ -456,21 +486,24 @@
     prev_mine = to_patch(to_next, 1)
     next_mine = to_patch(to_prev, -1)
     halo_blocks = [prev_mine, to_partner(prev_mine), next_mine, to_partner(next_mine)]
-    from_s, from_r, pre = call(
+    from_s, from_r, pre, halo_mask, sum_mask, edge_near, w1_near, w2_near = call(
         edge_start_kernel,
-        [shape((1024, 512), BF16)] * 2 + [shape((1024, 512), F32)],
-        [s_col, r_col, edge_latent] + table_blocks + [w_edge_first],
-        far=(2, 3, 11),
+        [shape((1024, 512), BF16)] * 2
+        + [
+            shape((1024, 512), F32),
+            shape((1024, 512), BF16),
+            shape((1024, 1024), BF16),
+            shape((1024, 512), BF16),
+            shape((1536, 512), BF16),
+            shape((512, 512), BF16),
+        ],
+        [s_col, r_col, r_row, table, edge_latent, w_edge_first, w_edge_second],
+        far=(4, 5, 6),
         far_out=(1,),
-        scratch=[
-            pltpu.VMEM((1024, 512), BF16),
-            pltpu.VMEM((1024, 512), BF16),
-            pltpu.VMEM((1536, 512), BF16),
-            pltpu.VMEM((1024, 512), BF16),
-            pltpu.SemaphoreType.DMA((3 + TILES,)),
-        ],
+        scratch=[pltpu.VMEM((1024, 512), BF16), pltpu.SemaphoreType.DMA((3 + TILES,))],
         flops=3_800_000_000,
         moved=8 * MIB,
+        vmem=10 * MIB,
     )
     from_s, act, slope, normed, inv, agg_keep, agg_send = call(
         edge_forward_kernel,
@@ -483,26 +516,21 @@
             shape((512, 512), F32),
             shape((512, 512), BF16),
         ],
-        [s_col, r_row, edge_latent, from_s, pre] + halo_blocks + [w_edge_first, w_edge_second],
-        far=(2, 9, 10),
+        [halo_mask, sum_mask, edge_near, from_s, pre] + halo_blocks + [w1_near, w2_near],
         far_out=(0, 1, 2, 3, 4),
         scratch=[
             pltpu.VMEM((512, 512), BF16),
             pltpu.VMEM((1024, 512), BF16),
             pltpu.VMEM((1024, 512), BF16),
-            pltpu.VMEM((512, 512), BF16),
-            pltpu.VMEM((512, 512), BF16),
-            pltpu.VMEM((1024, 512), BF16),
             pltpu.VMEM((1024, 512), BF16),
             pltpu.VMEM((1024, 512), F32),
             pltpu.VMEM((1024, 512), F32),
             pltpu.VMEM((1024, 1), F32),
-            pltpu.SemaphoreType.DMA((3,)),
             pltpu.SemaphoreType.DMA((5, TILES)),
         ],
         flops=2_700_000_000,
         moved=12 * MIB,
-        vmem=20 * MIB,
+        vmem=16 * MIB,
     )
     agg_came = to_partner(agg_send)
     agg_own, agg_1, agg_2, agg_3 = call(
@@ -532,23 +560,32 @@
     d_blocks = spread_over_shard(d_agg)
     node_blocks = weight_sum(n_keep, to_partner(n_send))
 
-    (r_mask,) = call(mask_kernel, [shape((1024, 1024), BF16)], [r_col], moved=2 * MIB, vmem=8 * MIB)
-    grad_edge_latent, back_keep, back_send, w_keep, w_send, sums = call(
+    r_mask, w1_back, w2_back = call(
+        mask_kernel,
+        [shape((1024, 1024), BF16), shape((1536, 512), BF16), shape((512, 512), BF16)],
+        [r_col, w_edge_first, w_edge_second],
+        far=(1, 2),
+        scratch=[pltpu.SemaphoreType.DMA((2,))],
+        moved=2 * MIB,
+        vmem=8 * MIB,
+    )
+    grad_edge_latent, dxs, dxr, back_keep, back_send, w_keep, w_send = call(
         edge_backward_kernel,
         [
+            shape((1024, 512), BF16),
+            shape((1024, 512), BF16),
             shape((1024, 512), BF16),
             shape((256, 512), F32),
             shape((256, 512), BF16),
             shape((512, 1024), F32),
             shape((512, 1024), BF16),
-            shape((1024, 512), F32),
         ],
-        [core_word, r_mask, s_row, r_row, grad_edge_new, normed, inv, slope, edge_latent, from_s, from_r, act]
+        [core_word, r_mask, s_row, grad_edge_new, normed, inv, slope, edge_latent, from_s, from_r, act]
         + d_blocks
-        + [w_edge_first, w_edge_second],
+        + [w1_back, w2_back],
         words=(0,),
-        far=(4, 5, 6, 7, 8, 9, 10, 11, 16, 20, 21),
-        far_out=(0,),
+        far=(3, 4, 5, 6, 7, 8, 9, 10, 15),
+        far_out=(0, 1, 2),
         scratch=[
             pltpu.VMEM((1024, 512), BF16),
             pltpu.VMEM((2, 512, 1024), BF16),
@@ -559,11 +596,9 @@
             pltpu.VMEM((1024, 512), F32),
             pltpu.VMEM((1024, 1), F32),
             pltpu.VMEM((1024, 512), F32),
-            pltpu.VMEM((1536, 512), BF16),
-            pltpu.VMEM((512, 512), BF16),
             pltpu.SemaphoreType.DMA((4, TILES)),
-            pltpu.SemaphoreType.DMA((7,)),
-            pltpu.SemaphoreType.DMA((TILES,)),
+            pltpu.SemaphoreType.DMA((5,)),
+            pltpu.SemaphoreType.DMA((3, TILES)),
         ],
         flops=8_200_000_000,
         moved=16 * MIB,
@@ -579,6 +614,16 @@
     got_next = to_patch(back_prev, -1)
     got_prev = to_patch(back_next, 1)
     edge_blocks = weight_sum(w_keep, to_partner(w_send))
+    (sums,) = call(
+        node_sums_kernel,
+        [shape((1024, 512), F32)],
+        [s_row, r_row, dxs, dxr],
+        far=(2, 3),
+        scratch=[pltpu.VMEM((1024, 512), BF16)] * 2 + [pltpu.SemaphoreType.DMA((2,))],
+        flops=2_100_000_000,
+        moved=4 * MIB,
+        vmem=12 * MIB,
+    )
     node_keep, node_send = call(
         returned_kernel,
         [shape((512, 512), F32), shape((512, 512), BF16)],

time: 179 us -> 175 us (0.978)
  waiting for transfers between devices: 52.1 us -> 48.4 us
    ppermute x4, waiting for transfers between devices: 16 us -> 13.5 us  [to_patch(): lax.ppermute(x, 'patch', [(i, (i + by) % count) for i in range(count)])]
    pallas_call x16 -> x17, Pallas kernels: 36.2 us -> 34.8 us  [call(): pl.pallas_call(kernel, out_shape=out_shapes, in_specs=in_specs, out_specs...]
  transfers between devices with their start and end apart: 37 -> 37, of which waited for: 15 -> 14; matrix products, arithmetic and copies ran while one was open for 1% -> 2% of each run, Pallas kernels for 15% -> 15%
where the time goes in v4:
time: 175 us; the launch traced here: 174 us
  starting transfers between devices  82.2 us (47%)
  waiting for transfers between devices  48.4 us (28%)
  Pallas kernels  34.8 us (20%)
  local copies, waits for them, and re-layouts  6.07 us (3%)
  other arithmetic  2.09 us (1%)
    ppermute x15, starting transfers between devices, over_ring(): lax.ppermute(x, 'shard', [(i, (i + 2 * by) % count) for i in range(count)])  36 us
    pallas_call x17, Pallas kernels, call(): pl.pallas_call(kernel, out_shape=out_shapes, in_specs=in_specs, out_specs...  34.8 us
    ppermute x15, waiting for transfers between devices, over_ring(): lax.ppermute(x, 'shard', [(i, (i + 2 * by) % count) for i in range(count)])  29 us
    ppermute x16, starting transfers between devices, to_partner(): return lax.ppermute(x, 'shard', [(i, i ^ 1) for i in range(count)])  21.6 us
    ppermute x4, waiting for transfers between devices, to_patch(): lax.ppermute(x, 'patch', [(i, (i + by) % count) for i in range(count)])  13.5 us
    all_to_all x2, starting transfers between devices, weight_sum(): lax.all_to_all(both.reshape(patches, units // patches, lanes), 'patch', 0...  12.7 us
    ppermute x4, starting transfers between devices, to_patch(): lax.ppermute(x, 'patch', [(i, (i + by) % count) for i in range(count)])  11.9 us
    ppermute x16, waiting for transfers between devices, to_partner(): return lax.ppermute(x, 'shard', [(i, i ^ 1) for i in range(count)])  5.92 us
  transfers between devices with their start and end apart: 37, of which 14 were waited for; matrix products, arithmetic and copies ran while one was open for 2% of the time, Pallas kernels for 15%

profile of v4, /device:TPU:1, one launch (start us, length us, event | category | flops | bytes accessed | tf_op | source)
XLA Modules:
  0.0 174.5 jit_solution(12645019522916154934)
XLA Ops:
  0.6 6.9 %collective-permute-start = (bf16[128,512]{1,0:T(8,128)(2,1)}, bf16[128,512]{1,0:T(8,128)(2,1)S(1)}, u32[]{:S(2)}, u32[]{:S(2)}) collective-permute-start(bf16[128,512]{1,0:T(8,128)(2,1)} %node.1), channel_id=1, source_target_pairs={{0,6},{1,7},{2,0},{3,1},{4,2},{5,3},{6,4},{7,5},{8,14},{9,15},{10,... | collective-permute-start | bytes 393224 | tf_op jit(solution)/shard_map/ppermute | solution.py:17
  7.5 1.0 collective-permute-start.1
  8.5 2.3 %collective-permute-start.2 = (bf16[128,512]{1,0:T(8,128)(2,1)}, bf16[128,512]{1,0:T(8,128)(2,1)S(1)}, u32[]{:S(2)}, u32[]{:S(2)}) collective-permute-start(bf16[128,512]{1,0:T(8,128)(2,1)} %node.1), channel_id=1, source_target_pairs={{0,2},{1,3},{2,4},{3,5},{4,6},{5,7},{6,0},{7,1},{8,10},{9,11},{10,... | collective-permute-start | bytes 393224 | tf_op jit(solution)/shard_map/ppermute | solution.py:17
  10.8 1.5 collective-permute-start.3
  12.3 0.7 add_add_fusion
  13.2 6.8 %collective-permute-start.4 = (bf16[128,512]{1,0:T(8,128)(2,1)S(1)}, bf16[128,512]{1,0:T(8,128)(2,1)S(1)}, u32[]{:S(2)}, u32[]{:S(2)}) collective-permute-start(bf16[128,512]{1,0:T(8,128)(2,1)S(1)} %collective-permute-done.refs_0_), channel_id=1, source_target_pairs={{0,1},{1,0},{2,3},{3,2},{4,5},{5,4},{6,7},{7,6},{8,9},{9,8},{10,11... | collective-permute-start | bytes 393224 | tf_op jit(solution)/shard_map/ppermute | solution.py:22
  20.0 1.7 collective-permute-start.5
  21.7 0.7 and_add_fusion
  23.1 1.4 shard_map.155
  24.4 5.9 %collective-permute-start.9 = (bf16[128,512]{1,0:T(8,128)(2,1)S(1)}, bf16[128,512]{1,0:T(8,128)(2,1)S(1)}, u32[]{:S(2)}, u32[]{:S(2)}) collective-permute-start(bf16[128,512]{1,0:T(8,128)(2,1)S(1)} %get-tuple-element.66), channel_id=1, source_target_pairs={{0,248},{8,0},{16,8},{24,16},{32,24},{40,32},{48,40},{56,48},{64,5... | collective-permute-start | bytes 393224 | tf_op jit(solution)/shard_map/ppermute | solution.py:27
  30.4 0.7 select_select_fusion
  31.3 1.6 collective-permute-done.9.refs_2_
  32.9 2.0 %collective-permute-start.10 = (bf16[128,512]{1,0:T(8,128)(2,1)S(1)}, bf16[128,512]{1,0:T(8,128)(2,1)S(1)}, u32[]{:S(2)}, u32[]{:S(2)}) collective-permute-start(bf16[128,512]{1,0:T(8,128)(2,1)S(1)} %collective-permute-done.9.refs_2_), channel_id=1, source_target_pairs={{0,1},{1,0},{2,3},{3,2},{4,5},{5,4},{6,7},{7,6},{8,9},{9,8},{10,11... | collective-permute-start | bytes 393224 | tf_op jit(solution)/shard_map/ppermute | solution.py:22
  34.9 4.1 %collective-permute-done.7.refs_0_ = bf16[128,512]{1,0:T(8,128)(2,1)S(1)} collective-permute-done((bf16[128,512]{1,0:T(8,128)(2,1)S(1)}, bf16[128,512]{1,0:T(8,128)(2,1)S(1)}, u32[]{:S(2)}, u32[]{:S(2)}) %collective-permute-start.7) | collective-permute-done | bytes 131104 | tf_op jit(solution)/shard_map/ppermute | solution.py:27
  39.0 1.5 collective-permute-start.8
  40.5 4.9 %shard_map.156 = (bf16[1024,512]{1,0:T(8,128)(2,1)S(1)}, bf16[1024,512]{1,0:T(8,128)(2,1)}, f32[1024,512]{1,0:T(8,128)S(1)}, bf16[1024,512]{1,0:T(8,128)(2,1)S(1...) custom-call(s32[1024,1]{1,0:T(8,128)S(1)} %copy.19.s_col, ...), custom_call_target="tpu_custom_call" | custom-call | flops 3800000000 | bytes 8388608 | tf_op jit(solution)/shard_map/pallas_call | solution.py:98
  45.5 0.9 copy-done.9
  46.4 4.5 %shard_map.157 = (bf16[1024,512]{1,0:T(8,128)(2,1)}, bf16[1024,512]{1,0:T(8,128)(2,1)}, f32[1024,512]{1,0:T(8,128)}, f32[1024,512]{1,0:T(8,128)}, f32[1024,1]{1,...) custom-call(bf16[1024,512]{1,0:T(8,128)(2,1)S(1)} %get-tuple-element.60.halo_mask, ...), custom_call_target="tpu_custom_call" | custom-call | flops 2700000000 | bytes 12582912 | tf_op jit(solution)/shard_map/pallas_call | solution.py:98
  51.2 1.9 %collective-permute-done.11.came = bf16[512,512]{1,0:T(8,128)(2,1)S(1)} collective-permute-done((bf16[512,512]{1,0:T(8,128)(2,1)S(1)}, bf16[512,512]{1,0:T(8,128)(2,1)S(1)}, u32[]{:S(2)}, u32[]{:S(2)}) %collective-permute-start.11) | collective-permute-done | bytes 524320 | tf_op jit(solution)/shard_map/ppermute | solution.py:22
  53.2 1.9 %collective-permute-start.12 = (bf16[128,512]{1,0:T(8,128)(2,1)S(1)}, bf16[128,512]{1,0:T(8,128)(2,1)S(1)}, u32[]{:S(2)}, u32[]{:S(2)}) collective-permute-start(bf16[128,512]{1,0:T(8,128)(2,1)S(1)} %get-tuple-element.78), channel_id=1, source_target_pairs={{0,2},{1,3},{2,4},{3,5},{4,6},{5,7},{6,0},{7,1},{8,10},{9,11},{10,... | collective-permute-start | bytes 393224 | tf_op jit(solution)/shard_map/ppermute | solution.py:17
  55.1 4.1 %collective-permute-start.13 = (bf16[128,512]{1,0:T(8,128)(2,1)S(1)}, bf16[128,512]{1,0:T(8,128)(2,1)S(1)}, u32[]{:S(2)}, u32[]{:S(2)}) collective-permute-start(bf16[128,512]{1,0:T(8,128)(2,1)S(1)} %get-tuple-element.79), channel_id=1, source_target_pairs={{0,4},{1,5},{2,6},{3,7},{4,0},{5,1},{6,2},{7,3},{8,12},{9,13},{10,... | collective-permute-start | bytes 393224 | tf_op jit(solution)/shard_map/ppermute | solution.py:17
  59.2 2.8 %collective-permute-start.14 = (bf16[128,512]{1,0:T(8,128)(2,1)S(1)}, bf16[128,512]{1,0:T(8,128)(2,1)S(1)}, u32[]{:S(2)}, u32[]{:S(2)}) collective-permute-start(bf16[128,512]{1,0:T(8,128)(2,1)S(1)} %get-tuple-element.80), channel_id=1, source_target_pairs={{0,6},{1,7},{2,0},{3,1},{4,2},{5,3},{6,4},{7,5},{8,14},{9,15},{10,... | collective-permute-start | bytes 393224 | tf_op jit(solution)/shard_map/ppermute | solution.py:17
  61.9 1.5 collective-permute-done.12.got1
  63.4 8.1 %collective-permute-done.13.got2 = bf16[128,512]{1,0:T(8,128)(2,1)S(1)} collective-permute-done((bf16[128,512]{1,0:T(8,128)(2,1)S(1)}, bf16[128,512]{1,0:T(8,128)(2,1)S(1)}, u32[]{:S(2)}, u32[]{:S(2)}) %collective-permute-start.13) | collective-permute-done | bytes 131104 | tf_op jit(solution)/shard_map/ppermute | solution.py:17
  71.5 1.8 %shard_map.159 = (bf16[128,512]{1,0:T(8,128)(2,1)S(1)}, f32[128,512]{1,0:T(8,128)S(1)}, f32[512,768]{1,0:T(8,128)S(1)}, bf16[512,768]{1,0:T(8,128)(2,1)S(1)}) custom-call(s32[1]{0:T(128)} %bitcast.5.core, f32[128,512]{1,0:T(8,128)S(1)} %get-tuple-element.77.own, bf16[128,512]{1,0:T(8,128)(2,1)S(1)} %collective-permute-done.12.got1, ...), custom_call_target="tpu_custom_call" | custom-call | flops 800000000 | bytes 5242880 | tf_op jit(solution)/shard_map/pallas_call | solution.py:98
  73.3 0.5 collective-permute-start.30
  73.9 1.9 %collective-permute-start.15 = (bf16[128,512]{1,0:T(8,128)(2,1)S(1)}, bf16[128,512]{1,0:T(8,128)(2,1)S(1)}, u32[]{:S(2)}, u32[]{:S(2)}) collective-permute-start(bf16[128,512]{1,0:T(8,128)(2,1)S(1)} %get-tuple-element.81.refs_0_), channel_id=1, source_target_pairs={{0,6},{1,7},{2,0},{3,1},{4,2},{5,3},{6,4},{7,5},{8,14},{9,15},{10,... | collective-permute-start | bytes 393224 | tf_op jit(solution)/shard_map/ppermute | solution.py:17
  75.7 1.5 collective-permute-start.16
  77.2 2.3 %collective-permute-start.17 = (bf16[128,512]{1,0:T(8,128)(2,1)S(1)}, bf16[128,512]{1,0:T(8,128)(2,1)S(1)}, u32[]{:S(2)}, u32[]{:S(2)}) collective-permute-start(bf16[128,512]{1,0:T(8,128)(2,1)S(1)} %get-tuple-element.81.refs_0_), channel_id=1, source_target_pairs={{0,2},{1,3},{2,4},{3,5},{4,6},{5,7},{6,0},{7,1},{8,10},{9,11},{10,... | collective-permute-start | bytes 393224 | tf_op jit(solution)/shard_map/ppermute | solution.py:17
  79.5 0.9 collective-permute-start.18
  80.4 3.2 %collective-permute-done.15.refs_1_ = bf16[128,512]{1,0:T(8,128)(2,1)S(1)} collective-permute-done((bf16[128,512]{1,0:T(8,128)(2,1)S(1)}, bf16[128,512]{1,0:T(8,128)(2,1)S(1)}, u32[]{:S(2)}, u32[]{:S(2)}) %collective-permute-start.15) | collective-permute-done | bytes 131104 | tf_op jit(solution)/shard_map/ppermute | solution.py:17
  83.6 0.9 collective-permute-start.19
  84.6 5.8 %collective-permute-done.16.refs_2_ = bf16[128,512]{1,0:T(8,128)(2,1)S(1)} collective-permute-done((bf16[128,512]{1,0:T(8,128)(2,1)S(1)}, bf16[128,512]{1,0:T(8,128)(2,1)S(1)}, u32[]{:S(2)}, u32[]{:S(2)}) %collective-permute-start.16) | collective-permute-done | bytes 131104 | tf_op jit(solution)/shard_map/ppermute | solution.py:17
  90.4 0.6 collective-permute-start.20
  90.9 1.5 shard_map.154
  92.5 1.1 shard_map.167
  94.6 4.7 %all-to-all-start.1 = ((bf16[32,16,768]{2,1,0:T(8,128)(2,1)}), bf16[32,16,768]{2,1,0:T(8,128)(2,1)}, u32[]{:S(2)}, u32[]{:S(2)}) async-start(bf16[32,16,768]{2,1,0:T(8,128)(2,1)} %bitcast.26), calls=%async_computation.1 | async-start | bytes 1572864 | tf_op jit(solution)/shard_map/all_to_all | solution.py:430
  99.3 0.6 copy-done.10
  100.0 1.6 copy-done.2
  101.6 1.4 copy-done.4
  103.0 10.8 %shard_map.160 = (bf16[1024,512]{1,0:T(8,128)(2,1)}, bf16[1024,512]{1,0:T(8,128)(2,1)}, bf16[1024,512]{1,0:T(8,128)(2,1)}, f32[256,512]{1,0:T(8,128)S(1)}, bf16[...) custom-call(s32[1]{0:T(128)} %bitcast.5.core, bf16[1024,1024]{1,0:T(8,128)(2,1)S(1)} %copy-done.2, ...), custom_call_target="tpu_custom_call" | custom-call | flops 8200000000 | bytes 16777216 | tf_op jit(solution)/shard_map/pallas_call | solution.py:98
  113.8 0.7 collective-permute-start.29
  114.5 2.3 %collective-permute-done.29.came = bf16[512,1024]{1,0:T(8,128)(2,1)S(1)} collective-permute-done((bf16[512,1024]{1,0:T(8,128)(2,1)S(1)}, bf16[512,1024]{1,0:T(8,128)(2,1)S(1)}, u32[]{:S(2)}, u32[]{:S(2)}) %collective-permute-start.29) | collective-permute-done | bytes 1048608 | tf_op jit(solution)/shard_map/ppermute | solution.py:22
  116.8 1.1 shard_map.166
  117.9 8.0 %all-to-all-start = ((bf16[32,16,1024]{2,1,0:T(8,128)(2,1)}), bf16[32,16,1024]{2,1,0:T(8,128)(2,1)S(1)}, u32[]{:S(2)}, u32[]{:S(2)}) async-start(bf16[32,16,1024]{2,1,0:T(8,128)(2,1)} %bitcast.25), calls=%async_computation | async-start | bytes 2097152 | tf_op jit(solution)/shard_map/all_to_all | solution.py:430
  125.9 0.7 collective-permute-start.22
  126.6 1.2 collective-permute-done.22.came
  127.8 1.6 collective-permute-start.23
  129.4 4.4 %collective-permute-start.24 = (bf16[128,512]{1,0:T(8,128)(2,1)S(1)}, bf16[128,512]{1,0:T(8,128)(2,1)S(1)}, u32[]{:S(2)}, u32[]{:S(2)}) collective-permute-start(bf16[128,512]{1,0:T(8,128)(2,1)S(1)} %get-tuple-element.89), channel_id=1, source_target_pairs={{0,248},{8,0},{16,8},{24,16},{32,24},{40,32},{48,40},{56,48},{64,5... | collective-permute-start | bytes 393224 | tf_op jit(solution)/shard_map/ppermute | solution.py:27
  133.8 4.1 %shard_map.161.sums = f32[1024,512]{1,0:T(8,128)S(1)} custom-call(s32[1,1024]{1,0:T(1,128)S(1)} %bitcast.22, s32[1,1024]{1,0:T(1,128)S(1)} %bitcast.19, bf16[1024,512]{1,0:T(8,128)(2,1)} %get-tuple-element.84.dxs_h, bf16[1024,512]{1,0:T(8,128)(2,1)} %get-tuple-element.85.dxr_h), custom_call_target="tpu_custom_call" | custom-call | flops 2100000000 | bytes 4194304 | tf_op jit(solution)/shard_map/pallas_call | solution.py:98
  137.9 7.8 %collective-permute-done.23.low = bf16[128,512]{1,0:T(8,128)(2,1)S(1)} collective-permute-done((bf16[128,512]{1,0:T(8,128)(2,1)S(1)}, bf16[128,512]{1,0:T(8,128)(2,1)S(1)}, u32[]{:S(2)}, u32[]{:S(2)}) %collective-permute-start.23) | collective-permute-done | bytes 131104 | tf_op jit(solution)/shard_map/ppermute | solution.py:27
  145.7 0.6 shard_map.163
  146.3 2.7 %collective-permute-start.25 = (bf16[512,512]{1,0:T(8,128)(2,1)S(1)}, bf16[512,512]{1,0:T(8,128)(2,1)S(1)}, u32[]{:S(2)}, u32[]{:S(2)}) collective-permute-start(bf16[512,512]{1,0:T(8,128)(2,1)S(1)} %get-tuple-element.91), channel_id=1, source_target_pairs={{0,1},{1,0},{2,3},{3,2},{4,5},{5,4},{6,7},{7,6},{8,9},{9,8},{10,11... | collective-permute-start | bytes 1572872 | tf_op jit(solution)/shard_map/ppermute | solution.py:22
  149.1 1.3 shard_map.168
  150.8 3.3 %collective-permute-start.26 = (bf16[128,512]{1,0:T(8,128)(2,1)S(1)}, bf16[128,512]{1,0:T(8,128)(2,1)S(1)}, u32[]{:S(2)}, u32[]{:S(2)}) collective-permute-start(bf16[128,512]{1,0:T(8,128)(2,1)S(1)} %get-tuple-element.93), channel_id=1, source_target_pairs={{0,2},{1,3},{2,4},{3,5},{4,6},{5,7},{6,0},{7,1},{8,10},{9,11},{10,... | collective-permute-start | bytes 393224 | tf_op jit(solution)/shard_map/ppermute | solution.py:17
  154.2 2.1 %collective-permute-start.27 = (bf16[128,512]{1,0:T(8,128)(2,1)S(1)}, bf16[128,512]{1,0:T(8,128)(2,1)S(1)}, u32[]{:S(2)}, u32[]{:S(2)}) collective-permute-start(bf16[128,512]{1,0:T(8,128)(2,1)S(1)} %get-tuple-element.94), channel_id=1, source_target_pairs={{0,4},{1,5},{2,6},{3,7},{4,0},{5,1},{6,2},{7,3},{8,12},{9,13},{10,... | collective-permute-start | bytes 393224 | tf_op jit(solution)/shard_map/ppermute | solution.py:17
  156.2 2.6 %collective-permute-start.28 = (bf16[128,512]{1,0:T(8,128)(2,1)S(1)}, bf16[128,512]{1,0:T(8,128)(2,1)S(1)}, u32[]{:S(2)}, u32[]{:S(2)}) collective-permute-start(bf16[128,512]{1,0:T(8,128)(2,1)S(1)} %get-tuple-element.95), channel_id=1, source_target_pairs={{0,6},{1,7},{2,0},{3,1},{4,2},{5,3},{6,4},{7,5},{8,14},{9,15},{10,... | collective-permute-start | bytes 393224 | tf_op jit(solution)/shard_map/ppermute | solution.py:17
  158.9 1.0 collective-permute-start.32
  159.9 2.0 %collective-permute-start.33 = (bf16[16,1792]{1,0:T(8,128)(2,1)S(1)}, bf16[16,1792]{1,0:T(8,128)(2,1)S(1)}, u32[]{:S(2)}, u32[]{:S(2)}) collective-permute-start(bf16[16,1792]{1,0:T(8,128)(2,1)S(1)} %get-tuple-element.103), channel_id=1, source_target_pairs={{0,6},{1,7},{2,0},{3,1},{4,2},{5,3},{6,4},{7,5},{8,14},{9,15},{10,... | collective-permute-start | bytes 172040 | tf_op jit(solution)/shard_map/ppermute | solution.py:17
  161.9 8.6 %collective-permute-done.32.got2 = bf16[16,1792]{1,0:T(8,128)(2,1)S(1)} collective-permute-done((bf16[16,1792]{1,0:T(8,128)(2,1)S(1)}, bf16[16,1792]{1,0:T(8,128)(2,1)S(1)}, u32[]{:S(2)}, u32[]{:S(2)}) %collective-permute-start.32) | collective-permute-done | bytes 57376 | tf_op jit(solution)/shard_map/ppermute | solution.py:17
  170.5 1.8 %collective-permute-done.33.got3 = bf16[16,1792]{1,0:T(8,128)(2,1)S(1)} collective-permute-done((bf16[16,1792]{1,0:T(8,128)(2,1)S(1)}, bf16[16,1792]{1,0:T(8,128)(2,1)S(1)}, u32[]{:S(2)}, u32[]{:S(2)}) %collective-permute-start.33) | collective-permute-done | bytes 57376 | tf_op jit(solution)/shard_map/ppermute | solution.py:17
  172.3 0.6 collective-permute-start.34
  172.9 0.7 shard_map.165
  173.8 0.7 shard_map.170
  (57 shorter events, 3.1 us)
Async XLA Ops:
  0.6 12.6 %collective-permute-start = (bf16[128,512]{1,0:T(8,128)(2,1)}, bf16[128,512]{1,0:T(8,128)(2,1)S(1)}, u32[]{:S(2)}, u32[]{:S(2)}) collective-permute-start(bf16[128,512]{1,0:T(8,128)(2,1)} %node.1), channel_id=1, source_target_pairs={{0,6},{1,7},{2,0},{3,1},{4,2},{5,3},{6,4},{7,5},{8,14},{9,15},{10,... | collective-permute-start | bytes 393224 | tf_op jit(solution)/shard_map/ppermute | solution.py:17
  7.5 12.5 %collective-permute-start.1 = (bf16[128,512]{1,0:T(8,128)(2,1)}, bf16[128,512]{1,0:T(8,128)(2,1)S(1)}, u32[]{:S(2)}, u32[]{:S(2)}) collective-permute-start(bf16[128,512]{1,0:T(8,128)(2,1)} %node.1), channel_id=1, source_target_pairs={{0,4},{1,5},{2,6},{3,7},{4,0},{5,1},{6,2},{7,3},{8,12},{9,13},{10,... | collective-permute-start | bytes 393224 | tf_op jit(solution)/shard_map/ppermute | solution.py:17
  8.5 13.2 %collective-permute-start.2 = (bf16[128,512]{1,0:T(8,128)(2,1)}, bf16[128,512]{1,0:T(8,128)(2,1)S(1)}, u32[]{:S(2)}, u32[]{:S(2)}) collective-permute-start(bf16[128,512]{1,0:T(8,128)(2,1)} %node.1), channel_id=1, source_target_pairs={{0,2},{1,3},{2,4},{3,5},{4,6},{5,7},{6,0},{7,1},{8,10},{9,11},{10,... | collective-permute-start | bytes 393224 | tf_op jit(solution)/shard_map/ppermute | solution.py:17
  10.8 11.9 %collective-permute-start.3 = (bf16[128,512]{1,0:T(8,128)(2,1)}, bf16[128,512]{1,0:T(8,128)(2,1)S(1)}, u32[]{:S(2)}, u32[]{:S(2)}) collective-permute-start(bf16[128,512]{1,0:T(8,128)(2,1)} %node.1), channel_id=1, source_target_pairs={{0,1},{1,0},{2,3},{3,2},{4,5},{5,4},{6,7},{7,6},{8,9},{9,8},{10,11... | collective-permute-start | bytes 393224 | tf_op jit(solution)/shard_map/ppermute | solution.py:22
  13.2 9.5 %collective-permute-start.4 = (bf16[128,512]{1,0:T(8,128)(2,1)S(1)}, bf16[128,512]{1,0:T(8,128)(2,1)S(1)}, u32[]{:S(2)}, u32[]{:S(2)}) collective-permute-start(bf16[128,512]{1,0:T(8,128)(2,1)S(1)} %collective-permute-done.refs_0_), channel_id=1, source_target_pairs={{0,1},{1,0},{2,3},{3,2},{4,5},{5,4},{6,7},{7,6},{8,9},{9,8},{10,11... | collective-permute-start | bytes 393224 | tf_op jit(solution)/shard_map/ppermute | solution.py:22
  20.0 2.7 %collective-permute-start.5 = (bf16[128,512]{1,0:T(8,128)(2,1)S(1)}, bf16[128,512]{1,0:T(8,128)(2,1)S(1)}, u32[]{:S(2)}, u32[]{:S(2)}) collective-permute-start(bf16[128,512]{1,0:T(8,128)(2,1)S(1)} %collective-permute-done.1.refs_1_), channel_id=1, source_target_pairs={{0,1},{1,0},{2,3},{3,2},{4,5},{5,4},{6,7},{7,6},{8,9},{9,8},{10,11... | collective-permute-start | bytes 393224 | tf_op jit(solution)/shard_map/ppermute | solution.py:22
  21.7 1.3 collective-permute-start.6
  24.4 8.4 %collective-permute-start.9 = (bf16[128,512]{1,0:T(8,128)(2,1)S(1)}, bf16[128,512]{1,0:T(8,128)(2,1)S(1)}, u32[]{:S(2)}, u32[]{:S(2)}) collective-permute-start(bf16[128,512]{1,0:T(8,128)(2,1)S(1)} %get-tuple-element.66), channel_id=1, source_target_pairs={{0,248},{8,0},{16,8},{24,16},{32,24},{40,32},{48,40},{56,48},{64,5... | collective-permute-start | bytes 393224 | tf_op jit(solution)/shard_map/ppermute | solution.py:27
  30.4 8.6 %collective-permute-start.7 = (bf16[128,512]{1,0:T(8,128)(2,1)S(1)}, bf16[128,512]{1,0:T(8,128)(2,1)S(1)}, u32[]{:S(2)}, u32[]{:S(2)}) collective-permute-start(bf16[128,512]{1,0:T(8,128)(2,1)S(1)} %get-tuple-element.65), channel_id=1, source_target_pairs={{0,8},{8,16},{16,24},{24,32},{32,40},{40,48},{48,56},{56,64},{64,7... | collective-permute-start | bytes 393224 | tf_op jit(solution)/shard_map/ppermute | solution.py:27
  32.9 12.6 %collective-permute-start.10 = (bf16[128,512]{1,0:T(8,128)(2,1)S(1)}, bf16[128,512]{1,0:T(8,128)(2,1)S(1)}, u32[]{:S(2)}, u32[]{:S(2)}) collective-permute-start(bf16[128,512]{1,0:T(8,128)(2,1)S(1)} %collective-permute-done.9.refs_2_), channel_id=1, source_target_pairs={{0,1},{1,0},{2,3},{3,2},{4,5},{5,4},{6,7},{7,6},{8,9},{9,8},{10,11... | collective-permute-start | bytes 393224 | tf_op jit(solution)/shard_map/ppermute | solution.py:22
  39.0 6.4 %copy-start.8 = (bf16[128,512]{1,0:T(8,128)(2,1)}, bf16[128,512]{1,0:T(8,128)(2,1)S(1)}, u32[]{:S(2)}) copy-start(bf16[128,512]{1,0:T(8,128)(2,1)S(1)} %collective-permute-done.7.refs_0_) | copy-start | bytes 393220
  39.0 6.5 %collective-permute-start.8 = (bf16[128,512]{1,0:T(8,128)(2,1)S(1)}, bf16[128,512]{1,0:T(8,128)(2,1)S(1)}, u32[]{:S(2)}, u32[]{:S(2)}) collective-permute-start(bf16[128,512]{1,0:T(8,128)(2,1)S(1)} %collective-permute-done.7.refs_0_), channel_id=1, source_target_pairs={{0,1},{1,0},{2,3},{3,2},{4,5},{5,4},{6,7},{7,6},{8,9},{9,8},{10,11... | collective-permute-start | bytes 393224 | tf_op jit(solution)/shard_map/ppermute | solution.py:22
  45.5 0.9 copy-start.9
  46.4 25.1 %copy-start = (bf16[128,512]{1,0:T(8,128)(2,1)S(1)}, bf16[128,512]{1,0:T(8,128)(2,1)}, u32[]{:S(2)}) copy-start(bf16[128,512]{1,0:T(8,128)(2,1)} %node.1) | copy-start | bytes 393220
  46.4 25.1 %copy-start.5 = (bf16[1024,512]{1,0:T(8,128)(2,1)S(1)}, bf16[1024,512]{1,0:T(8,128)(2,1)}, u32[]{:S(2)}) copy-start(bf16[1024,512]{1,0:T(8,128)(2,1)} %w1.1) | copy-start | bytes 3145732
  46.4 25.1 %copy-start.6 = (bf16[512,512]{1,0:T(8,128)(2,1)S(1)}, bf16[512,512]{1,0:T(8,128)(2,1)}, u32[]{:S(2)}) copy-start(bf16[512,512]{1,0:T(8,128)(2,1)} %w2.1) | copy-start | bytes 1572868
  46.4 25.1 %copy-start.7 = (bf16[128,512]{1,0:T(8,128)(2,1)S(1)}, bf16[128,512]{1,0:T(8,128)(2,1)}, u32[]{:S(2)}) copy-start(bf16[128,512]{1,0:T(8,128)(2,1)} %grad.1) | copy-start | bytes 393220
  50.9 2.2 %collective-permute-start.11 = (bf16[512,512]{1,0:T(8,128)(2,1)S(1)}, bf16[512,512]{1,0:T(8,128)(2,1)S(1)}, u32[]{:S(2)}, u32[]{:S(2)}) collective-permute-start(bf16[512,512]{1,0:T(8,128)(2,1)S(1)} %get-tuple-element.76), channel_id=1, source_target_pairs={{0,1},{1,0},{2,3},{3,2},{4,5},{5,4},{6,7},{7,6},{8,9},{9,8},{10,11... | collective-permute-start | bytes 1572872 | tf_op jit(solution)/shard_map/ppermute | solution.py:22
  53.2 10.2 %collective-permute-start.12 = (bf16[128,512]{1,0:T(8,128)(2,1)S(1)}, bf16[128,512]{1,0:T(8,128)(2,1)S(1)}, u32[]{:S(2)}, u32[]{:S(2)}) collective-permute-start(bf16[128,512]{1,0:T(8,128)(2,1)S(1)} %get-tuple-element.78), channel_id=1, source_target_pairs={{0,2},{1,3},{2,4},{3,5},{4,6},{5,7},{6,0},{7,1},{8,10},{9,11},{10,... | collective-permute-start | bytes 393224 | tf_op jit(solution)/shard_map/ppermute | solution.py:17
  55.1 16.4 %collective-permute-start.13 = (bf16[128,512]{1,0:T(8,128)(2,1)S(1)}, bf16[128,512]{1,0:T(8,128)(2,1)S(1)}, u32[]{:S(2)}, u32[]{:S(2)}) collective-permute-start(bf16[128,512]{1,0:T(8,128)(2,1)S(1)} %get-tuple-element.79), channel_id=1, source_target_pairs={{0,4},{1,5},{2,6},{3,7},{4,0},{5,1},{6,2},{7,3},{8,12},{9,13},{10,... | collective-permute-start | bytes 393224 | tf_op jit(solution)/shard_map/ppermute | solution.py:17
  59.2 12.3 %collective-permute-start.14 = (bf16[128,512]{1,0:T(8,128)(2,1)S(1)}, bf16[128,512]{1,0:T(8,128)(2,1)S(1)}, u32[]{:S(2)}, u32[]{:S(2)}) collective-permute-start(bf16[128,512]{1,0:T(8,128)(2,1)S(1)} %get-tuple-element.80), channel_id=1, source_target_pairs={{0,6},{1,7},{2,0},{3,1},{4,2},{5,3},{6,4},{7,5},{8,14},{9,15},{10,... | collective-permute-start | bytes 393224 | tf_op jit(solution)/shard_map/ppermute | solution.py:17
  73.3 19.2 %collective-permute-start.30 = (bf16[512,768]{1,0:T(8,128)(2,1)S(1)}, bf16[512,768]{1,0:T(8,128)(2,1)S(1)}, u32[]{:S(2)}, u32[]{:S(2)}) collective-permute-start(bf16[512,768]{1,0:T(8,128)(2,1)S(1)} %get-tuple-element.101), channel_id=1, source_target_pairs={{0,1},{1,0},{2,3},{3,2},{4,5},{5,4},{6,7},{7,6},{8,9},{9,8},{10,11... | collective-permute-start | bytes 2359304 | tf_op jit(solution)/shard_map/ppermute | solution.py:22
  73.9 9.8 %collective-permute-start.15 = (bf16[128,512]{1,0:T(8,128)(2,1)S(1)}, bf16[128,512]{1,0:T(8,128)(2,1)S(1)}, u32[]{:S(2)}, u32[]{:S(2)}) collective-permute-start(bf16[128,512]{1,0:T(8,128)(2,1)S(1)} %get-tuple-element.81.refs_0_), channel_id=1, source_target_pairs={{0,6},{1,7},{2,0},{3,1},{4,2},{5,3},{6,4},{7,5},{8,14},{9,15},{10,... | collective-permute-start | bytes 393224 | tf_op jit(solution)/shard_map/ppermute | solution.py:17
  75.7 14.6 %collective-permute-start.16 = (bf16[128,512]{1,0:T(8,128)(2,1)S(1)}, bf16[128,512]{1,0:T(8,128)(2,1)S(1)}, u32[]{:S(2)}, u32[]{:S(2)}) collective-permute-start(bf16[128,512]{1,0:T(8,128)(2,1)S(1)} %get-tuple-element.81.refs_0_), channel_id=1, source_target_pairs={{0,4},{1,5},{2,6},{3,7},{4,0},{5,1},{6,2},{7,3},{8,12},{9,13},{10,... | collective-permute-start | bytes 393224 | tf_op jit(solution)/shard_map/ppermute | solution.py:17
  77.2 13.7 %collective-permute-start.17 = (bf16[128,512]{1,0:T(8,128)(2,1)S(1)}, bf16[128,512]{1,0:T(8,128)(2,1)S(1)}, u32[]{:S(2)}, u32[]{:S(2)}) collective-permute-start(bf16[128,512]{1,0:T(8,128)(2,1)S(1)} %get-tuple-element.81.refs_0_), channel_id=1, source_target_pairs={{0,2},{1,3},{2,4},{3,5},{4,6},{5,7},{6,0},{7,1},{8,10},{9,11},{10,... | collective-permute-start | bytes 393224 | tf_op jit(solution)/shard_map/ppermute | solution.py:17
  79.5 19.8 %collective-permute-start.18 = (bf16[128,512]{1,0:T(8,128)(2,1)S(1)}, bf16[128,512]{1,0:T(8,128)(2,1)S(1)}, u32[]{:S(2)}, u32[]{:S(2)}) collective-permute-start(bf16[128,512]{1,0:T(8,128)(2,1)S(1)} %get-tuple-element.81.refs_0_), channel_id=1, source_target_pairs={{0,1},{1,0},{2,3},{3,2},{4,5},{5,4},{6,7},{7,6},{8,9},{9,8},{10,11... | collective-permute-start | bytes 393224 | tf_op jit(solution)/shard_map/ppermute | solution.py:22
  83.6 15.7 %collective-permute-start.19 = (bf16[128,512]{1,0:T(8,128)(2,1)S(1)}, bf16[128,512]{1,0:T(8,128)(2,1)}, u32[]{:S(2)}, u32[]{:S(2)}) collective-permute-start(bf16[128,512]{1,0:T(8,128)(2,1)S(1)} %collective-permute-done.15.refs_1_), channel_id=1, source_target_pairs={{0,1},{1,0},{2,3},{3,2},{4,5},{5,4},{6,7},{7,6},{8,9},{9,8},{10,11... | collective-permute-start | bytes 393224 | tf_op jit(solution)/shard_map/ppermute | solution.py:22
  90.4 9.0 %collective-permute-start.20 = (bf16[128,512]{1,0:T(8,128)(2,1)S(1)}, bf16[128,512]{1,0:T(8,128)(2,1)}, u32[]{:S(2)}, u32[]{:S(2)}) collective-permute-start(bf16[128,512]{1,0:T(8,128)(2,1)S(1)} %collective-permute-done.16.refs_2_), channel_id=1, source_target_pairs={{0,1},{1,0},{2,3},{3,2},{4,5},{5,4},{6,7},{7,6},{8,9},{9,8},{10,11... | collective-permute-start | bytes 393224 | tf_op jit(solution)/shard_map/ppermute | solution.py:22
  90.9 8.4 %collective-permute-start.21 = (bf16[128,512]{1,0:T(8,128)(2,1)S(1)}, bf16[128,512]{1,0:T(8,128)(2,1)}, u32[]{:S(2)}, u32[]{:S(2)}) collective-permute-start(bf16[128,512]{1,0:T(8,128)(2,1)S(1)} %collective-permute-done.17.refs_3_), channel_id=1, source_target_pairs={{0,1},{1,0},{2,3},{3,2},{4,5},{5,4},{6,7},{7,6},{8,9},{9,8},{10,11... | collective-permute-start | bytes 393224 | tf_op jit(solution)/shard_map/ppermute | solution.py:22
  92.5 1.6 copy-start.1
  92.5 2.1 %copy-start.3 = (bf16[1536,512]{1,0:T(8,128)(2,1)}, bf16[1536,512]{1,0:T(8,128)(2,1)S(1)}, u32[]{:S(2)}) copy-start(bf16[1536,512]{1,0:T(8,128)(2,1)S(1)} %get-tuple-element.82.refs_8_) | copy-start | bytes 4718596
  94.6 23.4 %all-to-all-start.1 = ((bf16[32,16,768]{2,1,0:T(8,128)(2,1)}), bf16[32,16,768]{2,1,0:T(8,128)(2,1)}, u32[]{:S(2)}, u32[]{:S(2)}) async-start(bf16[32,16,768]{2,1,0:T(8,128)(2,1)} %bitcast.26), calls=%async_computation.1 | async-start | bytes 1572864 | tf_op jit(solution)/shard_map/all_to_all | solution.py:430
  99.3 0.7 copy-start.10
  100.0 1.6 copy-start.2
  101.5 1.4 copy-start.4
  113.8 3.0 %collective-permute-start.29 = (bf16[512,1024]{1,0:T(8,128)(2,1)S(1)}, bf16[512,1024]{1,0:T(8,128)(2,1)S(1)}, u32[]{:S(2)}, u32[]{:S(2)}) collective-permute-start(bf16[512,1024]{1,0:T(8,128)(2,1)S(1)} %get-tuple-element.99), channel_id=1, source_target_pairs={{0,1},{1,0},{2,3},{3,2},{4,5},{5,4},{6,7},{7,6},{8,9},{9,8},{10,11... | collective-permute-start | bytes 3145736 | tf_op jit(solution)/shard_map/ppermute | solution.py:22
  117.9 31.1 %all-to-all-start = ((bf16[32,16,1024]{2,1,0:T(8,128)(2,1)}), bf16[32,16,1024]{2,1,0:T(8,128)(2,1)S(1)}, u32[]{:S(2)}, u32[]{:S(2)}) async-start(bf16[32,16,1024]{2,1,0:T(8,128)(2,1)} %bitcast.25), calls=%async_computation | async-start | bytes 2097152 | tf_op jit(solution)/shard_map/all_to_all | solution.py:430
  125.9 1.9 %collective-permute-start.22 = (bf16[256,512]{1,0:T(8,128)(2,1)S(1)}, bf16[256,512]{1,0:T(8,128)(2,1)S(1)}, u32[]{:S(2)}, u32[]{:S(2)}) collective-permute-start(bf16[256,512]{1,0:T(8,128)(2,1)S(1)} %get-tuple-element.87), channel_id=1, source_target_pairs={{0,1},{1,0},{2,3},{3,2},{4,5},{5,4},{6,7},{7,6},{8,9},{9,8},{10,11... | collective-permute-start | bytes 786440 | tf_op jit(solution)/shard_map/ppermute | solution.py:22
  127.8 17.9 %collective-permute-start.23 = (bf16[128,512]{1,0:T(8,128)(2,1)S(1)}, bf16[128,512]{1,0:T(8,128)(2,1)S(1)}, u32[]{:S(2)}, u32[]{:S(2)}) collective-permute-start(bf16[128,512]{1,0:T(8,128)(2,1)S(1)} %get-tuple-element.88), channel_id=1, source_target_pairs={{0,8},{8,16},{16,24},{24,32},{32,40},{40,48},{48,56},{56,64},{64,7... | collective-permute-start | bytes 393224 | tf_op jit(solution)/shard_map/ppermute | solution.py:27
  129.4 16.3 %collective-permute-start.24 = (bf16[128,512]{1,0:T(8,128)(2,1)S(1)}, bf16[128,512]{1,0:T(8,128)(2,1)S(1)}, u32[]{:S(2)}, u32[]{:S(2)}) collective-permute-start(bf16[128,512]{1,0:T(8,128)(2,1)S(1)} %get-tuple-element.89), channel_id=1, source_target_pairs={{0,248},{8,0},{16,8},{24,16},{32,24},{40,32},{48,40},{56,48},{64,5... | collective-permute-start | bytes 393224 | tf_op jit(solution)/shard_map/ppermute | solution.py:27
  146.3 4.4 %collective-permute-start.25 = (bf16[512,512]{1,0:T(8,128)(2,1)S(1)}, bf16[512,512]{1,0:T(8,128)(2,1)S(1)}, u32[]{:S(2)}, u32[]{:S(2)}) collective-permute-start(bf16[512,512]{1,0:T(8,128)(2,1)S(1)} %get-tuple-element.91), channel_id=1, source_target_pairs={{0,1},{1,0},{2,3},{3,2},{4,5},{5,4},{6,7},{7,6},{8,9},{9,8},{10,11... | collective-permute-start | bytes 1572872 | tf_op jit(solution)/shard_map/ppermute | solution.py:22
  150.3 9.6 %collective-permute-start.31 = (bf16[16,1792]{1,0:T(8,128)(2,1)S(1)}, bf16[16,1792]{1,0:T(8,128)(2,1)S(1)}, u32[]{:S(2)}, u32[]{:S(2)}) collective-permute-start(bf16[16,1792]{1,0:T(8,128)(2,1)S(1)} %get-tuple-element.103), channel_id=1, source_target_pairs={{0,2},{1,3},{2,4},{3,5},{4,6},{5,7},{6,0},{7,1},{8,10},{9,11},{10,... | collective-permute-start | bytes 172040 | tf_op jit(solution)/shard_map/ppermute | solution.py:17
  150.8 22.1 %collective-permute-start.26 = (bf16[128,512]{1,0:T(8,128)(2,1)S(1)}, bf16[128,512]{1,0:T(8,128)(2,1)S(1)}, u32[]{:S(2)}, u32[]{:S(2)}) collective-permute-start(bf16[128,512]{1,0:T(8,128)(2,1)S(1)} %get-tuple-element.93), channel_id=1, source_target_pairs={{0,2},{1,3},{2,4},{3,5},{4,6},{5,7},{6,0},{7,1},{8,10},{9,11},{10,... | collective-permute-start | bytes 393224 | tf_op jit(solution)/shard_map/ppermute | solution.py:17
  154.2 18.7 %collective-permute-start.27 = (bf16[128,512]{1,0:T(8,128)(2,1)S(1)}, bf16[128,512]{1,0:T(8,128)(2,1)S(1)}, u32[]{:S(2)}, u32[]{:S(2)}) collective-permute-start(bf16[128,512]{1,0:T(8,128)(2,1)S(1)} %get-tuple-element.94), channel_id=1, source_target_pairs={{0,4},{1,5},{2,6},{3,7},{4,0},{5,1},{6,2},{7,3},{8,12},{9,13},{10,... | collective-permute-start | bytes 393224 | tf_op jit(solution)/shard_map/ppermute | solution.py:17
  156.2 16.7 %collective-permute-start.28 = (bf16[128,512]{1,0:T(8,128)(2,1)S(1)}, bf16[128,512]{1,0:T(8,128)(2,1)S(1)}, u32[]{:S(2)}, u32[]{:S(2)}) collective-permute-start(bf16[128,512]{1,0:T(8,128)(2,1)S(1)} %get-tuple-element.95), channel_id=1, source_target_pairs={{0,6},{1,7},{2,0},{3,1},{4,2},{5,3},{6,4},{7,5},{8,14},{9,15},{10,... | collective-permute-start | bytes 393224 | tf_op jit(solution)/shard_map/ppermute | solution.py:17
  158.9 11.6 %collective-permute-start.32 = (bf16[16,1792]{1,0:T(8,128)(2,1)S(1)}, bf16[16,1792]{1,0:T(8,128)(2,1)S(1)}, u32[]{:S(2)}, u32[]{:S(2)}) collective-permute-start(bf16[16,1792]{1,0:T(8,128)(2,1)S(1)} %get-tuple-element.103), channel_id=1, source_target_pairs={{0,4},{1,5},{2,6},{3,7},{4,0},{5,1},{6,2},{7,3},{8,12},{9,13},{10,... | collective-permute-start | bytes 172040 | tf_op jit(solution)/shard_map/ppermute | solution.py:17
  159.9 12.4 %collective-permute-start.33 = (bf16[16,1792]{1,0:T(8,128)(2,1)S(1)}, bf16[16,1792]{1,0:T(8,128)(2,1)S(1)}, u32[]{:S(2)}, u32[]{:S(2)}) collective-permute-start(bf16[16,1792]{1,0:T(8,128)(2,1)S(1)} %get-tuple-element.103), channel_id=1, source_target_pairs={{0,6},{1,7},{2,0},{3,1},{4,2},{5,3},{6,4},{7,5},{8,14},{9,15},{10,... | collective-permute-start | bytes 172040 | tf_op jit(solution)/shard_map/ppermute | solution.py:17
  172.3 1.5 collective-permute-start.34

commit v5 on v4

--- a/solution.py
+++ b/solution.py
@@ -354,15 +354,17 @@
     lax.fori_loop(0, 4, finish, 0)
 
 
-def blocks_total_kernel(edge, node_h, sum_o, send_o, node, sem):
-    got_n = begin(node_h, node, sem.at[0])
+def node_blocks_kernel(node_h, out, node, sem):
+    begin(node_h, node, sem.at[0]).wait()
+    out[...] = jnp.sum(node[...].astype(F32), axis=0)
+
+
+def blocks_total_kernel(edge, node_part, sum_o, send_o):
     edge_part = jnp.sum(edge[...].astype(F32), axis=0)
     sum_o[:, pl.ds(0, 1024)] = edge_part
     send_o[:, pl.ds(0, 1024)] = edge_part.astype(BF16)
-    got_n.wait()
-    node_part = jnp.sum(node[...].astype(F32), axis=0)
-    sum_o[:, pl.ds(1024, 768)] = node_part
-    send_o[:, pl.ds(1024, 768)] = node_part.astype(BF16)
+    sum_o[:, pl.ds(1024, 768)] = node_part[...]
+    send_o[:, pl.ds(1024, 768)] = node_part[...].astype(BF16)
 
 
 def ring_total_kernel(own, got1, got2, got3, sum_o, send_o):
@@ -648,14 +650,21 @@
         vmem=8 * MIB,
     )
 
+    (node_sum,) = call(
+        node_blocks_kernel,
+        [shape((16, 768), F32)],
+        [node_blocks],
+        far=(0,),
+        scratch=[pltpu.VMEM((32, 16, 768), BF16), pltpu.SemaphoreType.DMA((1,))],
+        moved=MIB,
+        vmem=4 * MIB,
+    )
     w_rows, w_out = call(
         blocks_total_kernel,
         [shape((16, 1792), F32), shape((16, 1792), BF16)],
-        [edge_blocks, node_blocks],
-        far=(1,),
-        scratch=[pltpu.VMEM((32, 16, 768), BF16), pltpu.SemaphoreType.DMA((1,))],
-        moved=2 * MIB,
-        vmem=8 * MIB,
+        [edge_blocks, node_sum],
+        moved=MIB,
+        vmem=4 * MIB,
     )
     w_rows, w_out = call(
         ring_total_kernel,

time: 175 us -> 175 us (level)
    pallas_call x17 -> x18, Pallas kernels: 34.8 us -> 35 us  [call(): pl.pallas_call(kernel, out_shape=out_shapes, in_specs=in_specs, out_specs...]
where the time goes in v5:
time: 175 us
  starting transfers between devices  82.2 us (47%)
  waiting for transfers between devices  48.4 us (28%)
  Pallas kernels  35 us (20%)
  local copies, waits for them, and re-layouts  6.07 us (3%)
  other arithmetic  2.09 us (1%)
    ppermute x15, starting transfers between devices, over_ring(): lax.ppermute(x, 'shard', [(i, (i + 2 * by) % count) for i in range(count)])  36 us
    pallas_call x18, Pallas kernels, call(): pl.pallas_call(kernel, out_shape=out_shapes, in_specs=in_specs, out_specs...  35 us
    ppermute x15, waiting for transfers between devices, over_ring(): lax.ppermute(x, 'shard', [(i, (i + 2 * by) % count) for i in range(count)])  29 us
    ppermute x16, starting transfers between devices, to_partner(): return lax.ppermute(x, 'shard', [(i, i ^ 1) for i in range(count)])  21.6 us
    ppermute x4, waiting for transfers between devices, to_patch(): lax.ppermute(x, 'patch', [(i, (i + by) % count) for i in range(count)])  13.5 us
    all_to_all x2, starting transfers between devices, weight_sum(): lax.all_to_all(both.reshape(patches, units // patches, lanes), 'patch', 0...  12.7 us
    ppermute x4, starting transfers between devices, to_patch(): lax.ppermute(x, 'patch', [(i, (i + by) % count) for i in range(count)])  11.9 us
    ppermute x16, waiting for transfers between devices, to_partner(): return lax.ppermute(x, 'shard', [(i, i ^ 1) for i in range(count)])  5.92 us
  transfers between devices with their start and end apart: 37, of which 14 were waited for; matrix products, arithmetic and copies ran while one was open for 2% of the time, Pallas kernels for 15%

profile of v5, /device:TPU:1, one launch (start us, length us, event | category | flops | bytes accessed | tf_op | source)
XLA Modules:
  0.0 174.7 jit_solution(12681790980836426732)
XLA Ops:
  0.6 6.9 %collective-permute-start = (bf16[128,512]{1,0:T(8,128)(2,1)}, bf16[128,512]{1,0:T(8,128)(2,1)S(1)}, u32[]{:S(2)}, u32[]{:S(2)}) collective-permute-start(bf16[128,512]{1,0:T(8,128)(2,1)} %node.1), channel_id=1, source_target_pairs={{0,6},{1,7},{2,0},{3,1},{4,2},{5,3},{6,4},{7,5},{8,14},{9,15},{10,... | collective-permute-start | bytes 393224 | tf_op jit(solution)/shard_map/ppermute | solution.py:17
  7.5 1.0 collective-permute-start.1
  8.5 2.3 %collective-permute-start.2 = (bf16[128,512]{1,0:T(8,128)(2,1)}, bf16[128,512]{1,0:T(8,128)(2,1)S(1)}, u32[]{:S(2)}, u32[]{:S(2)}) collective-permute-start(bf16[128,512]{1,0:T(8,128)(2,1)} %node.1), channel_id=1, source_target_pairs={{0,2},{1,3},{2,4},{3,5},{4,6},{5,7},{6,0},{7,1},{8,10},{9,11},{10,... | collective-permute-start | bytes 393224 | tf_op jit(solution)/shard_map/ppermute | solution.py:17
  10.8 1.5 collective-permute-start.3
  12.3 0.7 add_add_fusion
  13.2 6.8 %collective-permute-start.4 = (bf16[128,512]{1,0:T(8,128)(2,1)S(1)}, bf16[128,512]{1,0:T(8,128)(2,1)S(1)}, u32[]{:S(2)}, u32[]{:S(2)}) collective-permute-start(bf16[128,512]{1,0:T(8,128)(2,1)S(1)} %collective-permute-done.refs_0_), channel_id=1, source_target_pairs={{0,1},{1,0},{2,3},{3,2},{4,5},{5,4},{6,7},{7,6},{8,9},{9,8},{10,11... | collective-permute-start | bytes 393224 | tf_op jit(solution)/shard_map/ppermute | solution.py:22
  20.0 1.7 collective-permute-start.5
  21.7 0.7 and_add_fusion
  23.1 1.4 shard_map.155
  24.4 5.9 %collective-permute-start.9 = (bf16[128,512]{1,0:T(8,128)(2,1)S(1)}, bf16[128,512]{1,0:T(8,128)(2,1)S(1)}, u32[]{:S(2)}, u32[]{:S(2)}) collective-permute-start(bf16[128,512]{1,0:T(8,128)(2,1)S(1)} %get-tuple-element.66), channel_id=1, source_target_pairs={{0,248},{8,0},{16,8},{24,16},{32,24},{40,32},{48,40},{56,48},{64,5... | collective-permute-start | bytes 393224 | tf_op jit(solution)/shard_map/ppermute | solution.py:27
  30.4 0.7 select_select_fusion
  31.3 1.6 collective-permute-done.9.refs_2_
  32.9 2.0 %collective-permute-start.10 = (bf16[128,512]{1,0:T(8,128)(2,1)S(1)}, bf16[128,512]{1,0:T(8,128)(2,1)S(1)}, u32[]{:S(2)}, u32[]{:S(2)}) collective-permute-start(bf16[128,512]{1,0:T(8,128)(2,1)S(1)} %collective-permute-done.9.refs_2_), channel_id=1, source_target_pairs={{0,1},{1,0},{2,3},{3,2},{4,5},{5,4},{6,7},{7,6},{8,9},{9,8},{10,11... | collective-permute-start | bytes 393224 | tf_op jit(solution)/shard_map/ppermute | solution.py:22
  34.9 4.1 %collective-permute-done.7.refs_0_ = bf16[128,512]{1,0:T(8,128)(2,1)S(1)} collective-permute-done((bf16[128,512]{1,0:T(8,128)(2,1)S(1)}, bf16[128,512]{1,0:T(8,128)(2,1)S(1)}, u32[]{:S(2)}, u32[]{:S(2)}) %collective-permute-start.7) | collective-permute-done | bytes 131104 | tf_op jit(solution)/shard_map/ppermute | solution.py:27
  39.0 1.5 collective-permute-start.8
  40.5 4.9 %shard_map.156 = (bf16[1024,512]{1,0:T(8,128)(2,1)S(1)}, bf16[1024,512]{1,0:T(8,128)(2,1)}, f32[1024,512]{1,0:T(8,128)S(1)}, bf16[1024,512]{1,0:T(8,128)(2,1)S(1...) custom-call(s32[1024,1]{1,0:T(8,128)S(1)} %copy.19.s_col, ...), custom_call_target="tpu_custom_call" | custom-call | flops 3800000000 | bytes 8388608 | tf_op jit(solution)/shard_map/pallas_call | solution.py:98
  45.5 0.9 copy-done.9
  46.4 4.5 %shard_map.157 = (bf16[1024,512]{1,0:T(8,128)(2,1)}, bf16[1024,512]{1,0:T(8,128)(2,1)}, f32[1024,512]{1,0:T(8,128)}, f32[1024,512]{1,0:T(8,128)}, f32[1024,1]{1,...) custom-call(bf16[1024,512]{1,0:T(8,128)(2,1)S(1)} %get-tuple-element.60.halo_mask, ...), custom_call_target="tpu_custom_call" | custom-call | flops 2700000000 | bytes 12582912 | tf_op jit(solution)/shard_map/pallas_call | solution.py:98
  51.2 1.9 %collective-permute-done.11.came = bf16[512,512]{1,0:T(8,128)(2,1)S(1)} collective-permute-done((bf16[512,512]{1,0:T(8,128)(2,1)S(1)}, bf16[512,512]{1,0:T(8,128)(2,1)S(1)}, u32[]{:S(2)}, u32[]{:S(2)}) %collective-permute-start.11) | collective-permute-done | bytes 524320 | tf_op jit(solution)/shard_map/ppermute | solution.py:22
  53.2 1.9 %collective-permute-start.12 = (bf16[128,512]{1,0:T(8,128)(2,1)S(1)}, bf16[128,512]{1,0:T(8,128)(2,1)S(1)}, u32[]{:S(2)}, u32[]{:S(2)}) collective-permute-start(bf16[128,512]{1,0:T(8,128)(2,1)S(1)} %get-tuple-element.78), channel_id=1, source_target_pairs={{0,2},{1,3},{2,4},{3,5},{4,6},{5,7},{6,0},{7,1},{8,10},{9,11},{10,... | collective-permute-start | bytes 393224 | tf_op jit(solution)/shard_map/ppermute | solution.py:17
  55.1 4.1 %collective-permute-start.13 = (bf16[128,512]{1,0:T(8,128)(2,1)S(1)}, bf16[128,512]{1,0:T(8,128)(2,1)S(1)}, u32[]{:S(2)}, u32[]{:S(2)}) collective-permute-start(bf16[128,512]{1,0:T(8,128)(2,1)S(1)} %get-tuple-element.79), channel_id=1, source_target_pairs={{0,4},{1,5},{2,6},{3,7},{4,0},{5,1},{6,2},{7,3},{8,12},{9,13},{10,... | collective-permute-start | bytes 393224 | tf_op jit(solution)/shard_map/ppermute | solution.py:17
  59.2 2.8 %collective-permute-start.14 = (bf16[128,512]{1,0:T(8,128)(2,1)S(1)}, bf16[128,512]{1,0:T(8,128)(2,1)S(1)}, u32[]{:S(2)}, u32[]{:S(2)}) collective-permute-start(bf16[128,512]{1,0:T(8,128)(2,1)S(1)} %get-tuple-element.80), channel_id=1, source_target_pairs={{0,6},{1,7},{2,0},{3,1},{4,2},{5,3},{6,4},{7,5},{8,14},{9,15},{10,... | collective-permute-start | bytes 393224 | tf_op jit(solution)/shard_map/ppermute | solution.py:17
  61.9 1.5 collective-permute-done.12.got1
  63.4 8.1 %collective-permute-done.13.got2 = bf16[128,512]{1,0:T(8,128)(2,1)S(1)} collective-permute-done((bf16[128,512]{1,0:T(8,128)(2,1)S(1)}, bf16[128,512]{1,0:T(8,128)(2,1)S(1)}, u32[]{:S(2)}, u32[]{:S(2)}) %collective-permute-start.13) | collective-permute-done | bytes 131104 | tf_op jit(solution)/shard_map/ppermute | solution.py:17
  71.5 1.8 %shard_map.159 = (bf16[128,512]{1,0:T(8,128)(2,1)S(1)}, f32[128,512]{1,0:T(8,128)S(1)}, f32[512,768]{1,0:T(8,128)S(1)}, bf16[512,768]{1,0:T(8,128)(2,1)S(1)}) custom-call(s32[1]{0:T(128)} %bitcast.5.core, f32[128,512]{1,0:T(8,128)S(1)} %get-tuple-element.77.own, bf16[128,512]{1,0:T(8,128)(2,1)S(1)} %collective-permute-done.12.got1, ...), custom_call_target="tpu_custom_call" | custom-call | flops 800000000 | bytes 5242880 | tf_op jit(solution)/shard_map/pallas_call | solution.py:98
  73.3 0.5 collective-permute-start.30
  73.9 1.9 %collective-permute-start.15 = (bf16[128,512]{1,0:T(8,128)(2,1)S(1)}, bf16[128,512]{1,0:T(8,128)(2,1)S(1)}, u32[]{:S(2)}, u32[]{:S(2)}) collective-permute-start(bf16[128,512]{1,0:T(8,128)(2,1)S(1)} %get-tuple-element.81.refs_0_), channel_id=1, source_target_pairs={{0,6},{1,7},{2,0},{3,1},{4,2},{5,3},{6,4},{7,5},{8,14},{9,15},{10,... | collective-permute-start | bytes 393224 | tf_op jit(solution)/shard_map/ppermute | solution.py:17
  75.7 1.5 collective-permute-start.16
  77.2 2.3 %collective-permute-start.17 = (bf16[128,512]{1,0:T(8,128)(2,1)S(1)}, bf16[128,512]{1,0:T(8,128)(2,1)S(1)}, u32[]{:S(2)}, u32[]{:S(2)}) collective-permute-start(bf16[128,512]{1,0:T(8,128)(2,1)S(1)} %get-tuple-element.81.refs_0_), channel_id=1, source_target_pairs={{0,2},{1,3},{2,4},{3,5},{4,6},{5,7},{6,0},{7,1},{8,10},{9,11},{10,... | collective-permute-start | bytes 393224 | tf_op jit(solution)/shard_map/ppermute | solution.py:17
  79.5 0.9 collective-permute-start.18
  80.4 3.2 %collective-permute-done.15.refs_1_ = bf16[128,512]{1,0:T(8,128)(2,1)S(1)} collective-permute-done((bf16[128,512]{1,0:T(8,128)(2,1)S(1)}, bf16[128,512]{1,0:T(8,128)(2,1)S(1)}, u32[]{:S(2)}, u32[]{:S(2)}) %collective-permute-start.15) | collective-permute-done | bytes 131104 | tf_op jit(solution)/shard_map/ppermute | solution.py:17
  83.6 0.9 collective-permute-start.19
  84.6 5.8 %collective-permute-done.16.refs_2_ = bf16[128,512]{1,0:T(8,128)(2,1)S(1)} collective-permute-done((bf16[128,512]{1,0:T(8,128)(2,1)S(1)}, bf16[128,512]{1,0:T(8,128)(2,1)S(1)}, u32[]{:S(2)}, u32[]{:S(2)}) %collective-permute-start.16) | collective-permute-done | bytes 131104 | tf_op jit(solution)/shard_map/ppermute | solution.py:17
  90.4 0.6 collective-permute-start.20
  90.9 1.5 shard_map.154
  92.5 1.1 shard_map.167
  94.6 4.7 %all-to-all-start.1 = ((bf16[32,16,768]{2,1,0:T(8,128)(2,1)}), bf16[32,16,768]{2,1,0:T(8,128)(2,1)}, u32[]{:S(2)}, u32[]{:S(2)}) async-start(bf16[32,16,768]{2,1,0:T(8,128)(2,1)} %bitcast.26), calls=%async_computation.1 | async-start | bytes 1572864 | tf_op jit(solution)/shard_map/all_to_all | solution.py:432
  99.3 0.6 copy-done.10
  100.0 1.6 copy-done.2
  101.6 1.4 copy-done.4
  103.0 10.8 %shard_map.160 = (bf16[1024,512]{1,0:T(8,128)(2,1)}, bf16[1024,512]{1,0:T(8,128)(2,1)}, bf16[1024,512]{1,0:T(8,128)(2,1)}, f32[256,512]{1,0:T(8,128)S(1)}, bf16[...) custom-call(s32[1]{0:T(128)} %bitcast.5.core, bf16[1024,1024]{1,0:T(8,128)(2,1)S(1)} %copy-done.2, ...), custom_call_target="tpu_custom_call" | custom-call | flops 8200000000 | bytes 16777216 | tf_op jit(solution)/shard_map/pallas_call | solution.py:98
  113.8 0.7 collective-permute-start.29
  114.5 2.3 %collective-permute-done.29.came = bf16[512,1024]{1,0:T(8,128)(2,1)S(1)} collective-permute-done((bf16[512,1024]{1,0:T(8,128)(2,1)S(1)}, bf16[512,1024]{1,0:T(8,128)(2,1)S(1)}, u32[]{:S(2)}, u32[]{:S(2)}) %collective-permute-start.29) | collective-permute-done | bytes 1048608 | tf_op jit(solution)/shard_map/ppermute | solution.py:22
  116.8 1.1 shard_map.166
  117.9 8.0 %all-to-all-start = ((bf16[32,16,1024]{2,1,0:T(8,128)(2,1)}), bf16[32,16,1024]{2,1,0:T(8,128)(2,1)S(1)}, u32[]{:S(2)}, u32[]{:S(2)}) async-start(bf16[32,16,1024]{2,1,0:T(8,128)(2,1)} %bitcast.25), calls=%async_computation | async-start | bytes 2097152 | tf_op jit(solution)/shard_map/all_to_all | solution.py:432
  125.9 0.7 collective-permute-start.22
  126.6 1.2 collective-permute-done.22.came
  127.8 1.6 collective-permute-start.23
  129.4 4.4 %collective-permute-start.24 = (bf16[128,512]{1,0:T(8,128)(2,1)S(1)}, bf16[128,512]{1,0:T(8,128)(2,1)S(1)}, u32[]{:S(2)}, u32[]{:S(2)}) collective-permute-start(bf16[128,512]{1,0:T(8,128)(2,1)S(1)} %get-tuple-element.89), channel_id=1, source_target_pairs={{0,248},{8,0},{16,8},{24,16},{32,24},{40,32},{48,40},{56,48},{64,5... | collective-permute-start | bytes 393224 | tf_op jit(solution)/shard_map/ppermute | solution.py:27
  133.8 4.1 %shard_map.161.sums = f32[1024,512]{1,0:T(8,128)S(1)} custom-call(s32[1,1024]{1,0:T(1,128)S(1)} %bitcast.22, s32[1,1024]{1,0:T(1,128)S(1)} %bitcast.19, bf16[1024,512]{1,0:T(8,128)(2,1)} %get-tuple-element.84.dxs_h, bf16[1024,512]{1,0:T(8,128)(2,1)} %get-tuple-element.85.dxr_h), custom_call_target="tpu_custom_call" | custom-call | flops 2100000000 | bytes 4194304 | tf_op jit(solution)/shard_map/pallas_call | solution.py:98
  137.9 7.8 %collective-permute-done.23.low = bf16[128,512]{1,0:T(8,128)(2,1)S(1)} collective-permute-done((bf16[128,512]{1,0:T(8,128)(2,1)S(1)}, bf16[128,512]{1,0:T(8,128)(2,1)S(1)}, u32[]{:S(2)}, u32[]{:S(2)}) %collective-permute-start.23) | collective-permute-done | bytes 131104 | tf_op jit(solution)/shard_map/ppermute | solution.py:27
  145.7 0.6 shard_map.163
  146.3 2.7 %collective-permute-start.25 = (bf16[512,512]{1,0:T(8,128)(2,1)S(1)}, bf16[512,512]{1,0:T(8,128)(2,1)S(1)}, u32[]{:S(2)}, u32[]{:S(2)}) collective-permute-start(bf16[512,512]{1,0:T(8,128)(2,1)S(1)} %get-tuple-element.91), channel_id=1, source_target_pairs={{0,1},{1,0},{2,3},{3,2},{4,5},{5,4},{6,7},{7,6},{8,9},{9,8},{10,11... | collective-permute-start | bytes 1572872 | tf_op jit(solution)/shard_map/ppermute | solution.py:22
  149.1 1.3 shard_map.168.node_part
  151.0 3.3 %collective-permute-start.26 = (bf16[128,512]{1,0:T(8,128)(2,1)S(1)}, bf16[128,512]{1,0:T(8,128)(2,1)S(1)}, u32[]{:S(2)}, u32[]{:S(2)}) collective-permute-start(bf16[128,512]{1,0:T(8,128)(2,1)S(1)} %get-tuple-element.93), channel_id=1, source_target_pairs={{0,2},{1,3},{2,4},{3,5},{4,6},{5,7},{6,0},{7,1},{8,10},{9,11},{10,... | collective-permute-start | bytes 393224 | tf_op jit(solution)/shard_map/ppermute | solution.py:17
  154.3 2.1 %collective-permute-start.27 = (bf16[128,512]{1,0:T(8,128)(2,1)S(1)}, bf16[128,512]{1,0:T(8,128)(2,1)S(1)}, u32[]{:S(2)}, u32[]{:S(2)}) collective-permute-start(bf16[128,512]{1,0:T(8,128)(2,1)S(1)} %get-tuple-element.94), channel_id=1, source_target_pairs={{0,4},{1,5},{2,6},{3,7},{4,0},{5,1},{6,2},{7,3},{8,12},{9,13},{10,... | collective-permute-start | bytes 393224 | tf_op jit(solution)/shard_map/ppermute | solution.py:17
  156.4 2.6 %collective-permute-start.28 = (bf16[128,512]{1,0:T(8,128)(2,1)S(1)}, bf16[128,512]{1,0:T(8,128)(2,1)S(1)}, u32[]{:S(2)}, u32[]{:S(2)}) collective-permute-start(bf16[128,512]{1,0:T(8,128)(2,1)S(1)} %get-tuple-element.95), channel_id=1, source_target_pairs={{0,6},{1,7},{2,0},{3,1},{4,2},{5,3},{6,4},{7,5},{8,14},{9,15},{10,... | collective-permute-start | bytes 393224 | tf_op jit(solution)/shard_map/ppermute | solution.py:17
  159.0 1.0 collective-permute-start.32
  160.0 2.0 %collective-permute-start.33 = (bf16[16,1792]{1,0:T(8,128)(2,1)S(1)}, bf16[16,1792]{1,0:T(8,128)(2,1)S(1)}, u32[]{:S(2)}, u32[]{:S(2)}) collective-permute-start(bf16[16,1792]{1,0:T(8,128)(2,1)S(1)} %get-tuple-element.103), channel_id=1, source_target_pairs={{0,6},{1,7},{2,0},{3,1},{4,2},{5,3},{6,4},{7,5},{8,14},{9,15},{10,... | collective-permute-start | bytes 172040 | tf_op jit(solution)/shard_map/ppermute | solution.py:17
  162.1 8.6 %collective-permute-done.32.got2 = bf16[16,1792]{1,0:T(8,128)(2,1)S(1)} collective-permute-done((bf16[16,1792]{1,0:T(8,128)(2,1)S(1)}, bf16[16,1792]{1,0:T(8,128)(2,1)S(1)}, u32[]{:S(2)}, u32[]{:S(2)}) %collective-permute-start.32) | collective-permute-done | bytes 57376 | tf_op jit(solution)/shard_map/ppermute | solution.py:17
  170.6 1.8 %collective-permute-done.33.got3 = bf16[16,1792]{1,0:T(8,128)(2,1)S(1)} collective-permute-done((bf16[16,1792]{1,0:T(8,128)(2,1)S(1)}, bf16[16,1792]{1,0:T(8,128)(2,1)S(1)}, u32[]{:S(2)}, u32[]{:S(2)}) %collective-permute-start.33) | collective-permute-done | bytes 57376 | tf_op jit(solution)/shard_map/ppermute | solution.py:17
  172.5 0.6 collective-permute-start.34
  173.1 0.7 shard_map.165
  174.0 0.7 shard_map.171
  (58 shorter events, 3.3 us)
Async XLA Ops:
  0.6 12.6 %collective-permute-start = (bf16[128,512]{1,0:T(8,128)(2,1)}, bf16[128,512]{1,0:T(8,128)(2,1)S(1)}, u32[]{:S(2)}, u32[]{:S(2)}) collective-permute-start(bf16[128,512]{1,0:T(8,128)(2,1)} %node.1), channel_id=1, source_target_pairs={{0,6},{1,7},{2,0},{3,1},{4,2},{5,3},{6,4},{7,5},{8,14},{9,15},{10,... | collective-permute-start | bytes 393224 | tf_op jit(solution)/shard_map/ppermute | solution.py:17
  7.5 12.5 %collective-permute-start.1 = (bf16[128,512]{1,0:T(8,128)(2,1)}, bf16[128,512]{1,0:T(8,128)(2,1)S(1)}, u32[]{:S(2)}, u32[]{:S(2)}) collective-permute-start(bf16[128,512]{1,0:T(8,128)(2,1)} %node.1), channel_id=1, source_target_pairs={{0,4},{1,5},{2,6},{3,7},{4,0},{5,1},{6,2},{7,3},{8,12},{9,13},{10,... | collective-permute-start | bytes 393224 | tf_op jit(solution)/shard_map/ppermute | solution.py:17
  8.5 13.2 %collective-permute-start.2 = (bf16[128,512]{1,0:T(8,128)(2,1)}, bf16[128,512]{1,0:T(8,128)(2,1)S(1)}, u32[]{:S(2)}, u32[]{:S(2)}) collective-permute-start(bf16[128,512]{1,0:T(8,128)(2,1)} %node.1), channel_id=1, source_target_pairs={{0,2},{1,3},{2,4},{3,5},{4,6},{5,7},{6,0},{7,1},{8,10},{9,11},{10,... | collective-permute-start | bytes 393224 | tf_op jit(solution)/shard_map/ppermute | solution.py:17
  10.8 11.9 %collective-permute-start.3 = (bf16[128,512]{1,0:T(8,128)(2,1)}, bf16[128,512]{1,0:T(8,128)(2,1)S(1)}, u32[]{:S(2)}, u32[]{:S(2)}) collective-permute-start(bf16[128,512]{1,0:T(8,128)(2,1)} %node.1), channel_id=1, source_target_pairs={{0,1},{1,0},{2,3},{3,2},{4,5},{5,4},{6,7},{7,6},{8,9},{9,8},{10,11... | collective-permute-start | bytes 393224 | tf_op jit(solution)/shard_map/ppermute | solution.py:22
  13.2 9.5 %collective-permute-start.4 = (bf16[128,512]{1,0:T(8,128)(2,1)S(1)}, bf16[128,512]{1,0:T(8,128)(2,1)S(1)}, u32[]{:S(2)}, u32[]{:S(2)}) collective-permute-start(bf16[128,512]{1,0:T(8,128)(2,1)S(1)} %collective-permute-done.refs_0_), channel_id=1, source_target_pairs={{0,1},{1,0},{2,3},{3,2},{4,5},{5,4},{6,7},{7,6},{8,9},{9,8},{10,11... | collective-permute-start | bytes 393224 | tf_op jit(solution)/shard_map/ppermute | solution.py:22
  20.0 2.7 %collective-permute-start.5 = (bf16[128,512]{1,0:T(8,128)(2,1)S(1)}, bf16[128,512]{1,0:T(8,128)(2,1)S(1)}, u32[]{:S(2)}, u32[]{:S(2)}) collective-permute-start(bf16[128,512]{1,0:T(8,128)(2,1)S(1)} %collective-permute-done.1.refs_1_), channel_id=1, source_target_pairs={{0,1},{1,0},{2,3},{3,2},{4,5},{5,4},{6,7},{7,6},{8,9},{9,8},{10,11... | collective-permute-start | bytes 393224 | tf_op jit(solution)/shard_map/ppermute | solution.py:22
  21.7 1.3 collective-permute-start.6
  24.4 8.4 %collective-permute-start.9 = (bf16[128,512]{1,0:T(8,128)(2,1)S(1)}, bf16[128,512]{1,0:T(8,128)(2,1)S(1)}, u32[]{:S(2)}, u32[]{:S(2)}) collective-permute-start(bf16[128,512]{1,0:T(8,128)(2,1)S(1)} %get-tuple-element.66), channel_id=1, source_target_pairs={{0,248},{8,0},{16,8},{24,16},{32,24},{40,32},{48,40},{56,48},{64,5... | collective-permute-start | bytes 393224 | tf_op jit(solution)/shard_map/ppermute | solution.py:27
  30.4 8.6 %collective-permute-start.7 = (bf16[128,512]{1,0:T(8,128)(2,1)S(1)}, bf16[128,512]{1,0:T(8,128)(2,1)S(1)}, u32[]{:S(2)}, u32[]{:S(2)}) collective-permute-start(bf16[128,512]{1,0:T(8,128)(2,1)S(1)} %get-tuple-element.65), channel_id=1, source_target_pairs={{0,8},{8,16},{16,24},{24,32},{32,40},{40,48},{48,56},{56,64},{64,7... | collective-permute-start | bytes 393224 | tf_op jit(solution)/shard_map/ppermute | solution.py:27
  32.9 12.6 %collective-permute-start.10 = (bf16[128,512]{1,0:T(8,128)(2,1)S(1)}, bf16[128,512]{1,0:T(8,128)(2,1)S(1)}, u32[]{:S(2)}, u32[]{:S(2)}) collective-permute-start(bf16[128,512]{1,0:T(8,128)(2,1)S(1)} %collective-permute-done.9.refs_2_), channel_id=1, source_target_pairs={{0,1},{1,0},{2,3},{3,2},{4,5},{5,4},{6,7},{7,6},{8,9},{9,8},{10,11... | collective-permute-start | bytes 393224 | tf_op jit(solution)/shard_map/ppermute | solution.py:22
  39.0 6.4 %copy-start.8 = (bf16[128,512]{1,0:T(8,128)(2,1)}, bf16[128,512]{1,0:T(8,128)(2,1)S(1)}, u32[]{:S(2)}) copy-start(bf16[128,512]{1,0:T(8,128)(2,1)S(1)} %collective-permute-done.7.refs_0_) | copy-start | bytes 393220
  39.0 6.5 %collective-permute-start.8 = (bf16[128,512]{1,0:T(8,128)(2,1)S(1)}, bf16[128,512]{1,0:T(8,128)(2,1)S(1)}, u32[]{:S(2)}, u32[]{:S(2)}) collective-permute-start(bf16[128,512]{1,0:T(8,128)(2,1)S(1)} %collective-permute-done.7.refs_0_), channel_id=1, source_target_pairs={{0,1},{1,0},{2,3},{3,2},{4,5},{5,4},{6,7},{7,6},{8,9},{9,8},{10,11... | collective-permute-start | bytes 393224 | tf_op jit(solution)/shard_map/ppermute | solution.py:22
  45.5 0.9 copy-start.9
  46.4 25.1 %copy-start = (bf16[128,512]{1,0:T(8,128)(2,1)S(1)}, bf16[128,512]{1,0:T(8,128)(2,1)}, u32[]{:S(2)}) copy-start(bf16[128,512]{1,0:T(8,128)(2,1)} %node.1) | copy-start | bytes 393220
  46.4 25.1 %copy-start.5 = (bf16[1024,512]{1,0:T(8,128)(2,1)S(1)}, bf16[1024,512]{1,0:T(8,128)(2,1)}, u32[]{:S(2)}) copy-start(bf16[1024,512]{1,0:T(8,128)(2,1)} %w1.1) | copy-start | bytes 3145732
  46.4 25.1 %copy-start.6 = (bf16[512,512]{1,0:T(8,128)(2,1)S(1)}, bf16[512,512]{1,0:T(8,128)(2,1)}, u32[]{:S(2)}) copy-start(bf16[512,512]{1,0:T(8,128)(2,1)} %w2.1) | copy-start | bytes 1572868
  46.4 25.1 %copy-start.7 = (bf16[128,512]{1,0:T(8,128)(2,1)S(1)}, bf16[128,512]{1,0:T(8,128)(2,1)}, u32[]{:S(2)}) copy-start(bf16[128,512]{1,0:T(8,128)(2,1)} %grad.1) | copy-start | bytes 393220
  50.9 2.2 %collective-permute-start.11 = (bf16[512,512]{1,0:T(8,128)(2,1)S(1)}, bf16[512,512]{1,0:T(8,128)(2,1)S(1)}, u32[]{:S(2)}, u32[]{:S(2)}) collective-permute-start(bf16[512,512]{1,0:T(8,128)(2,1)S(1)} %get-tuple-element.76), channel_id=1, source_target_pairs={{0,1},{1,0},{2,3},{3,2},{4,5},{5,4},{6,7},{7,6},{8,9},{9,8},{10,11... | collective-permute-start | bytes 1572872 | tf_op jit(solution)/shard_map/ppermute | solution.py:22
  53.2 10.2 %collective-permute-start.12 = (bf16[128,512]{1,0:T(8,128)(2,1)S(1)}, bf16[128,512]{1,0:T(8,128)(2,1)S(1)}, u32[]{:S(2)}, u32[]{:S(2)}) collective-permute-start(bf16[128,512]{1,0:T(8,128)(2,1)S(1)} %get-tuple-element.78), channel_id=1, source_target_pairs={{0,2},{1,3},{2,4},{3,5},{4,6},{5,7},{6,0},{7,1},{8,10},{9,11},{10,... | collective-permute-start | bytes 393224 | tf_op jit(solution)/shard_map/ppermute | solution.py:17
  55.1 16.4 %collective-permute-start.13 = (bf16[128,512]{1,0:T(8,128)(2,1)S(1)}, bf16[128,512]{1,0:T(8,128)(2,1)S(1)}, u32[]{:S(2)}, u32[]{:S(2)}) collective-permute-start(bf16[128,512]{1,0:T(8,128)(2,1)S(1)} %get-tuple-element.79), channel_id=1, source_target_pairs={{0,4},{1,5},{2,6},{3,7},{4,0},{5,1},{6,2},{7,3},{8,12},{9,13},{10,... | collective-permute-start | bytes 393224 | tf_op jit(solution)/shard_map/ppermute | solution.py:17
  59.2 12.3 %collective-permute-start.14 = (bf16[128,512]{1,0:T(8,128)(2,1)S(1)}, bf16[128,512]{1,0:T(8,128)(2,1)S(1)}, u32[]{:S(2)}, u32[]{:S(2)}) collective-permute-start(bf16[128,512]{1,0:T(8,128)(2,1)S(1)} %get-tuple-element.80), channel_id=1, source_target_pairs={{0,6},{1,7},{2,0},{3,1},{4,2},{5,3},{6,4},{7,5},{8,14},{9,15},{10,... | collective-permute-start | bytes 393224 | tf_op jit(solution)/shard_map/ppermute | solution.py:17
  73.3 19.2 %collective-permute-start.30 = (bf16[512,768]{1,0:T(8,128)(2,1)S(1)}, bf16[512,768]{1,0:T(8,128)(2,1)S(1)}, u32[]{:S(2)}, u32[]{:S(2)}) collective-permute-start(bf16[512,768]{1,0:T(8,128)(2,1)S(1)} %get-tuple-element.101), channel_id=1, source_target_pairs={{0,1},{1,0},{2,3},{3,2},{4,5},{5,4},{6,7},{7,6},{8,9},{9,8},{10,11... | collective-permute-start | bytes 2359304 | tf_op jit(solution)/shard_map/ppermute | solution.py:22
  73.9 9.8 %collective-permute-start.15 = (bf16[128,512]{1,0:T(8,128)(2,1)S(1)}, bf16[128,512]{1,0:T(8,128)(2,1)S(1)}, u32[]{:S(2)}, u32[]{:S(2)}) collective-permute-start(bf16[128,512]{1,0:T(8,128)(2,1)S(1)} %get-tuple-element.81.refs_0_), channel_id=1, source_target_pairs={{0,6},{1,7},{2,0},{3,1},{4,2},{5,3},{6,4},{7,5},{8,14},{9,15},{10,... | collective-permute-start | bytes 393224 | tf_op jit(solution)/shard_map/ppermute | solution.py:17
  75.7 14.6 %collective-permute-start.16 = (bf16[128,512]{1,0:T(8,128)(2,1)S(1)}, bf16[128,512]{1,0:T(8,128)(2,1)S(1)}, u32[]{:S(2)}, u32[]{:S(2)}) collective-permute-start(bf16[128,512]{1,0:T(8,128)(2,1)S(1)} %get-tuple-element.81.refs_0_), channel_id=1, source_target_pairs={{0,4},{1,5},{2,6},{3,7},{4,0},{5,1},{6,2},{7,3},{8,12},{9,13},{10,... | collective-permute-start | bytes 393224 | tf_op jit(solution)/shard_map/ppermute | solution.py:17
  77.2 13.7 %collective-permute-start.17 = (bf16[128,512]{1,0:T(8,128)(2,1)S(1)}, bf16[128,512]{1,0:T(8,128)(2,1)S(1)}, u32[]{:S(2)}, u32[]{:S(2)}) collective-permute-start(bf16[128,512]{1,0:T(8,128)(2,1)S(1)} %get-tuple-element.81.refs_0_), channel_id=1, source_target_pairs={{0,2},{1,3},{2,4},{3,5},{4,6},{5,7},{6,0},{7,1},{8,10},{9,11},{10,... | collective-permute-start | bytes 393224 | tf_op jit(solution)/shard_map/ppermute | solution.py:17
  79.5 19.8 %collective-permute-start.18 = (bf16[128,512]{1,0:T(8,128)(2,1)S(1)}, bf16[128,512]{1,0:T(8,128)(2,1)S(1)}, u32[]{:S(2)}, u32[]{:S(2)}) collective-permute-start(bf16[128,512]{1,0:T(8,128)(2,1)S(1)} %get-tuple-element.81.refs_0_), channel_id=1, source_target_pairs={{0,1},{1,0},{2,3},{3,2},{4,5},{5,4},{6,7},{7,6},{8,9},{9,8},{10,11... | collective-permute-start | bytes 393224 | tf_op jit(solution)/shard_map/ppermute | solution.py:22
  83.6 15.7 %collective-permute-start.19 = (bf16[128,512]{1,0:T(8,128)(2,1)S(1)}, bf16[128,512]{1,0:T(8,128)(2,1)}, u32[]{:S(2)}, u32[]{:S(2)}) collective-permute-start(bf16[128,512]{1,0:T(8,128)(2,1)S(1)} %collective-permute-done.15.refs_1_), channel_id=1, source_target_pairs={{0,1},{1,0},{2,3},{3,2},{4,5},{5,4},{6,7},{7,6},{8,9},{9,8},{10,11... | collective-permute-start | bytes 393224 | tf_op jit(solution)/shard_map/ppermute | solution.py:22
  90.4 9.0 %collective-permute-start.20 = (bf16[128,512]{1,0:T(8,128)(2,1)S(1)}, bf16[128,512]{1,0:T(8,128)(2,1)}, u32[]{:S(2)}, u32[]{:S(2)}) collective-permute-start(bf16[128,512]{1,0:T(8,128)(2,1)S(1)} %collective-permute-done.16.refs_2_), channel_id=1, source_target_pairs={{0,1},{1,0},{2,3},{3,2},{4,5},{5,4},{6,7},{7,6},{8,9},{9,8},{10,11... | collective-permute-start | bytes 393224 | tf_op jit(solution)/shard_map/ppermute | solution.py:22
  90.9 8.4 %collective-permute-start.21 = (bf16[128,512]{1,0:T(8,128)(2,1)S(1)}, bf16[128,512]{1,0:T(8,128)(2,1)}, u32[]{:S(2)}, u32[]{:S(2)}) collective-permute-start(bf16[128,512]{1,0:T(8,128)(2,1)S(1)} %collective-permute-done.17.refs_3_), channel_id=1, source_target_pairs={{0,1},{1,0},{2,3},{3,2},{4,5},{5,4},{6,7},{7,6},{8,9},{9,8},{10,11... | collective-permute-start | bytes 393224 | tf_op jit(solution)/shard_map/ppermute | solution.py:22
  92.5 1.6 copy-start.1
  92.5 2.1 %copy-start.3 = (bf16[1536,512]{1,0:T(8,128)(2,1)}, bf16[1536,512]{1,0:T(8,128)(2,1)S(1)}, u32[]{:S(2)}) copy-start(bf16[1536,512]{1,0:T(8,128)(2,1)S(1)} %get-tuple-element.82.refs_8_) | copy-start | bytes 4718596
  94.6 23.4 %all-to-all-start.1 = ((bf16[32,16,768]{2,1,0:T(8,128)(2,1)}), bf16[32,16,768]{2,1,0:T(8,128)(2,1)}, u32[]{:S(2)}, u32[]{:S(2)}) async-start(bf16[32,16,768]{2,1,0:T(8,128)(2,1)} %bitcast.26), calls=%async_computation.1 | async-start | bytes 1572864 | tf_op jit(solution)/shard_map/all_to_all | solution.py:432
  99.3 0.7 copy-start.10
  100.0 1.6 copy-start.2
  101.5 1.4 copy-start.4
  113.8 3.0 %collective-permute-start.29 = (bf16[512,1024]{1,0:T(8,128)(2,1)S(1)}, bf16[512,1024]{1,0:T(8,128)(2,1)S(1)}, u32[]{:S(2)}, u32[]{:S(2)}) collective-permute-start(bf16[512,1024]{1,0:T(8,128)(2,1)S(1)} %get-tuple-element.99), channel_id=1, source_target_pairs={{0,1},{1,0},{2,3},{3,2},{4,5},{5,4},{6,7},{7,6},{8,9},{9,8},{10,11... | collective-permute-start | bytes 3145736 | tf_op jit(solution)/shard_map/ppermute | solution.py:22
  117.9 32.4 %all-to-all-start = ((bf16[32,16,1024]{2,1,0:T(8,128)(2,1)}), bf16[32,16,1024]{2,1,0:T(8,128)(2,1)S(1)}, u32[]{:S(2)}, u32[]{:S(2)}) async-start(bf16[32,16,1024]{2,1,0:T(8,128)(2,1)} %bitcast.25), calls=%async_computation | async-start | bytes 2097152 | tf_op jit(solution)/shard_map/all_to_all | solution.py:432
  125.9 1.9 %collective-permute-start.22 = (bf16[256,512]{1,0:T(8,128)(2,1)S(1)}, bf16[256,512]{1,0:T(8,128)(2,1)S(1)}, u32[]{:S(2)}, u32[]{:S(2)}) collective-permute-start(bf16[256,512]{1,0:T(8,128)(2,1)S(1)} %get-tuple-element.87), channel_id=1, source_target_pairs={{0,1},{1,0},{2,3},{3,2},{4,5},{5,4},{6,7},{7,6},{8,9},{9,8},{10,11... | collective-permute-start | bytes 786440 | tf_op jit(solution)/shard_map/ppermute | solution.py:22
  127.8 17.9 %collective-permute-start.23 = (bf16[128,512]{1,0:T(8,128)(2,1)S(1)}, bf16[128,512]{1,0:T(8,128)(2,1)S(1)}, u32[]{:S(2)}, u32[]{:S(2)}) collective-permute-start(bf16[128,512]{1,0:T(8,128)(2,1)S(1)} %get-tuple-element.88), channel_id=1, source_target_pairs={{0,8},{8,16},{16,24},{24,32},{32,40},{40,48},{48,56},{56,64},{64,7... | collective-permute-start | bytes 393224 | tf_op jit(solution)/shard_map/ppermute | solution.py:27
  129.4 16.3 %collective-permute-start.24 = (bf16[128,512]{1,0:T(8,128)(2,1)S(1)}, bf16[128,512]{1,0:T(8,128)(2,1)S(1)}, u32[]{:S(2)}, u32[]{:S(2)}) collective-permute-start(bf16[128,512]{1,0:T(8,128)(2,1)S(1)} %get-tuple-element.89), channel_id=1, source_target_pairs={{0,248},{8,0},{16,8},{24,16},{32,24},{40,32},{48,40},{56,48},{64,5... | collective-permute-start | bytes 393224 | tf_op jit(solution)/shard_map/ppermute | solution.py:27
  146.3 4.6 %collective-permute-start.25 = (bf16[512,512]{1,0:T(8,128)(2,1)S(1)}, bf16[512,512]{1,0:T(8,128)(2,1)S(1)}, u32[]{:S(2)}, u32[]{:S(2)}) collective-permute-start(bf16[512,512]{1,0:T(8,128)(2,1)S(1)} %get-tuple-element.91), channel_id=1, source_target_pairs={{0,1},{1,0},{2,3},{3,2},{4,5},{5,4},{6,7},{7,6},{8,9},{9,8},{10,11... | collective-permute-start | bytes 1572872 | tf_op jit(solution)/shard_map/ppermute | solution.py:22
  150.5 9.6 %collective-permute-start.31 = (bf16[16,1792]{1,0:T(8,128)(2,1)S(1)}, bf16[16,1792]{1,0:T(8,128)(2,1)S(1)}, u32[]{:S(2)}, u32[]{:S(2)}) collective-permute-start(bf16[16,1792]{1,0:T(8,128)(2,1)S(1)} %get-tuple-element.103), channel_id=1, source_target_pairs={{0,2},{1,3},{2,4},{3,5},{4,6},{5,7},{6,0},{7,1},{8,10},{9,11},{10,... | collective-permute-start | bytes 172040 | tf_op jit(solution)/shard_map/ppermute | solution.py:17
  151.0 22.1 %collective-permute-start.26 = (bf16[128,512]{1,0:T(8,128)(2,1)S(1)}, bf16[128,512]{1,0:T(8,128)(2,1)S(1)}, u32[]{:S(2)}, u32[]{:S(2)}) collective-permute-start(bf16[128,512]{1,0:T(8,128)(2,1)S(1)} %get-tuple-element.93), channel_id=1, source_target_pairs={{0,2},{1,3},{2,4},{3,5},{4,6},{5,7},{6,0},{7,1},{8,10},{9,11},{10,... | collective-permute-start | bytes 393224 | tf_op jit(solution)/shard_map/ppermute | solution.py:17
  154.3 18.7 %collective-permute-start.27 = (bf16[128,512]{1,0:T(8,128)(2,1)S(1)}, bf16[128,512]{1,0:T(8,128)(2,1)S(1)}, u32[]{:S(2)}, u32[]{:S(2)}) collective-permute-start(bf16[128,512]{1,0:T(8,128)(2,1)S(1)} %get-tuple-element.94), channel_id=1, source_target_pairs={{0,4},{1,5},{2,6},{3,7},{4,0},{5,1},{6,2},{7,3},{8,12},{9,13},{10,... | collective-permute-start | bytes 393224 | tf_op jit(solution)/shard_map/ppermute | solution.py:17
  156.4 16.7 %collective-permute-start.28 = (bf16[128,512]{1,0:T(8,128)(2,1)S(1)}, bf16[128,512]{1,0:T(8,128)(2,1)S(1)}, u32[]{:S(2)}, u32[]{:S(2)}) collective-permute-start(bf16[128,512]{1,0:T(8,128)(2,1)S(1)} %get-tuple-element.95), channel_id=1, source_target_pairs={{0,6},{1,7},{2,0},{3,1},{4,2},{5,3},{6,4},{7,5},{8,14},{9,15},{10,... | collective-permute-start | bytes 393224 | tf_op jit(solution)/shard_map/ppermute | solution.py:17
  159.0 11.6 %collective-permute-start.32 = (bf16[16,1792]{1,0:T(8,128)(2,1)S(1)}, bf16[16,1792]{1,0:T(8,128)(2,1)S(1)}, u32[]{:S(2)}, u32[]{:S(2)}) collective-permute-start(bf16[16,1792]{1,0:T(8,128)(2,1)S(1)} %get-tuple-element.103), channel_id=1, source_target_pairs={{0,4},{1,5},{2,6},{3,7},{4,0},{5,1},{6,2},{7,3},{8,12},{9,13},{10,... | collective-permute-start | bytes 172040 | tf_op jit(solution)/shard_map/ppermute | solution.py:17
  160.0 12.4 %collective-permute-start.33 = (bf16[16,1792]{1,0:T(8,128)(2,1)S(1)}, bf16[16,1792]{1,0:T(8,128)(2,1)S(1)}, u32[]{:S(2)}, u32[]{:S(2)}) collective-permute-start(bf16[16,1792]{1,0:T(8,128)(2,1)S(1)} %get-tuple-element.103), channel_id=1, source_target_pairs={{0,6},{1,7},{2,0},{3,1},{4,2},{5,3},{6,4},{7,5},{8,14},{9,15},{10,... | collective-permute-start | bytes 172040 | tf_op jit(solution)/shard_map/ppermute | solution.py:17
  172.5 1.5 collective-permute-start.34
